TPU v7x, 128 devices: a whole 4x4x4 slice. The times are simulated.
128 devices in a mesh: req: 16 (over y_lo, z, core), tp: 8 (over y_hi, x).
Axes of the slice: x: 4, y: 4 (y_hi: 2, y_lo: 2; y = y_hi * 2 + y_lo), z: 4, core: 2. Of those that a mesh axis runs over, the one named last changes fastest.
Arguments:
- tokens: bfloat16 [2048, 2048], P('req')
- attn_gain: float32 [2048], replicated, may hold values from 0.25 to 1.75
- query_gain: float32 [128], replicated, may hold values from 0.8 to 2
- key_gain: float32 [128], replicated, may hold values from 0.8 to 2
- moe_gain: float32 [2048], replicated, may hold values from 0.25 to 1.75
- query_weight: float32 [2048, 2048], P('req', 'tp'), may hold values from -0.125 to 0.125
- key_weight: float32 [2048, 2048], P('req', 'tp'), may hold values from -0.125 to 0.125
- value_weight: float32 [2048, 2048], P('req', 'tp'), may hold values from -0.125 to 0.125
- out_weight: float32 [2048, 2048], P('tp', 'req'), may hold values from -0.125 to 0.125
- gate_weight: float32 [64, 2048, 1024], P(None, ('req', 'tp')), may hold values from -0.125 to 0.125
- up_weight: float32 [64, 2048, 1024], P(None, ('req', 'tp')), may hold values from -0.125 to 0.125
- down_weight: bfloat16 [128, 512, 2048], P(('req', 'tp')), may hold values from -0.1875 to 0.1875
- router_weight: bfloat16 [2048, 64], replicated, may hold values from -0.125 to 0.125
- page_store: bfloat16 [128, 128, 2, 2048], P('req', None, None, 'tp'), may hold values from -3 to 3
- prompt_lengths: int32 [32], replicated, may hold values from 32 to 96, as said below
- continues: int32 [32], replicated, may hold values from 0 to 1, as said below
- page_owner: int32 [16, 16], replicated, may hold values from 0 to 15, as said below
- page_slot: int32 [16, 16], replicated, may hold values from 0 to 7
- routes: int32 [2048, 8], P(('req', 'tp')), may hold values from 0 to 63, as said below
Outputs:
- server_qkv: bfloat16 [2048, 6144], P(None, 'tp')
- server_out: bfloat16 [2048, 2048], P('tp')
- server_gate_up: bfloat16 [128, 2048, 1024], P(('req', 'tp'))
- hidden: bfloat16 [2048, 2048], P(('req', 'tp'))
- new_cache: bfloat16 [2048, 2, 2048], P('req', None, 'tp')
Inputs may be any that keep to these rules, and one draw needn't show every extreme that they name: `prompt_lengths`: entries 2g and 2g + 1 are the two prompt lengths of group g and sum to 128. Exactly one of the two prompts of each group continues an earlier request. `page_owner`: no page of group g lies on g itself; at most 2 of a group's 16 pages lie on one owner, and every group has exactly 2 pages on some owner. `routes`: each row names 8 different experts. In each aligned block of 16 rows (the rows of one device) no expert is named by more than 3 rows, and one expert, the same in every block, is named by exactly 3 rows in each block.
All inputs are finite; a program needn't handle non-finite values.
Results may differ from a plain program's by a relative error of at most 0.0057.
Values may be sent and summed in bfloat16 or wider, within the bound.
A program may use at most 128 MiB of HBM per device.

v0:
```python
import math

import jax
import jax.numpy as jnp
from jax import lax
from jax.sharding import PartitionSpec as P

norm_eps = 1e-06
rope_base = 50000.0


def rms_scale(values, gain_vec):
    return (
        values * lax.rsqrt(jnp.mean(values * values, axis=-1, keepdims=True) + norm_eps) * gain_vec
    )


def rotate_half(values, cosine, sine_part):
    half_width = values.shape[-1] // 2
    first_half = values[..., :half_width]
    second_half = values[..., half_width:]
    return jnp.concatenate(
        [
            first_half * cosine - second_half * sine_part,
            second_half * cosine + first_half * sine_part,
        ],
        axis=-1,
    )


def split_halves(weights):
    expert_count, rows_here, hidden_units = weights.shape
    return weights.reshape(expert_count, rows_here, 2, hidden_units // 2).transpose(0, 2, 1, 3)


def body(
    tokens,
    attn_gain,
    query_gain,
    key_gain,
    moe_gain,
    query_weight,
    key_weight,
    value_weight,
    out_weight,
    gate_weight,
    up_weight,
    down_weight,
    router_weight,
    page_store,
    prompt_lengths,
    continues,
    page_owner,
    page_slot,
    routes,
):
    req_count = lax.axis_size("req")
    req_index = lax.axis_index("req")
    lane_index = lax.axis_index("tp")
    joined_local = jnp.concatenate(
        [
            query_weight.astype(jnp.bfloat16),
            key_weight.astype(jnp.bfloat16),
            value_weight.astype(jnp.bfloat16),
        ],
        axis=1,
    )
    server_qkv, server_out = (
        lax.all_gather(joined_local, "req", axis=0, tiled=True),
        lax.all_gather(out_weight.astype(jnp.bfloat16), "req", axis=1, tiled=True),
    )
    expert_count, rows_here, hidden_units = gate_weight.shape
    half_units = hidden_units // 2
    packed = jnp.concatenate(
        [
            split_halves(gate_weight.astype(jnp.bfloat16)),
            split_halves(up_weight.astype(jnp.bfloat16)),
        ],
        axis=3,
    ).reshape(2 * expert_count, rows_here, hidden_units)
    server_gate_up = lax.all_to_all(packed, ("req", "tp"), split_axis=0, concat_axis=1, tiled=True)
    group_rows, model_width = tokens.shape
    tokens_f32 = tokens.astype(jnp.float32)
    normed = rms_scale(tokens_f32, attn_gain).astype(jnp.bfloat16)
    projected = jnp.dot(normed, server_qkv, preferred_element_type=jnp.float32)
    head_dim = query_gain.shape[0]
    lane_width = server_qkv.shape[1] // 3
    lane_heads = lane_width // head_dim
    query_raw = projected[:, :lane_width].reshape(group_rows, lane_heads, head_dim)
    key_raw = projected[:, lane_width : 2 * lane_width].reshape(group_rows, lane_heads, head_dim)
    value_raw = projected[:, 2 * lane_width :]
    first_length = lax.dynamic_index_in_dim(prompt_lengths, 2 * req_index, 0, keepdims=False)
    carry_flags = lax.dynamic_slice_in_dim(continues, 2 * req_index, 2)
    row_ids = jnp.arange(group_rows, dtype=jnp.int32)
    second = (row_ids >= first_length).astype(jnp.int32)
    within = row_ids - second * first_length
    carried = jnp.where(second == 1, carry_flags[1], carry_flags[0])
    pages_per = page_owner.shape[1]
    page_rows = page_store.shape[1]
    context_len = pages_per * page_rows
    position = (within + context_len * carried).astype(jnp.float32)
    inverse = jnp.power(
        jnp.float32(rope_base), -(jnp.arange(head_dim // 2, dtype=jnp.float32) * 2.0 / head_dim)
    )
    angles = position[:, None, None] * inverse[None, None, :]
    cosine = jnp.cos(angles)
    sine_part = jnp.sin(angles)
    query_rows = rotate_half(rms_scale(query_raw, query_gain), cosine, sine_part).astype(
        jnp.bfloat16
    )
    keys_new = rotate_half(rms_scale(key_raw, key_gain), cosine, sine_part).astype(jnp.bfloat16)
    values_new = value_raw.astype(jnp.bfloat16)
    new_cache = jnp.stack([keys_new.reshape(group_rows, lane_width), values_new], axis=1)
    capacity = max(2, (pages_per + req_count - 2) // (req_count - 1))
    page_ids = jnp.arange(pages_per, dtype=jnp.int32)
    earlier = page_ids[None, :] < page_ids[:, None]
    same_owner = page_owner[:, :, None] == page_owner[:, None, :]
    page_rank = jnp.sum((same_owner & earlier[None]).astype(jnp.int32), axis=2)
    owned_here = page_owner == req_index
    chosen = owned_here[:, None, :] & (
        page_rank[:, None, :] == jnp.arange(capacity, dtype=jnp.int32)[None, :, None]
    )
    send_slot = jnp.sum(jnp.where(chosen, page_slot[:, None, :], 0), axis=2)
    send_live = jnp.any(chosen, axis=2)
    page_shape = page_store.shape[1:]
    outgoing_pages = jnp.take(page_store, send_slot.reshape(-1), axis=0).reshape(
        (req_count, capacity) + page_shape
    )
    outgoing_pages = jnp.where(
        send_live[:, :, None, None, None], outgoing_pages, jnp.zeros_like(outgoing_pages)
    )
    arrived_pages = lax.all_to_all(outgoing_pages, "req", split_axis=0, concat_axis=0, tiled=True)
    own_owner = jnp.take(page_owner, req_index, axis=0)
    own_rank = jnp.take(page_rank, req_index, axis=0)
    context = jnp.take(
        arrived_pages.reshape((req_count * capacity,) + page_shape),
        own_owner * capacity + own_rank,
        axis=0,
    )
    context = context.reshape(context_len, 2, lane_heads, head_dim)
    score_scale = 1.0 / math.sqrt(head_dim)
    near_scores = (
        jnp.einsum("ihc,jhc->hij", query_rows, keys_new, preferred_element_type=jnp.float32)
        * score_scale
    )
    far_scores = (
        jnp.einsum("ihc,jhc->hij", query_rows, context[:, 0], preferred_element_type=jnp.float32)
        * score_scale
    )
    same_request = second[:, None] == second[None, :]
    near_weights = jnp.where(same_request[None], jnp.exp(near_scores), jnp.float32(0.0))
    far_weights = jnp.where((carried == 1)[None, :, None], jnp.exp(far_scores), jnp.float32(0.0))
    totals = jnp.sum(near_weights, axis=2, keepdims=True) + jnp.sum(
        far_weights, axis=2, keepdims=True
    )
    near_probs = (near_weights / totals).astype(jnp.bfloat16)
    far_probs = (far_weights / totals).astype(jnp.bfloat16)
    attended = jnp.einsum(
        "hij,jhc->ihc",
        near_probs,
        values_new.reshape(group_rows, lane_heads, head_dim),
        preferred_element_type=jnp.float32,
    )
    attended = attended + jnp.einsum(
        "hij,jhc->ihc", far_probs, context[:, 1], preferred_element_type=jnp.float32
    )
    attended = attended.astype(jnp.bfloat16).reshape(group_rows, lane_width)
    shard_rows = routes.shape[0]
    row_start = lane_index * shard_rows
    head_terms = jnp.dot(attended, server_out, preferred_element_type=jnp.float32)
    mixed_all = lax.psum(head_terms, "tp")
    mixed_own = lax.dynamic_slice_in_dim(mixed_all, row_start, shard_rows, 0)
    residual_own = lax.dynamic_slice_in_dim(tokens_f32, row_start, shard_rows, 0) + mixed_own
    moe_own = rms_scale(residual_own, moe_gain).astype(jnp.bfloat16)
    logits = jnp.dot(moe_own, router_weight, preferred_element_type=jnp.float32)
    exps = jnp.exp(logits)
    routed_exps = jnp.take_along_axis(exps, routes, axis=1)
    entry_gates = routed_exps / jnp.sum(routed_exps, axis=1, keepdims=True)
    top_count = routes.shape[1]
    slot_depth = 3 * shard_rows * top_count // (2 * expert_count)
    flat_routes = routes.reshape(-1)
    onehot = (flat_routes[:, None] == jnp.arange(expert_count, dtype=jnp.int32)[None, :]).astype(
        jnp.int32
    )
    entry_rank = jnp.sum((jnp.cumsum(onehot, axis=0) - onehot) * onehot, axis=1)
    entry_slot = (flat_routes * slot_depth + entry_rank).reshape(shard_rows, top_count)
    select_table = jnp.any(
        entry_slot[None, :, :]
        == jnp.arange(expert_count * slot_depth, dtype=jnp.int32)[:, None, None],
        axis=2,
    ).astype(jnp.bfloat16)
    outgoing_rows = jnp.dot(select_table, moe_own, preferred_element_type=jnp.float32).astype(
        jnp.bfloat16
    )
    send_rows = jnp.broadcast_to(
        outgoing_rows.reshape(expert_count, 1, slot_depth, model_width),
        (expert_count, 2, slot_depth, model_width),
    ).reshape(2 * expert_count, slot_depth, model_width)
    arrived_rows = lax.all_to_all(send_rows, ("req", "tp"), split_axis=0, concat_axis=0, tiled=True)
    flat_rows = arrived_rows.reshape(-1, model_width)
    both = jnp.dot(flat_rows, server_gate_up[0], preferred_element_type=jnp.float32)
    act = (jax.nn.silu(both[:, :half_units]) * both[:, half_units:]).astype(jnp.bfloat16)
    expert_rows = (
        jnp.dot(act, down_weight[0], preferred_element_type=jnp.float32)
        .astype(jnp.bfloat16)
        .reshape(arrived_rows.shape)
    )
    returned = lax.all_to_all(expert_rows, ("req", "tp"), split_axis=0, concat_axis=0, tiled=True)
    returned = returned.reshape(expert_count, 2, slot_depth, model_width)
    joined_out = (returned[:, 0].astype(jnp.float32) + returned[:, 1].astype(jnp.float32)).reshape(
        expert_count * slot_depth, model_width
    )
    picked_rows = jnp.take(joined_out, entry_slot.reshape(-1), axis=0).reshape(
        shard_rows, top_count, model_width
    )
    moe_out = jnp.sum(picked_rows * entry_gates[:, :, None], axis=1)
    hidden_rows = (residual_own + moe_out).astype(jnp.bfloat16)
    return (server_qkv, server_out, server_gate_up, hidden_rows, new_cache)


def solution(mesh):
    in_specs = (
        P("req", None),
        P(),
        P(),
        P(),
        P(),
        P("req", "tp"),
        P("req", "tp"),
        P("req", "tp"),
        P("tp", "req"),
        P(None, ("req", "tp"), None),
        P(None, ("req", "tp"), None),
        P(("req", "tp"), None, None),
        P(),
        P("req", None, None, "tp"),
        P(),
        P(),
        P(),
        P(),
        P(("req", "tp"), None),
    )
    out_specs = (
        P(None, "tp"),
        P("tp", None),
        P(("req", "tp"), None, None),
        P(("req", "tp"), None),
        P("req", None, "tp"),
    )
    return jax.shard_map(body, mesh=mesh, in_specs=in_specs, out_specs=out_specs, check_vma=False)
```

profile of v0, /device:TPU:1, one launch (start us, length us, event | category | flops | bytes accessed | tf_op | source)
XLA Modules:
  0.0 396.6 jit_solution(3636944397927276136)
XLA Ops:
  14.1 10.0 %gather_fusion = bf16[32,128,2,256]{3,2,1,0:T(2,128)(2,1)} fusion(bf16[8,128,2,256]{3,2,1,0:T(2,128)(2,1)S(1)} %copy-done.1, s32[1024]{0:T(1024)S(1)} %pad_clamp_fusion.2), kind=kCustom, calls=%fused_computation | custom fusion | bytes 8388736 | tf_op jit(solution)/shard_map/jit(_take)/gather | solution.py:126
  24.2 4.2 %fusion = bf16[16,2,128,2,256]{4,2,3,1,0:T(8,128)(2,1)} fusion(bf16[16,2,128,2,256]{4,3,2,1,0:T(2,128)(2,1)} %bitcast.101, pred[16,2]{1,0:T(8,128)(4,1)S(1)} %copy.132, pred[16,2]{1,0:T(8,128)(4,1)S(1)} %copy.131), kind=kLoop, calls=%fused_computation.6 | loop fusion | flops 4194304 | bytes 8388672 | tf_op jit(solution)/shard_map/jit(_where)/select_n | solution.py:129
  28.4 8.0 %all-to-all-start.1 = ((bf16[16,2,128,2,256]{4,2,3,1,0:T(8,128)(2,1)}), bf16[16,2,128,2,256]{4,2,3,1,0:T(8,128)(2,1)}, u32[]{:S(2)}, u32[]{:S(2)}) async-start(bf16[16,2,128,2,256]{4,2,3,1,0:T(8,128)(2,1)} %fusion), calls=%async_computation.1 | async-start | bytes 8388608 | tf_op jit(solution)/shard_map/all_to_all | solution.py:132
  43.8 50.3 %all-to-all-done.1 = bf16[16,2,128,2,256]{4,2,3,1,0:T(8,128)(2,1)} async-done(((bf16[16,2,128,2,256]{4,2,3,1,0:T(8,128)(2,1)}), bf16[16,2,128,2,256]{4,2,3,1,0:T(8,128)(2,1)}, u32[]{:S(2)}, u32[]{:S(2)}) %all-to-all-start.1) | async-done | bytes 4194336 | tf_op jit(solution)/shard_map/all_to_all | solution.py:132
  94.1 4.2 %gather_fusion.1 = bf16[16,128,2,256]{3,1,2,0:T(8,128)(2,1)} fusion(bf16[32,128,2,256]{3,1,2,0:T(8,128)(2,1)} %bitcast.13, s32[1024]{0:T(1024)S(1)} %pad_clamp_fusion.1), kind=kCustom, calls=%fused_computation.1 | custom fusion | bytes 4194368 | tf_op jit(solution)/shard_map/jit(_take)/gather | solution.py:135
  98.3 4.5 %copy.135 = bf16[16,128,2,256]{1,0,3,2:T(8,128)(2,1)} copy(bf16[16,128,2,256]{3,1,2,0:T(8,128)(2,1)} %gather_fusion.1) | data formatting | bytes 4194304 | tf_op jit(solution)/shard_map/jit(_take)/gather | solution.py:135
  102.8 4.2 %gather.28 = bf16[2048,2,2,128]{0,3,2,1:T(8,128)(2,1)} reshape(bf16[16,128,2,256]{1,0,3,2:T(8,128)(2,1)} %copy.135) | data formatting | bytes 4194304 | tf_op jit(solution)/shard_map/jit(_take)/gather | solution.py:135
  107.0 3.9 copy.136
  110.9 2.8 broadcast_select_fusion
  113.7 2.5 fusion.11
  121.0 2.5 fusion.43
  125.7 81.7 %all-reduce.2.cloned.1.call-done = f32[128,2048]{1,0:T(8,128)} async-done(((f32[128,2048]{1,0:T(8,128)}), f32[128,2048]{1,0:T(8,128)}) %all-reduce.2.cloned.1.call-update) | async-done | bytes 1048592 | tf_op jit(solution)/shard_map/psum | solution.py:171
  212.2 2.6 broadcast_in_dim.157
  214.8 11.8 %all-to-all-start.2 = ((bf16[128,3,2048]{2,1,0:T(4,128)(2,1)}), bf16[128,3,2048]{2,1,0:T(4,128)(2,1)}, u32[]{:S(2)}, u32[]{:S(2)}) async-start(bf16[128,3,2048]{2,1,0:T(4,128)(2,1)} %bitcast.102), calls=%async_computation.2 | async-start | bytes 4194304 | tf_op jit(solution)/shard_map/all_to_all | solution.py:199
  226.5 3.8 convert_element_type.113
  230.4 4.5 %reshape.372 = bf16[64,16,2,512]{3,2,1,0:T(2,128)(2,1)} reshape(bf16[64,16,1024]{2,1,0:T(8,128)(2,1)} %convert_element_type.113) | data formatting | bytes 4194304 | tf_op jit(solution)/shard_map/reshape | solution.py:33
  234.9 3.8 convert_element_type.114
  238.7 4.5 %reshape.373 = bf16[64,16,2,512]{3,2,1,0:T(2,128)(2,1)} reshape(bf16[64,16,1024]{2,1,0:T(8,128)(2,1)} %convert_element_type.114) | data formatting | bytes 4194304 | tf_op jit(solution)/shard_map/reshape | solution.py:33
  243.2 10.6 %pad_maximum_fusion = bf16[64,2,16,1024]{3,1,2,0:T(2,128)(2,1)} fusion(bf16[64,2,16,512]{3,1,2,0:T(2,128)(2,1)} %bitcast.104, bf16[64,2,16,512]{3,1,2,0:T(2,128)(2,1)} %bitcast.103), kind=kLoop, calls=%fused_computation.4 | loop fusion | flops 8388608 | bytes 8388608 | tf_op jit(solution)/shard_map/concatenate | solution.py:74
  253.8 5.6 %copy.126 = bf16[64,2,16,1024]{3,2,1,0:T(8,128)(2,1)} copy(bf16[64,2,16,1024]{3,1,2,0:T(2,128)(2,1)} %pad_maximum_fusion) | data formatting | bytes 8388608 | tf_op jit(solution)/shard_map/concatenate | solution.py:74
  259.4 10.2 %all-to-all-start = ((bf16[128,16,1024]{2,1,0:T(8,128)(2,1)}), bf16[128,16,1024]{2,1,0:T(8,128)(2,1)}, u32[]{:S(2)}, u32[]{:S(2)}) async-start(bf16[128,16,1024]{2,1,0:T(8,128)(2,1)} %bitcast.100), calls=%async_computation | async-start | bytes 8388608 | tf_op jit(solution)/shard_map/all_to_all | solution.py:81
  269.6 5.0 %reshape.383 = bf16[384,2048]{1,0:T(8,128)(2,1)} reshape(bf16[128,3,2048]{2,1,0:T(4,128)(2,1)} %all-to-all-done.2) | data formatting | bytes 3145728 | tf_op jit(solution)/shard_map/reshape | solution.py:200
  274.7 46.3 %all-to-all-done = bf16[128,16,1024]{2,1,0:T(8,128)(2,1)} async-done(((bf16[128,16,1024]{2,1,0:T(8,128)(2,1)}), bf16[128,16,1024]{2,1,0:T(8,128)(2,1)}, u32[]{:S(2)}, u32[]{:S(2)}) %all-to-all-start) | async-done | bytes 4194336 | tf_op jit(solution)/shard_map/all_to_all | solution.py:81
  320.9 4.4 %fusion.44 = f32[384,1024]{1,0:T(8,128)S(1)} fusion(bf16[384,2048]{1,0:T(8,128)(2,1)} %reshape.383, bf16[2048,1024]{1,0:T(8,128)(2,1)} %bitcast.19), kind=kOutput, calls=%fused_computation.128 | convolution fusion | flops 1610612736 | bytes 7340032 | tf_op jit(solution)/shard_map/dot_general | solution.py:201
  327.6 5.2 %reshape.384 = bf16[128,3,2048]{2,1,0:T(4,128)(2,1)} reshape(bf16[384,2048]{1,0:T(8,128)(2,1)} %convolution_convert_fusion) | data formatting | bytes 3145728 | tf_op jit(solution)/shard_map/reshape | solution.py:206
  332.7 7.4 %all-to-all-start.3 = ((bf16[128,3,2048]{2,1,0:T(4,128)(2,1)}), bf16[128,3,2048]{2,1,0:T(4,128)(2,1)}, u32[]{:S(2)}, u32[]{:S(2)}) async-start(bf16[128,3,2048]{2,1,0:T(4,128)(2,1)} %reshape.384), calls=%async_computation.3 | async-start | bytes 4194304 | tf_op jit(solution)/shard_map/all_to_all | solution.py:208
  344.3 24.4 %all-to-all-done.3 = bf16[128,3,2048]{2,1,0:T(4,128)(2,1)} async-done(((bf16[128,3,2048]{2,1,0:T(4,128)(2,1)}), bf16[128,3,2048]{2,1,0:T(4,128)(2,1)}, u32[]{:S(2)}, u32[]{:S(2)}) %all-to-all-start.3) | async-done | bytes 1572896 | tf_op jit(solution)/shard_map/all_to_all | solution.py:208
  368.7 3.7 convert_add_fusion
  372.4 3.8 add.191
  376.2 2.9 gather_fusion.2
  380.7 3.8 copy.168
  385.5 4.6 %copy.170 = bf16[1,2048,1024]{2,1,0:T(8,128)(2,1)} copy(bf16[1,2048,1024]{2,1,0:T(8,128)(2,1)} %bitcast.3) | data formatting | bytes 8388608
  (129 shorter events, 34.6 us)
Async XLA Ops:
  7.2 318.2 %copy-start = (bf16[1,512,2048]{2,1,0:T(8,128)(2,1)S(1)}, bf16[1,512,2048]{2,1,0:T(8,128)(2,1)}, u32[]{:S(2)}) copy-start(bf16[1,512,2048]{2,1,0:T(8,128)(2,1)} %param.32) | copy-start | bytes 6291460
  7.2 7.0 %copy-start.1 = (bf16[8,128,2,256]{3,2,1,0:T(2,128)(2,1)S(1)}, bf16[8,128,2,256]{3,2,1,0:T(2,128)(2,1)}, u32[]{:S(2)}) copy-start(bf16[8,128,2,256]{3,2,1,0:T(2,128)(2,1)} %param.34) | copy-start | bytes 3145732
  7.2 106.5 %all-gather.3.cloned.1.call-start = ((), (), s32[]{:S(2)}) async-start(), calls=%async_computation.4 | async-start | bytes 3342336 | tf_op jit(solution)/shard_map/all_gather | solution.py:69
  28.4 8.1 %copy-start.8 = (f32[256,128]{1,0:T(8,128)S(1)}, f32[256,128]{1,0:T(8,128)}, u32[]{:S(2)}) copy-start(f32[256,128]{1,0:T(8,128)} %param.29) | copy-start | bytes 393220
  28.4 8.8 %copy-start.13 = (s32[32]{0:T(128)S(1)}, s32[32]{0:T(128)}, u32[]{:S(2)}) copy-start(s32[32]{0:T(128)} %param.36) | copy-start | bytes 388
  28.4 8.9 %copy-start.14 = (s32[32]{0:T(128)S(1)}, s32[32]{0:T(128)}, u32[]{:S(2)}) copy-start(s32[32]{0:T(128)} %param.35) | copy-start | bytes 388
  28.4 14.7 %copy-start.2 = (bf16[128,2048]{1,0:T(8,128)(2,1)S(1)}, bf16[128,2048]{1,0:T(8,128)(2,1)}, u32[]{:S(2)}) copy-start(bf16[128,2048]{1,0:T(8,128)(2,1)} %param.21) | copy-start | bytes 1572868
  28.4 65.7 %all-to-all-start.1 = ((bf16[16,2,128,2,256]{4,2,3,1,0:T(8,128)(2,1)}), bf16[16,2,128,2,256]{4,2,3,1,0:T(8,128)(2,1)}, u32[]{:S(2)}, u32[]{:S(2)}) async-start(bf16[16,2,128,2,256]{4,2,3,1,0:T(8,128)(2,1)} %fusion), calls=%async_computation.1 | async-start | bytes 8388608 | tf_op jit(solution)/shard_map/all_to_all | solution.py:132
  36.4 84.6 %all-gather.5.cloned.1.call-start = ((), (), s32[]{:S(2)}) async-start(), calls=%async_computation.5 | async-start | bytes 1114112 | tf_op jit(solution)/shard_map/all_gather | solution.py:70
  37.2 170.2 %all-reduce.2.cloned.1.call-start = ((), (), s32[]{:S(2)}) async-start(), calls=%async_computation.6 | async-start | bytes 2097152 | tf_op jit(solution)/shard_map/psum | solution.py:171
  110.9 2.8 copy-start.10
  113.7 4.2 %copy-start.11 = (f32[128]{0:T(128)S(1)}, f32[128]{0:T(128)}, u32[]{:S(2)}) copy-start(f32[128]{0:T(128)} %param.24) | copy-start | bytes 1540
  113.7 4.2 %copy-start.12 = (f32[128]{0:T(128)S(1)}, f32[128]{0:T(128)}, u32[]{:S(2)}) copy-start(f32[128]{0:T(128)} %param.23) | copy-start | bytes 1540
  116.2 0.8 copy-start.5
  117.9 1.6 copy-start.4
  121.0 3.6 copy-start.7
  123.6 84.9 %copy-start.9 = (f32[2048]{0:T(1024)S(1)}, f32[2048]{0:T(1024)}, u32[]{:S(2)}) copy-start(f32[2048]{0:T(1024)} %param.25) | copy-start | bytes 24580
  214.8 44.6 %all-to-all-start.2 = ((bf16[128,3,2048]{2,1,0:T(4,128)(2,1)}), bf16[128,3,2048]{2,1,0:T(4,128)(2,1)}, u32[]{:S(2)}, u32[]{:S(2)}) async-start(bf16[128,3,2048]{2,1,0:T(4,128)(2,1)} %bitcast.102), calls=%async_computation.2 | async-start | bytes 4194304 | tf_op jit(solution)/shard_map/all_to_all | solution.py:199
  259.4 61.5 %all-to-all-start = ((bf16[128,16,1024]{2,1,0:T(8,128)(2,1)}), bf16[128,16,1024]{2,1,0:T(8,128)(2,1)}, u32[]{:S(2)}, u32[]{:S(2)}) async-start(bf16[128,16,1024]{2,1,0:T(8,128)(2,1)} %bitcast.100), calls=%async_computation | async-start | bytes 8388608 | tf_op jit(solution)/shard_map/all_to_all | solution.py:81
  332.7 9.8 %copy-start.6 = (bf16[2048,64]{0,1:T(8,128)(2,1)S(1)}, bf16[2048,64]{0,1:T(8,128)(2,1)}, u32[]{:S(2)}) copy-start(bf16[2048,64]{0,1:T(8,128)(2,1)} %param.33) | copy-start | bytes 786436
  332.7 36.0 %all-to-all-start.3 = ((bf16[128,3,2048]{2,1,0:T(4,128)(2,1)}), bf16[128,3,2048]{2,1,0:T(4,128)(2,1)}, u32[]{:S(2)}, u32[]{:S(2)}) async-start(bf16[128,3,2048]{2,1,0:T(4,128)(2,1)} %reshape.384), calls=%async_computation.3 | async-start | bytes 4194304 | tf_op jit(solution)/shard_map/all_to_all | solution.py:208
  380.7 3.8 copy-start.3
Sparse Core Ops, SparseCore 0:
  11.0 65.4 all-gather.2
  78.7 38.0 all-gather.4
  123.7 83.5 all-reduce.1
where the time goes:
time: 398 us; the launch traced here: 397 us
  waiting for transfers between devices  203 us (51%)
  local copies, waits for them, and re-layouts  80.7 us (20%)
  other arithmetic  46.5 us (12%)
  starting transfers between devices  37.6 us (9%)
  matrix products  15 us (4%)
  between operations  14.2 us (4%)
    psum x1, waiting for transfers between devices, body(): mixed_all = lax.psum(head_terms, 'tp')  81.7 us
    all_to_all x1, waiting for transfers between devices, body(): lax.all_to_all(outgoing_pages, 'req', split_axis=0, concat_axis=0, tiled=...  50.3 us
    all_to_all x1, waiting for transfers between devices, body(): lax.all_to_all(packed, ('req', 'tp'), split_axis=0, concat_axis=1, tiled=...  46.3 us
    all_to_all x1, waiting for transfers between devices, body(): lax.all_to_all(expert_rows, ('req', 'tp'), split_axis=0, concat_axis=0, t...  24.4 us
    gather x4, local copies, waits for them, and re-layouts, body(): jnp.take(arrived_pages.reshape((req_count * capacity,) + page_shape), own...  16.8 us
    unnamed x35, local copies, waits for them, and re-layouts  11.9 us
    all_to_all x1, starting transfers between devices, body(): lax.all_to_all(send_rows, ('req', 'tp'), split_axis=0, concat_axis=0, til...  11.8 us
    concatenate x1, other arithmetic, body(): jnp.concatenate([split_halves(gate_weight.astype(jnp.bfloat16)), split_ha...  10.6 us
  transfers between devices with their start and end apart: 7, of which 4 were waited for; matrix products, arithmetic and copies ran while one was open for 24% of the time, Pallas kernels for 0%

commit v1 on v0

--- a/solution.py
+++ b/solution.py
@@ -168,8 +168,8 @@
     shard_rows = routes.shape[0]
     row_start = lane_index * shard_rows
     head_terms = jnp.dot(attended, server_out, preferred_element_type=jnp.float32)
-    mixed_all = lax.psum(head_terms, "tp")
-    mixed_own = lax.dynamic_slice_in_dim(mixed_all, row_start, shard_rows, 0)
+    server_gate_up, head_terms = lax.optimization_barrier((server_gate_up, head_terms))
+    mixed_own = lax.psum_scatter(head_terms, "tp", scatter_dimension=0, tiled=True)
     residual_own = lax.dynamic_slice_in_dim(tokens_f32, row_start, shard_rows, 0) + mixed_own
     moe_own = rms_scale(residual_own, moe_gain).astype(jnp.bfloat16)
     logits = jnp.dot(moe_own, router_weight, preferred_element_type=jnp.float32)

time: 398 us -> 358 us (0.90)
  waiting for transfers between devices: 203 us -> 139 us
  blocking collectives: 0 us -> 38 us
  starting transfers between devices: 37.6 us -> 24.4 us
    psum x1 -> x0, waiting for transfers between devices: 81.7 us -> none  [body(): mixed_all = lax.psum(head_terms, 'tp')]
    reduce_scatter x0 -> x1, waiting for transfers between devices: none -> 72.8 us  [body(): lax.psum_scatter(head_terms, 'tp', scatter_dimension=0, tiled=True)]
    all_to_all x1, waiting for transfers between devices: 46.3 us -> 0.01 us  [body(): lax.all_to_all(packed, ('req', 'tp'), split_axis=0, concat_axis=1, tiled=...]
    all_to_all x0 -> x1, blocking collectives: none -> 38 us  [body(): lax.all_to_all(send_rows, ('req', 'tp'), split_axis=0, concat_axis=0, til...]
    all_to_all x1, waiting for transfers between devices: 50.3 us -> 17.4 us  [body(): lax.all_to_all(outgoing_pages, 'req', split_axis=0, concat_axis=0, tiled=...]
    all_gather x1, waiting for transfers between devices: 0.02 us -> 24.2 us  [body(): lax.all_gather(out_weight.astype(jnp.bfloat16), 'req', axis=1, tiled=True)]
    all_to_all x1 -> x0, starting transfers between devices: 11.8 us -> none  [body(): lax.all_to_all(send_rows, ('req', 'tp'), split_axis=0, concat_axis=0, til...]
  transfers between devices with their start and end apart: 7 -> 6, of which waited for: 4 -> 4; matrix products, arithmetic and copies ran while one was open for 24% -> 26% of each run, Pallas kernels for 0% -> 0%
where the time goes in v1:
time: 358 us; the launch traced here: 356 us
  waiting for transfers between devices  139 us (39%)
  local copies, waits for them, and re-layouts  79.4 us (22%)
  other arithmetic  46.5 us (13%)
  blocking collectives  38 us (11%)
  starting transfers between devices  24.4 us (7%)
  matrix products  15 us (4%)
  between operations  14.2 us (4%)
    reduce_scatter x1, waiting for transfers between devices, body(): lax.psum_scatter(head_terms, 'tp', scatter_dimension=0, tiled=True)  72.8 us
    all_to_all x1, blocking collectives, body(): lax.all_to_all(send_rows, ('req', 'tp'), split_axis=0, concat_axis=0, til...  38 us
    all_to_all x1, waiting for transfers between devices, body(): lax.all_to_all(expert_rows, ('req', 'tp'), split_axis=0, concat_axis=0, t...  24.4 us
    all_gather x1, waiting for transfers between devices, body(): lax.all_gather(out_weight.astype(jnp.bfloat16), 'req', axis=1, tiled=True)  24.2 us
    all_to_all x1, waiting for transfers between devices, body(): lax.all_to_all(outgoing_pages, 'req', split_axis=0, concat_axis=0, tiled=...  17.4 us
    gather x4, local copies, waits for them, and re-layouts, body(): jnp.take(arrived_pages.reshape((req_count * capacity,) + page_shape), own...  16.8 us
    unnamed x35, local copies, waits for them, and re-layouts  11.9 us
    concatenate x1, other arithmetic, body(): jnp.concatenate([split_halves(gate_weight.astype(jnp.bfloat16)), split_ha...  10.6 us
  transfers between devices with their start and end apart: 6, of which 4 were waited for; matrix products, arithmetic and copies ran while one was open for 26% of the time, Pallas kernels for 0%

profile of v1, /device:TPU:1, one launch (start us, length us, event | category | flops | bytes accessed | tf_op | source)
XLA Modules:
  0.0 356.2 jit_solution(3697008645255823486)
XLA Ops:
  14.1 10.0 %gather_fusion = bf16[32,128,2,256]{3,2,1,0:T(2,128)(2,1)} fusion(bf16[8,128,2,256]{3,2,1,0:T(2,128)(2,1)S(1)} %copy-done.1, s32[1024]{0:T(1024)S(1)} %pad_clamp_fusion.2), kind=kCustom, calls=%fused_computation | custom fusion | bytes 8388736 | tf_op jit(solution)/shard_map/jit(_take)/gather | solution.py:126
  24.2 4.1 %fusion.2 = bf16[16,2,128,2,256]{4,2,3,1,0:T(8,128)(2,1)} fusion(bf16[16,2,128,2,256]{4,3,2,1,0:T(2,128)(2,1)} %bitcast.102, pred[16,2]{1,0:T(8,128)(4,1)S(1)} %copy.132, pred[16,2]{1,0:T(8,128)(4,1)S(1)} %copy.131), kind=kLoop, calls=%fused_computation.8 | loop fusion | flops 4194304 | bytes 8388672 | tf_op jit(solution)/shard_map/jit(_where)/select_n | solution.py:129
  28.3 8.1 %all-to-all-start.1 = ((bf16[16,2,128,2,256]{4,2,3,1,0:T(8,128)(2,1)}), bf16[16,2,128,2,256]{4,2,3,1,0:T(8,128)(2,1)}, u32[]{:S(2)}, u32[]{:S(2)}) async-start(bf16[16,2,128,2,256]{4,2,3,1,0:T(8,128)(2,1)} %fusion.2), calls=%async_computation.1 | async-start | bytes 8388608 | tf_op jit(solution)/shard_map/all_to_all | solution.py:132
  37.8 3.9 %convert_element_type.113 = bf16[64,16,1024]{2,1,0:T(8,128)(2,1)} convert(f32[64,16,1024]{2,1,0:T(8,128)} %param.30) | non-fusion elementwise | flops 1048576 | bytes 6291456 | tf_op jit(solution)/shard_map/convert_element_type | solution.py:76
  41.7 4.5 %reshape.371 = bf16[64,16,2,512]{3,2,1,0:T(2,128)(2,1)} reshape(bf16[64,16,1024]{2,1,0:T(8,128)(2,1)} %convert_element_type.113) | data formatting | bytes 4194304 | tf_op jit(solution)/shard_map/reshape | solution.py:33
  46.3 3.9 %convert_element_type.114 = bf16[64,16,1024]{2,1,0:T(8,128)(2,1)} convert(f32[64,16,1024]{2,1,0:T(8,128)} %param.31) | non-fusion elementwise | flops 1048576 | bytes 6291456 | tf_op jit(solution)/shard_map/convert_element_type | solution.py:77
  50.1 4.5 %reshape.372 = bf16[64,16,2,512]{3,2,1,0:T(2,128)(2,1)} reshape(bf16[64,16,1024]{2,1,0:T(8,128)(2,1)} %convert_element_type.114) | data formatting | bytes 4194304 | tf_op jit(solution)/shard_map/reshape | solution.py:33
  54.7 10.6 %pad_maximum_fusion = bf16[64,2,16,1024]{3,1,2,0:T(2,128)(2,1)} fusion(bf16[64,2,16,512]{3,1,2,0:T(2,128)(2,1)} %bitcast.105, bf16[64,2,16,512]{3,1,2,0:T(2,128)(2,1)} %bitcast.104), kind=kLoop, calls=%fused_computation.4 | loop fusion | flops 8388608 | bytes 8388608 | tf_op jit(solution)/shard_map/concatenate | solution.py:74
  65.3 5.7 %copy.126 = bf16[64,2,16,1024]{3,2,1,0:T(8,128)(2,1)} copy(bf16[64,2,16,1024]{3,1,2,0:T(2,128)(2,1)} %pad_maximum_fusion) | data formatting | bytes 8388608 | tf_op jit(solution)/shard_map/concatenate | solution.py:74
  76.8 17.4 %all-to-all-done.1 = bf16[16,2,128,2,256]{4,2,3,1,0:T(8,128)(2,1)} async-done(((bf16[16,2,128,2,256]{4,2,3,1,0:T(8,128)(2,1)}), bf16[16,2,128,2,256]{4,2,3,1,0:T(8,128)(2,1)}, u32[]{:S(2)}, u32[]{:S(2)}) %all-to-all-start.1) | async-done | bytes 4194336 | tf_op jit(solution)/shard_map/all_to_all | solution.py:132
  94.2 9.6 %all-to-all-start = ((bf16[128,16,1024]{2,1,0:T(8,128)(2,1)}), bf16[128,16,1024]{2,1,0:T(8,128)(2,1)}, u32[]{:S(2)}, u32[]{:S(2)}) async-start(bf16[128,16,1024]{2,1,0:T(8,128)(2,1)} %bitcast.101), calls=%async_computation | async-start | bytes 8388608 | tf_op jit(solution)/shard_map/all_to_all | solution.py:81
  103.9 4.2 %gather_fusion.1 = bf16[16,128,2,256]{3,1,2,0:T(8,128)(2,1)} fusion(bf16[32,128,2,256]{3,1,2,0:T(8,128)(2,1)} %bitcast.13, s32[1024]{0:T(1024)S(1)} %pad_clamp_fusion.1), kind=kCustom, calls=%fused_computation.1 | custom fusion | bytes 4194368 | tf_op jit(solution)/shard_map/jit(_take)/gather | solution.py:135
  108.1 4.5 %copy.135 = bf16[16,128,2,256]{1,0,3,2:T(8,128)(2,1)} copy(bf16[16,128,2,256]{3,1,2,0:T(8,128)(2,1)} %gather_fusion.1) | data formatting | bytes 4194304 | tf_op jit(solution)/shard_map/jit(_take)/gather | solution.py:135
  112.6 4.2 %gather.28 = bf16[2048,2,2,128]{0,3,2,1:T(8,128)(2,1)} reshape(bf16[16,128,2,256]{1,0,3,2:T(8,128)(2,1)} %copy.135) | data formatting | bytes 4194304 | tf_op jit(solution)/shard_map/jit(_take)/gather | solution.py:135
  116.7 3.9 %copy.136 = bf16[2048,2,2,128]{3,0,2,1:T(8,128)(2,1)} copy(bf16[2048,2,2,128]{0,3,2,1:T(8,128)(2,1)} %gather.28) | data formatting | bytes 4194304 | tf_op jit(solution)/shard_map/jit(_take)/gather | solution.py:135
  120.6 2.8 broadcast_select_fusion
  123.4 2.5 fusion.13
  130.7 24.2 %all-gather.5.cloned.1.call-done = bf16[256,2048]{1,0:T(8,128)(2,1)} async-done(((bf16[256,128]{1,0:T(8,128)(2,1)}), bf16[256,2048]{1,0:T(8,128)(2,1)}) %all-gather.5.cloned.1.call-update) | async-done | bytes 1048592 | tf_op jit(solution)/shard_map/all_gather | solution.py:70
  154.9 2.5 fusion.45
  159.6 72.8 %reduce-scatter.2.cloned.1.call-done = f32[16,2048]{1,0:T(8,128)} async-done(((f32[128,2048]{1,0:T(8,128)}), f32[16,2048]{1,0:T(8,128)}) %reduce-scatter.2.cloned.1.call-update) | async-done | bytes 131088 | tf_op jit(solution)/shard_map/reduce_scatter | solution.py:172
  234.7 2.4 broadcast_in_dim.156
  238.4 38.0 %all_to_all.27 = bf16[128,3,2048]{2,1,0:T(4,128)(2,1)} all-to-all(bf16[128,3,2048]{2,1,0:T(4,128)(2,1)S(1)} %bitcast.103), channel_id=1, replica_groups=mesh['req'=16,'tp'=8] {'req','tp'}, dimensions={0} | all-to-all | bytes 3145728 | tf_op jit(solution)/shard_map/all_to_all | solution.py:199
  276.4 5.0 %reshape.382 = bf16[384,2048]{1,0:T(8,128)(2,1)} reshape(bf16[128,3,2048]{2,1,0:T(4,128)(2,1)} %all_to_all.27) | data formatting | bytes 3145728 | tf_op jit(solution)/shard_map/reshape | solution.py:200
  281.4 4.4 %fusion = f32[384,1024]{1,0:T(8,128)S(1)} fusion(bf16[384,2048]{1,0:T(8,128)(2,1)} %reshape.382, bf16[1,2048,1024]{2,1,0:T(8,128)(2,1)} %bitcast.3), kind=kOutput, calls=%fused_computation.5 | convolution fusion | flops 1610612736 | bytes 7340032 | tf_op jit(solution)/shard_map/dot_general | solution.py:201
  288.1 5.2 %reshape.383 = bf16[128,3,2048]{2,1,0:T(4,128)(2,1)} reshape(bf16[384,2048]{1,0:T(8,128)(2,1)} %convolution_convert_fusion) | data formatting | bytes 3145728 | tf_op jit(solution)/shard_map/reshape | solution.py:206
  293.2 6.6 %all-to-all-start.3 = ((bf16[128,3,2048]{2,1,0:T(4,128)(2,1)}), bf16[128,3,2048]{2,1,0:T(4,128)(2,1)}, u32[]{:S(2)}, u32[]{:S(2)}) async-start(bf16[128,3,2048]{2,1,0:T(4,128)(2,1)} %reshape.383), calls=%async_computation.4 | async-start | bytes 4194304 | tf_op jit(solution)/shard_map/all_to_all | solution.py:208
  303.9 24.4 %all-to-all-done.3 = bf16[128,3,2048]{2,1,0:T(4,128)(2,1)} async-done(((bf16[128,3,2048]{2,1,0:T(4,128)(2,1)}), bf16[128,3,2048]{2,1,0:T(4,128)(2,1)}, u32[]{:S(2)}, u32[]{:S(2)}) %all-to-all-start.3) | async-done | bytes 1572896 | tf_op jit(solution)/shard_map/all_to_all | solution.py:208
  328.3 3.7 %convert_add_fusion = f32[64,1,3,2048]{3,2,0,1:T(4,128)} fusion(bf16[64,2,3,2048]{3,2,1,0:T(4,128)(2,1)} %bitcast.21), kind=kLoop, calls=%fused_computation.15 | loop fusion | flops 1179648 | bytes 3145728 | tf_op jit(solution)/shard_map/add | solution.py:210
  332.0 3.8 %add.190 = f32[192,2048]{1,0:T(8,128)} reshape(f32[64,1,3,2048]{3,2,0,1:T(4,128)} %convert_add_fusion) | data formatting | bytes 3145728 | tf_op jit(solution)/shard_map/add | solution.py:210
  335.8 2.9 gather_fusion.2
  340.2 3.8 %copy.167 = bf16[2048,768]{1,0:T(8,128)(2,1)} copy(bf16[2048,768]{1,0:T(8,128)(2,1)} %all-gather.3.cloned.1.call-done) | data formatting | bytes 6291456
  345.1 4.6 %copy.169 = bf16[1,2048,1024]{2,1,0:T(8,128)(2,1)} copy(bf16[1,2048,1024]{2,1,0:T(8,128)(2,1)} %bitcast.3) | data formatting | bytes 8388608
  (128 shorter events, 33.3 us)
Async XLA Ops:
  7.2 278.7 %copy-start = (bf16[1,512,2048]{2,1,0:T(8,128)(2,1)S(1)}, bf16[1,512,2048]{2,1,0:T(8,128)(2,1)}, u32[]{:S(2)}) copy-start(bf16[1,512,2048]{2,1,0:T(8,128)(2,1)} %param.32) | copy-start | bytes 6291460
  7.2 7.0 %copy-start.1 = (bf16[8,128,2,256]{3,2,1,0:T(2,128)(2,1)S(1)}, bf16[8,128,2,256]{3,2,1,0:T(2,128)(2,1)}, u32[]{:S(2)}) copy-start(bf16[8,128,2,256]{3,2,1,0:T(2,128)(2,1)} %param.34) | copy-start | bytes 3145732
  7.2 116.2 %all-gather.3.cloned.1.call-start = ((), (), s32[]{:S(2)}) async-start(), calls=%async_computation.5 | async-start | bytes 3342336 | tf_op jit(solution)/shard_map/all_gather | solution.py:69
  28.3 8.2 %copy-start.8 = (f32[256,128]{1,0:T(8,128)S(1)}, f32[256,128]{1,0:T(8,128)}, u32[]{:S(2)}) copy-start(f32[256,128]{1,0:T(8,128)} %param.29) | copy-start | bytes 393220
  28.3 8.9 %copy-start.13 = (s32[32]{0:T(128)S(1)}, s32[32]{0:T(128)}, u32[]{:S(2)}) copy-start(s32[32]{0:T(128)} %param.36) | copy-start | bytes 388
  28.3 8.9 %copy-start.14 = (s32[32]{0:T(128)S(1)}, s32[32]{0:T(128)}, u32[]{:S(2)}) copy-start(s32[32]{0:T(128)} %param.35) | copy-start | bytes 388
  28.3 65.9 %all-to-all-start.1 = ((bf16[16,2,128,2,256]{4,2,3,1,0:T(8,128)(2,1)}), bf16[16,2,128,2,256]{4,2,3,1,0:T(8,128)(2,1)}, u32[]{:S(2)}, u32[]{:S(2)}) async-start(bf16[16,2,128,2,256]{4,2,3,1,0:T(8,128)(2,1)} %fusion.2), calls=%async_computation.1 | async-start | bytes 8388608 | tf_op jit(solution)/shard_map/all_to_all | solution.py:132
  36.4 118.5 %all-gather.5.cloned.1.call-start = ((), (), s32[]{:S(2)}) async-start(), calls=%async_computation.6 | async-start | bytes 1114112 | tf_op jit(solution)/shard_map/all_gather | solution.py:70
  65.2 10.9 %copy-start.2 = (bf16[128,2048]{1,0:T(8,128)(2,1)S(1)}, bf16[128,2048]{1,0:T(8,128)(2,1)}, u32[]{:S(2)}) copy-start(bf16[128,2048]{1,0:T(8,128)(2,1)} %param.21) | copy-start | bytes 1572868
  94.2 63.3 %all-to-all-start = ((bf16[128,16,1024]{2,1,0:T(8,128)(2,1)}), bf16[128,16,1024]{2,1,0:T(8,128)(2,1)}, u32[]{:S(2)}, u32[]{:S(2)}) async-start(bf16[128,16,1024]{2,1,0:T(8,128)(2,1)} %bitcast.101), calls=%async_computation | async-start | bytes 8388608 | tf_op jit(solution)/shard_map/all_to_all | solution.py:81
  103.8 128.5 %reduce-scatter.2.cloned.1.call-start = ((), (), s32[]{:S(2)}) async-start(), calls=%async_computation.7 | async-start | bytes 1179648 | tf_op jit(solution)/shard_map/reduce_scatter | solution.py:172
  120.6 2.8 copy-start.10
  123.4 4.3 %copy-start.11 = (f32[128]{0:T(128)S(1)}, f32[128]{0:T(128)}, u32[]{:S(2)}) copy-start(f32[128]{0:T(128)} %param.24) | copy-start | bytes 1540
  123.4 4.3 %copy-start.12 = (f32[128]{0:T(128)S(1)}, f32[128]{0:T(128)}, u32[]{:S(2)}) copy-start(f32[128]{0:T(128)} %param.23) | copy-start | bytes 1540
  126.0 0.8 copy-start.5
  127.6 1.6 copy-start.4
  154.9 3.6 %copy-start.7 = (s32[16,8]{0,1:T(8,128)S(1)}, s32[16,8]{0,1:T(8,128)}, u32[]{:S(2)}) copy-start(s32[16,8]{0,1:T(8,128)} %param.39) | copy-start | bytes 1540
  157.5 76.0 %copy-start.9 = (f32[2048]{0:T(1024)S(1)}, f32[2048]{0:T(1024)}, u32[]{:S(2)}) copy-start(f32[2048]{0:T(1024)} %param.25) | copy-start | bytes 24580
  293.2 8.9 %copy-start.6 = (bf16[2048,64]{0,1:T(8,128)(2,1)S(1)}, bf16[2048,64]{0,1:T(8,128)(2,1)}, u32[]{:S(2)}) copy-start(bf16[2048,64]{0,1:T(8,128)(2,1)} %param.33) | copy-start | bytes 786436
  293.2 35.1 %all-to-all-start.3 = ((bf16[128,3,2048]{2,1,0:T(4,128)(2,1)}), bf16[128,3,2048]{2,1,0:T(4,128)(2,1)}, u32[]{:S(2)}, u32[]{:S(2)}) async-start(bf16[128,3,2048]{2,1,0:T(4,128)(2,1)} %reshape.383), calls=%async_computation.4 | async-start | bytes 4194304 | tf_op jit(solution)/shard_map/all_to_all | solution.py:208
  340.2 3.8 %copy-start.3 = (bf16[256,2048]{1,0:T(8,128)(2,1)S(1)}, bf16[256,2048]{1,0:T(8,128)(2,1)}, u32[]{:S(2)}) copy-start(bf16[256,2048]{1,0:T(8,128)(2,1)} %all-gather.5.cloned.1.call-done) | copy-start | bytes 3145732
Sparse Core Ops, SparseCore 0:
  11.0 65.5 all-gather.2
  78.8 76.1 all-gather.4
  159.2 73.1 reduce-scatter.1

commit v2 on v1

--- a/solution.py
+++ b/solution.py
@@ -1,9 +1,14 @@
+import functools
 import math
 
 import jax
 import jax.numpy as jnp
 from jax import lax
+from jax.experimental import pallas as pl
+from jax.experimental.pallas import tpu as pltpu
 from jax.sharding import PartitionSpec as P
+
+MESH = pl.DeviceIdType.MESH
 
 norm_eps = 1e-06
 rope_base = 50000.0
@@ -31,6 +36,64 @@
 def split_halves(weights):
     expert_count, rows_here, hidden_units = weights.shape
     return weights.reshape(expert_count, rows_here, 2, hidden_units // 2).transpose(0, 2, 1, 3)
+
+
+def scatter_sum_kernel(parts, x_ref, out_ref, held, send_sem, recv_sem):
+    me = lax.axis_index("tp")
+    group = lax.axis_index("req")
+    rows = out_ref.shape[0]
+    barrier = pltpu.get_barrier_semaphore()
+    for step in range(1, parts):
+        peer = lax.rem(me + step, parts)
+        pl.semaphore_signal(barrier, inc=1, device_id=(group, peer), device_id_type=MESH)
+    pl.semaphore_wait(barrier, parts - 1)
+
+    def outgoing(peer):
+        return pltpu.make_async_remote_copy(
+            src_ref=x_ref.at[pl.ds(pl.multiple_of(peer * rows, rows), rows)],
+            dst_ref=held.at[me],
+            send_sem=send_sem.at[peer],
+            recv_sem=recv_sem.at[me],
+            device_id=(group, peer),
+            device_id_type=MESH,
+        )
+
+    def incoming(peer):
+        return pltpu.make_async_remote_copy(
+            src_ref=x_ref.at[pl.ds(pl.multiple_of(me * rows, rows), rows)],
+            dst_ref=held.at[peer],
+            send_sem=send_sem.at[peer],
+            recv_sem=recv_sem.at[peer],
+            device_id=(group, peer),
+            device_id_type=MESH,
+        )
+
+    for step in range(1, parts):
+        outgoing(lax.rem(me + step, parts)).start()
+    total = x_ref[pl.ds(pl.multiple_of(me * rows, rows), rows), :]
+    for step in range(1, parts):
+        peer = lax.rem(me + parts - step, parts)
+        incoming(peer).wait_recv()
+        total = total + held[peer]
+    for step in range(1, parts):
+        outgoing(lax.rem(me + step, parts)).wait_send()
+    out_ref[...] = total
+
+
+def scatter_sum(x, parts):
+    rows = x.shape[0] // parts
+    return pl.pallas_call(
+        functools.partial(scatter_sum_kernel, parts),
+        out_shape=jax.ShapeDtypeStruct((rows, x.shape[1]), x.dtype),
+        in_specs=[pl.BlockSpec(memory_space=pltpu.VMEM)],
+        out_specs=pl.BlockSpec(memory_space=pltpu.VMEM),
+        scratch_shapes=[
+            pltpu.VMEM((parts, rows, x.shape[1]), x.dtype),
+            pltpu.SemaphoreType.DMA((parts,)),
+            pltpu.SemaphoreType.DMA((parts,)),
+        ],
+        compiler_params=pltpu.CompilerParams(collective_id=0, has_side_effects=True),
+    )(x)
 
 
 def body(
@@ -169,7 +232,7 @@
     row_start = lane_index * shard_rows
     head_terms = jnp.dot(attended, server_out, preferred_element_type=jnp.float32)
     server_gate_up, head_terms = lax.optimization_barrier((server_gate_up, head_terms))
-    mixed_own = lax.psum_scatter(head_terms, "tp", scatter_dimension=0, tiled=True)
+    mixed_own = scatter_sum(head_terms, lax.axis_size("tp"))
     residual_own = lax.dynamic_slice_in_dim(tokens_f32, row_start, shard_rows, 0) + mixed_own
     moe_own = rms_scale(residual_own, moe_gain).astype(jnp.bfloat16)
     logits = jnp.dot(moe_own, router_weight, preferred_element_type=jnp.float32)

time: 358 us -> 307 us (0.86)
  waiting for transfers between devices: 139 us -> 63.5 us
  Pallas kernels: 0 us -> 22.7 us
    reduce_scatter x1 -> x0, waiting for transfers between devices: 72.8 us -> none  [body(): lax.psum_scatter(head_terms, 'tp', scatter_dimension=0, tiled=True)]
    pallas_call x0 -> x1, Pallas kernels: none -> 22.7 us  [scatter_sum(): pl.pallas_call(functools.partial(scatter_sum_kernel, parts), out_shape=ja...]
  transfers between devices with their start and end apart: 6 -> 5, of which waited for: 4 -> 3; matrix products, arithmetic and copies ran while one was open for 26% -> 30% of each run, Pallas kernels for 0% -> 0%
where the time goes in v2:
time: 307 us; the launch traced here: 305 us
  local copies, waits for them, and re-layouts  79.4 us (26%)
  waiting for transfers between devices  63.5 us (21%)
  other arithmetic  46.6 us (15%)
  blocking collectives  38.9 us (13%)
  starting transfers between devices  24.7 us (8%)
  Pallas kernels  22.7 us (7%)
  matrix products  15 us (5%)
  between operations  14.5 us (5%)
    all_to_all x1, blocking collectives, body(): lax.all_to_all(send_rows, ('req', 'tp'), split_axis=0, concat_axis=0, til...  38.9 us
    all_to_all x1, waiting for transfers between devices, body(): lax.all_to_all(expert_rows, ('req', 'tp'), split_axis=0, concat_axis=0, t...  24.3 us
    all_gather x1, waiting for transfers between devices, body(): lax.all_gather(out_weight.astype(jnp.bfloat16), 'req', axis=1, tiled=True)  24.1 us
    pallas_call x1, Pallas kernels, scatter_sum(): pl.pallas_call(functools.partial(scatter_sum_kernel, parts), out_shape=ja...  22.7 us
    gather x4, local copies, waits for them, and re-layouts, body(): jnp.take(arrived_pages.reshape((req_count * capacity,) + page_shape), own...  16.8 us
    all_to_all x1, waiting for transfers between devices, body(): lax.all_to_all(outgoing_pages, 'req', split_axis=0, concat_axis=0, tiled=...  15 us
    unnamed x35, local copies, waits for them, and re-layouts  11.9 us
    concatenate x1, other arithmetic, body(): jnp.concatenate([split_halves(gate_weight.astype(jnp.bfloat16)), split_ha...  10.6 us
  transfers between devices with their start and end apart: 5, of which 3 were waited for; matrix products, arithmetic and copies ran while one was open for 30% of the time, Pallas kernels for 0%

profile of v2, /device:TPU:1, one launch (start us, length us, event | category | flops | bytes accessed | tf_op | source)
XLA Modules:
  0.0 305.2 jit_solution(14915285220935237210)
XLA Ops:
  14.1 10.0 %gather_fusion = bf16[32,128,2,256]{3,2,1,0:T(2,128)(2,1)} fusion(bf16[8,128,2,256]{3,2,1,0:T(2,128)(2,1)S(1)} %copy-done.1, s32[1024]{0:T(1024)S(1)} %pad_clamp_fusion.2), kind=kCustom, calls=%fused_computation | custom fusion | bytes 8388736 | tf_op jit(solution)/shard_map/jit(_take)/gather | solution.py:189
  24.2 4.1 %fusion.2 = bf16[16,2,128,2,256]{4,2,3,1,0:T(8,128)(2,1)} fusion(bf16[16,2,128,2,256]{4,3,2,1,0:T(2,128)(2,1)} %bitcast.102, pred[16,2]{1,0:T(8,128)(4,1)S(1)} %copy.132, pred[16,2]{1,0:T(8,128)(4,1)S(1)} %copy.131), kind=kLoop, calls=%fused_computation.8 | loop fusion | flops 4194304 | bytes 8388672 | tf_op jit(solution)/shard_map/jit(_where)/select_n | solution.py:192
  28.3 8.0 %all-to-all-start.1 = ((bf16[16,2,128,2,256]{4,2,3,1,0:T(8,128)(2,1)}), bf16[16,2,128,2,256]{4,2,3,1,0:T(8,128)(2,1)}, u32[]{:S(2)}, u32[]{:S(2)}) async-start(bf16[16,2,128,2,256]{4,2,3,1,0:T(8,128)(2,1)} %fusion.2), calls=%async_computation.1 | async-start | bytes 8388608 | tf_op jit(solution)/shard_map/all_to_all | solution.py:195
  37.9 3.9 %convert_element_type.113 = bf16[64,16,1024]{2,1,0:T(8,128)(2,1)} convert(f32[64,16,1024]{2,1,0:T(8,128)} %param.30) | non-fusion elementwise | flops 1048576 | bytes 6291456 | tf_op jit(solution)/shard_map/convert_element_type | solution.py:139
  41.8 4.5 %reshape.371 = bf16[64,16,2,512]{3,2,1,0:T(2,128)(2,1)} reshape(bf16[64,16,1024]{2,1,0:T(8,128)(2,1)} %convert_element_type.113) | data formatting | bytes 4194304 | tf_op jit(solution)/shard_map/reshape | solution.py:38
  46.3 3.9 %convert_element_type.114 = bf16[64,16,1024]{2,1,0:T(8,128)(2,1)} convert(f32[64,16,1024]{2,1,0:T(8,128)} %param.31) | non-fusion elementwise | flops 1048576 | bytes 6291456 | tf_op jit(solution)/shard_map/convert_element_type | solution.py:140
  50.2 4.6 %reshape.372 = bf16[64,16,2,512]{3,2,1,0:T(2,128)(2,1)} reshape(bf16[64,16,1024]{2,1,0:T(8,128)(2,1)} %convert_element_type.114) | data formatting | bytes 4194304 | tf_op jit(solution)/shard_map/reshape | solution.py:38
  54.7 10.6 %pad_maximum_fusion = bf16[64,2,16,1024]{3,1,2,0:T(2,128)(2,1)} fusion(bf16[64,2,16,512]{3,1,2,0:T(2,128)(2,1)} %bitcast.105, bf16[64,2,16,512]{3,1,2,0:T(2,128)(2,1)} %bitcast.104), kind=kLoop, calls=%fused_computation.4 | loop fusion | flops 8388608 | bytes 8388608 | tf_op jit(solution)/shard_map/concatenate | solution.py:137
  65.3 5.7 %copy.126 = bf16[64,2,16,1024]{3,2,1,0:T(8,128)(2,1)} copy(bf16[64,2,16,1024]{3,1,2,0:T(2,128)(2,1)} %pad_maximum_fusion) | data formatting | bytes 8388608 | tf_op jit(solution)/shard_map/concatenate | solution.py:137
  78.9 15.0 %all-to-all-done.1 = bf16[16,2,128,2,256]{4,2,3,1,0:T(8,128)(2,1)} async-done(((bf16[16,2,128,2,256]{4,2,3,1,0:T(8,128)(2,1)}), bf16[16,2,128,2,256]{4,2,3,1,0:T(8,128)(2,1)}, u32[]{:S(2)}, u32[]{:S(2)}) %all-to-all-start.1) | async-done | bytes 4194336 | tf_op jit(solution)/shard_map/all_to_all | solution.py:195
  93.9 9.9 %all-to-all-start = ((bf16[128,16,1024]{2,1,0:T(8,128)(2,1)}), bf16[128,16,1024]{2,1,0:T(8,128)(2,1)}, u32[]{:S(2)}, u32[]{:S(2)}) async-start(bf16[128,16,1024]{2,1,0:T(8,128)(2,1)} %bitcast.101), calls=%async_computation | async-start | bytes 8388608 | tf_op jit(solution)/shard_map/all_to_all | solution.py:144
  103.8 4.2 %gather_fusion.1 = bf16[16,128,2,256]{3,1,2,0:T(8,128)(2,1)} fusion(bf16[32,128,2,256]{3,1,2,0:T(8,128)(2,1)} %bitcast.13, s32[1024]{0:T(1024)S(1)} %pad_clamp_fusion.1), kind=kCustom, calls=%fused_computation.1 | custom fusion | bytes 4194368 | tf_op jit(solution)/shard_map/jit(_take)/gather | solution.py:198
  108.0 4.5 %copy.135 = bf16[16,128,2,256]{1,0,3,2:T(8,128)(2,1)} copy(bf16[16,128,2,256]{3,1,2,0:T(8,128)(2,1)} %gather_fusion.1) | data formatting | bytes 4194304 | tf_op jit(solution)/shard_map/jit(_take)/gather | solution.py:198
  112.5 4.2 %gather.28 = bf16[2048,2,2,128]{0,3,2,1:T(8,128)(2,1)} reshape(bf16[16,128,2,256]{1,0,3,2:T(8,128)(2,1)} %copy.135) | data formatting | bytes 4194304 | tf_op jit(solution)/shard_map/jit(_take)/gather | solution.py:198
  116.7 3.9 %copy.136 = bf16[2048,2,2,128]{3,0,2,1:T(8,128)(2,1)} copy(bf16[2048,2,2,128]{0,3,2,1:T(8,128)(2,1)} %gather.28) | data formatting | bytes 4194304 | tf_op jit(solution)/shard_map/jit(_take)/gather | solution.py:198
  120.6 2.8 broadcast_select_fusion
  123.4 2.5 fusion.13
  130.7 24.1 %all-gather.5.cloned.1.call-done = bf16[256,2048]{1,0:T(8,128)(2,1)} async-done(((bf16[256,128]{1,0:T(8,128)(2,1)}), bf16[256,2048]{1,0:T(8,128)(2,1)}) %all-gather.5.cloned.1.call-update) | async-done | bytes 1048592 | tf_op jit(solution)/shard_map/all_gather | solution.py:133
  154.8 2.5 fusion.45.x_ref
  157.4 22.7 %shard_map.218 = f32[16,2048]{1,0:T(8,128)} custom-call(f32[128,2048]{1,0:T(8,128)} %fusion.45.x_ref), custom_call_target="tpu_custom_call" | custom-call | tf_op jit(solution)/shard_map/pallas_call | solution.py:85
  182.5 2.4 broadcast_in_dim.156
  186.2 38.9 %all_to_all.27 = bf16[128,3,2048]{2,1,0:T(4,128)(2,1)} all-to-all(bf16[128,3,2048]{2,1,0:T(4,128)(2,1)S(1)} %bitcast.103), channel_id=1, replica_groups=mesh['req'=16,'tp'=8] {'req','tp'}, dimensions={0} | all-to-all | bytes 3145728 | tf_op jit(solution)/shard_map/all_to_all | solution.py:262
  225.1 5.0 %reshape.382 = bf16[384,2048]{1,0:T(8,128)(2,1)} reshape(bf16[128,3,2048]{2,1,0:T(4,128)(2,1)} %all_to_all.27) | data formatting | bytes 3145728 | tf_op jit(solution)/shard_map/reshape | solution.py:263
  230.1 4.4 %fusion = f32[384,1024]{1,0:T(8,128)S(1)} fusion(bf16[384,2048]{1,0:T(8,128)(2,1)} %reshape.382, bf16[1,2048,1024]{2,1,0:T(8,128)(2,1)} %bitcast.3), kind=kOutput, calls=%fused_computation.5 | convolution fusion | flops 1610612736 | bytes 7340032 | tf_op jit(solution)/shard_map/dot_general | solution.py:264
  236.7 5.2 %reshape.383 = bf16[128,3,2048]{2,1,0:T(4,128)(2,1)} reshape(bf16[384,2048]{1,0:T(8,128)(2,1)} %convolution_convert_fusion) | data formatting | bytes 3145728 | tf_op jit(solution)/shard_map/reshape | solution.py:269
  241.9 6.6 %all-to-all-start.3 = ((bf16[128,3,2048]{2,1,0:T(4,128)(2,1)}), bf16[128,3,2048]{2,1,0:T(4,128)(2,1)}, u32[]{:S(2)}, u32[]{:S(2)}) async-start(bf16[128,3,2048]{2,1,0:T(4,128)(2,1)} %reshape.383), calls=%async_computation.3 | async-start | bytes 4194304 | tf_op jit(solution)/shard_map/all_to_all | solution.py:271
  252.6 24.3 %all-to-all-done.3 = bf16[128,3,2048]{2,1,0:T(4,128)(2,1)} async-done(((bf16[128,3,2048]{2,1,0:T(4,128)(2,1)}), bf16[128,3,2048]{2,1,0:T(4,128)(2,1)}, u32[]{:S(2)}, u32[]{:S(2)}) %all-to-all-start.3) | async-done | bytes 1572896 | tf_op jit(solution)/shard_map/all_to_all | solution.py:271
  277.0 3.7 %convert_add_fusion = f32[64,1,3,2048]{3,2,0,1:T(4,128)} fusion(bf16[64,2,3,2048]{3,2,1,0:T(4,128)(2,1)} %bitcast.21), kind=kLoop, calls=%fused_computation.15 | loop fusion | flops 1179648 | bytes 3145728 | tf_op jit(solution)/shard_map/add | solution.py:273
  280.7 3.8 %add.188 = f32[192,2048]{1,0:T(8,128)} reshape(f32[64,1,3,2048]{3,2,0,1:T(4,128)} %convert_add_fusion) | data formatting | bytes 3145728 | tf_op jit(solution)/shard_map/add | solution.py:273
  284.5 2.9 gather_fusion.2
  288.9 3.8 %copy.167 = bf16[2048,768]{1,0:T(8,128)(2,1)} copy(bf16[2048,768]{1,0:T(8,128)(2,1)} %all-gather.3.cloned.1.call-done) | data formatting | bytes 6291456
  293.7 4.6 %copy.169 = bf16[1,2048,1024]{2,1,0:T(8,128)(2,1)} copy(bf16[1,2048,1024]{2,1,0:T(8,128)(2,1)} %bitcast.3) | data formatting | bytes 8388608
  (126 shorter events, 33.5 us)
Async XLA Ops:
  7.2 227.4 %copy-start = (bf16[1,512,2048]{2,1,0:T(8,128)(2,1)S(1)}, bf16[1,512,2048]{2,1,0:T(8,128)(2,1)}, u32[]{:S(2)}) copy-start(bf16[1,512,2048]{2,1,0:T(8,128)(2,1)} %param.32) | copy-start | bytes 6291460
  7.2 7.0 %copy-start.1 = (bf16[8,128,2,256]{3,2,1,0:T(2,128)(2,1)S(1)}, bf16[8,128,2,256]{3,2,1,0:T(2,128)(2,1)}, u32[]{:S(2)}) copy-start(bf16[8,128,2,256]{3,2,1,0:T(2,128)(2,1)} %param.34) | copy-start | bytes 3145732
  7.2 116.2 %all-gather.3.cloned.1.call-start = ((), (), s32[]{:S(2)}) async-start(), calls=%async_computation.4 | async-start | bytes 3342336 | tf_op jit(solution)/shard_map/all_gather | solution.py:132
  28.3 8.2 %copy-start.8 = (f32[256,128]{1,0:T(8,128)S(1)}, f32[256,128]{1,0:T(8,128)}, u32[]{:S(2)}) copy-start(f32[256,128]{1,0:T(8,128)} %param.29) | copy-start | bytes 393220
  28.3 8.9 %copy-start.13 = (s32[32]{0:T(128)S(1)}, s32[32]{0:T(128)}, u32[]{:S(2)}) copy-start(s32[32]{0:T(128)} %param.36) | copy-start | bytes 388
  28.3 9.0 %copy-start.14 = (s32[32]{0:T(128)S(1)}, s32[32]{0:T(128)}, u32[]{:S(2)}) copy-start(s32[32]{0:T(128)} %param.35) | copy-start | bytes 388
  28.3 65.6 %all-to-all-start.1 = ((bf16[16,2,128,2,256]{4,2,3,1,0:T(8,128)(2,1)}), bf16[16,2,128,2,256]{4,2,3,1,0:T(8,128)(2,1)}, u32[]{:S(2)}, u32[]{:S(2)}) async-start(bf16[16,2,128,2,256]{4,2,3,1,0:T(8,128)(2,1)} %fusion.2), calls=%async_computation.1 | async-start | bytes 8388608 | tf_op jit(solution)/shard_map/all_to_all | solution.py:195
  36.3 118.5 %all-gather.5.cloned.1.call-start = ((), (), s32[]{:S(2)}) async-start(), calls=%async_computation.5 | async-start | bytes 1114112 | tf_op jit(solution)/shard_map/all_gather | solution.py:133
  65.3 5.7 %copy-start.2 = (bf16[128,2048]{1,0:T(8,128)(2,1)S(1)}, bf16[128,2048]{1,0:T(8,128)(2,1)}, u32[]{:S(2)}) copy-start(bf16[128,2048]{1,0:T(8,128)(2,1)} %param.21) | copy-start | bytes 1572868
  65.3 6.8 %copy-start.7 = (s32[16,8]{0,1:T(8,128)S(1)}, s32[16,8]{0,1:T(8,128)}, u32[]{:S(2)}) copy-start(s32[16,8]{0,1:T(8,128)} %param.39) | copy-start | bytes 1540
  93.9 63.5 %all-to-all-start = ((bf16[128,16,1024]{2,1,0:T(8,128)(2,1)}), bf16[128,16,1024]{2,1,0:T(8,128)(2,1)}, u32[]{:S(2)}, u32[]{:S(2)}) async-start(bf16[128,16,1024]{2,1,0:T(8,128)(2,1)} %bitcast.101), calls=%async_computation | async-start | bytes 8388608 | tf_op jit(solution)/shard_map/all_to_all | solution.py:144
  120.6 2.8 copy-start.10
  123.4 4.3 %copy-start.11 = (f32[128]{0:T(128)S(1)}, f32[128]{0:T(128)}, u32[]{:S(2)}) copy-start(f32[128]{0:T(128)} %param.24) | copy-start | bytes 1540
  123.4 4.3 %copy-start.12 = (f32[128]{0:T(128)S(1)}, f32[128]{0:T(128)}, u32[]{:S(2)}) copy-start(f32[128]{0:T(128)} %param.23) | copy-start | bytes 1540
  125.9 0.8 copy-start.5
  127.6 1.6 copy-start.4
  130.5 50.7 %copy-start.9 = (f32[2048]{0:T(1024)S(1)}, f32[2048]{0:T(1024)}, u32[]{:S(2)}) copy-start(f32[2048]{0:T(1024)} %param.25) | copy-start | bytes 24580
  241.9 7.1 %copy-start.6 = (bf16[2048,64]{0,1:T(8,128)(2,1)S(1)}, bf16[2048,64]{0,1:T(8,128)(2,1)}, u32[]{:S(2)}) copy-start(bf16[2048,64]{0,1:T(8,128)(2,1)} %param.33) | copy-start | bytes 786436
  241.9 35.1 %all-to-all-start.3 = ((bf16[128,3,2048]{2,1,0:T(4,128)(2,1)}), bf16[128,3,2048]{2,1,0:T(4,128)(2,1)}, u32[]{:S(2)}, u32[]{:S(2)}) async-start(bf16[128,3,2048]{2,1,0:T(4,128)(2,1)} %reshape.383), calls=%async_computation.3 | async-start | bytes 4194304 | tf_op jit(solution)/shard_map/all_to_all | solution.py:271
  288.9 3.8 %copy-start.3 = (bf16[256,2048]{1,0:T(8,128)(2,1)S(1)}, bf16[256,2048]{1,0:T(8,128)(2,1)}, u32[]{:S(2)}) copy-start(bf16[256,2048]{1,0:T(8,128)(2,1)} %all-gather.5.cloned.1.call-done) | copy-start | bytes 3145732
Sparse Core Ops, SparseCore 0:
  11.0 65.4 all-gather.2
  78.6 76.1 all-gather.4

commit v3 on v2

--- a/solution.py
+++ b/solution.py
@@ -93,6 +93,64 @@
             pltpu.SemaphoreType.DMA((parts,)),
         ],
         compiler_params=pltpu.CompilerParams(collective_id=0, has_side_effects=True),
+    )(x)
+
+
+def exchange_kernel(count, width, x_ref, out_ref, held, send_sem, recv_sem):
+    me = lax.axis_index("req") * width + lax.axis_index("tp")
+    barrier = pltpu.get_barrier_semaphore()
+
+    def greet(step, carry):
+        peer = lax.rem(me + step, count)
+        pl.semaphore_signal(
+            barrier, inc=1, device_id=(peer // width, lax.rem(peer, width)), device_id_type=MESH
+        )
+        return carry
+
+    lax.fori_loop(1, count, greet, 0)
+    pl.semaphore_wait(barrier, count - 1)
+
+    def send(step, carry):
+        peer = lax.rem(me + step, count)
+        pltpu.make_async_remote_copy(
+            src_ref=x_ref.at[peer],
+            dst_ref=held.at[me],
+            send_sem=send_sem,
+            recv_sem=recv_sem,
+            device_id=(peer // width, lax.rem(peer, width)),
+            device_id_type=MESH,
+        ).start()
+        return carry
+
+    lax.fori_loop(1, count, send, 0)
+    held[me] = x_ref[me]
+    everything = pltpu.make_async_remote_copy(
+        src_ref=x_ref.at[pl.ds(0, count - 1)],
+        dst_ref=held.at[pl.ds(0, count - 1)],
+        send_sem=send_sem,
+        recv_sem=recv_sem,
+        device_id=(0, 0),
+        device_id_type=MESH,
+    )
+    everything.wait_recv()
+    everything.wait_send()
+    out_ref[...] = held[...]
+
+
+def exchange(x, collective):
+    count = x.shape[0]
+    width = lax.axis_size("tp")
+    return pl.pallas_call(
+        functools.partial(exchange_kernel, count, width),
+        out_shape=jax.ShapeDtypeStruct(x.shape, x.dtype),
+        in_specs=[pl.BlockSpec(memory_space=pltpu.VMEM)],
+        out_specs=pl.BlockSpec(memory_space=pltpu.VMEM),
+        scratch_shapes=[
+            pltpu.VMEM(x.shape, x.dtype),
+            pltpu.SemaphoreType.DMA(()),
+            pltpu.SemaphoreType.DMA(()),
+        ],
+        compiler_params=pltpu.CompilerParams(collective_id=collective, has_side_effects=True),
     )(x)
 
 
@@ -259,7 +317,7 @@
         outgoing_rows.reshape(expert_count, 1, slot_depth, model_width),
         (expert_count, 2, slot_depth, model_width),
     ).reshape(2 * expert_count, slot_depth, model_width)
-    arrived_rows = lax.all_to_all(send_rows, ("req", "tp"), split_axis=0, concat_axis=0, tiled=True)
+    arrived_rows = exchange(send_rows, 1)
     flat_rows = arrived_rows.reshape(-1, model_width)
     both = jnp.dot(flat_rows, server_gate_up[0], preferred_element_type=jnp.float32)
     act = (jax.nn.silu(both[:, :half_units]) * both[:, half_units:]).astype(jnp.bfloat16)
@@ -268,7 +326,7 @@
         .astype(jnp.bfloat16)
         .reshape(arrived_rows.shape)
     )
-    returned = lax.all_to_all(expert_rows, ("req", "tp"), split_axis=0, concat_axis=0, tiled=True)
+    returned = exchange(expert_rows, 2)
     returned = returned.reshape(expert_count, 2, slot_depth, model_width)
     joined_out = (returned[:, 0].astype(jnp.float32) + returned[:, 1].astype(jnp.float32)).reshape(
         expert_count * slot_depth, model_width

time: 307 us -> 326 us (1.062)
  Pallas kernels: 22.7 us -> 103 us
  blocking collectives: 38.9 us -> 0 us
  waiting for transfers between devices: 63.5 us -> 46.1 us
  starting transfers between devices: 24.7 us -> 19.5 us
    pallas_call x0 -> x2, Pallas kernels: none -> 76.7 us  [exchange(): pl.pallas_call(functools.partial(exchange_kernel, count, width), out_shap...]
    all_to_all x1 -> x0, blocking collectives: 38.9 us -> none  [body(): lax.all_to_all(send_rows, ('req', 'tp'), split_axis=0, concat_axis=0, til...]
    all_to_all x1 -> x0, waiting for transfers between devices: 24.3 us -> none  [body(): lax.all_to_all(expert_rows, ('req', 'tp'), split_axis=0, concat_axis=0, t...]
    all_gather x1, waiting for transfers between devices: 24.1 us -> 0.12 us  [body(): lax.all_gather(out_weight.astype(jnp.bfloat16), 'req', axis=1, tiled=True)]
    all_gather x1, waiting for transfers between devices: 0.01 us -> 14.5 us  [body(): lax.all_gather(joined_local, 'req', axis=0, tiled=True)]
    all_to_all x1, waiting for transfers between devices: 0.01 us -> 9.79 us  [body(): lax.all_to_all(packed, ('req', 'tp'), split_axis=0, concat_axis=1, tiled=...]
    all_to_all x1, waiting for transfers between devices: 15 us -> 21.6 us  [body(): lax.all_to_all(outgoing_pages, 'req', split_axis=0, concat_axis=0, tiled=...]
    all_to_all x1 -> x0, starting transfers between devices: 6.59 us -> none  [body(): lax.all_to_all(expert_rows, ('req', 'tp'), split_axis=0, concat_axis=0, t...]
  transfers between devices with their start and end apart: 5 -> 4, of which waited for: 3 -> 4; matrix products, arithmetic and copies ran while one was open for 30% -> 28% of each run, Pallas kernels for 0% -> 0%
where the time goes in v3:
time: 326 us; the launch traced here: 323 us
  Pallas kernels  103 us (32%)
  local copies, waits for them, and re-layouts  79.4 us (24%)
  other arithmetic  47.4 us (15%)
  waiting for transfers between devices  46.1 us (14%)
  starting transfers between devices  19.5 us (6%)
  between operations  14.5 us (4%)
  matrix products  13.7 us (4%)
    pallas_call x2, Pallas kernels, exchange(): pl.pallas_call(functools.partial(exchange_kernel, count, width), out_shap...  76.7 us
    pallas_call x1, Pallas kernels, scatter_sum(): pl.pallas_call(functools.partial(scatter_sum_kernel, parts), out_shape=ja...  26.1 us
    all_to_all x1, waiting for transfers between devices, body(): lax.all_to_all(outgoing_pages, 'req', split_axis=0, concat_axis=0, tiled=...  21.6 us
    gather x4, local copies, waits for them, and re-layouts, body(): jnp.take(arrived_pages.reshape((req_count * capacity,) + page_shape), own...  16.8 us
    all_gather x1, waiting for transfers between devices, body(): lax.all_gather(joined_local, 'req', axis=0, tiled=True)  14.5 us
    unnamed x33, local copies, waits for them, and re-layouts  11.5 us
    all_to_all x1, starting transfers between devices, body(): lax.all_to_all(packed, ('req', 'tp'), split_axis=0, concat_axis=1, tiled=...  11.4 us
    concatenate x1, other arithmetic, body(): jnp.concatenate([split_halves(gate_weight.astype(jnp.bfloat16)), split_ha...  10.6 us
  transfers between devices with their start and end apart: 4, of which 4 were waited for; matrix products, arithmetic and copies ran while one was open for 28% of the time, Pallas kernels for 0%

profile of v3, /device:TPU:1, one launch (start us, length us, event | category | flops | bytes accessed | tf_op | source)
XLA Modules:
  0.0 323.4 jit_solution(3353732690958939692)
XLA Ops:
  15.8 10.1 %gather_fusion = bf16[32,128,2,256]{3,2,1,0:T(2,128)(2,1)} fusion(bf16[8,128,2,256]{3,2,1,0:T(2,128)(2,1)S(1)} %copy-done.1, s32[1024]{0:T(1024)S(1)} %pad_clamp_fusion.2), kind=kCustom, calls=%fused_computation | custom fusion | bytes 8388736 | tf_op jit(solution)/shard_map/jit(_take)/gather | solution.py:247
  25.8 4.1 %fusion.2 = bf16[16,2,128,2,256]{4,2,3,1,0:T(8,128)(2,1)} fusion(bf16[16,2,128,2,256]{4,3,2,1,0:T(2,128)(2,1)} %bitcast.102, pred[16,2]{1,0:T(8,128)(4,1)S(1)} %copy.130, pred[16,2]{1,0:T(8,128)(4,1)S(1)} %copy.129), kind=kLoop, calls=%fused_computation.8 | loop fusion | flops 4194304 | bytes 8388672 | tf_op jit(solution)/shard_map/jit(_where)/select_n | solution.py:250
  30.0 8.0 %all-to-all-start.1 = ((bf16[16,2,128,2,256]{4,2,3,1,0:T(8,128)(2,1)}), bf16[16,2,128,2,256]{4,2,3,1,0:T(8,128)(2,1)}, u32[]{:S(2)}, u32[]{:S(2)}) async-start(bf16[16,2,128,2,256]{4,2,3,1,0:T(8,128)(2,1)} %fusion.2), calls=%async_computation.1 | async-start | bytes 8388608 | tf_op jit(solution)/shard_map/all_to_all | solution.py:253
  38.6 3.9 %convert_element_type.113 = bf16[64,16,1024]{2,1,0:T(8,128)(2,1)} convert(f32[64,16,1024]{2,1,0:T(8,128)} %param.30) | non-fusion elementwise | flops 1048576 | bytes 6291456 | tf_op jit(solution)/shard_map/convert_element_type | solution.py:197
  42.5 4.5 %reshape.371 = bf16[64,16,2,512]{3,2,1,0:T(2,128)(2,1)} reshape(bf16[64,16,1024]{2,1,0:T(8,128)(2,1)} %convert_element_type.113) | data formatting | bytes 4194304 | tf_op jit(solution)/shard_map/reshape | solution.py:38
  47.0 3.8 %convert_element_type.114 = bf16[64,16,1024]{2,1,0:T(8,128)(2,1)} convert(f32[64,16,1024]{2,1,0:T(8,128)} %param.31) | non-fusion elementwise | flops 1048576 | bytes 6291456 | tf_op jit(solution)/shard_map/convert_element_type | solution.py:198
  50.8 4.5 %reshape.372 = bf16[64,16,2,512]{3,2,1,0:T(2,128)(2,1)} reshape(bf16[64,16,1024]{2,1,0:T(8,128)(2,1)} %convert_element_type.114) | data formatting | bytes 4194304 | tf_op jit(solution)/shard_map/reshape | solution.py:38
  55.4 10.6 %pad_maximum_fusion = bf16[64,2,16,1024]{3,1,2,0:T(2,128)(2,1)} fusion(bf16[64,2,16,512]{3,1,2,0:T(2,128)(2,1)} %bitcast.106, bf16[64,2,16,512]{3,1,2,0:T(2,128)(2,1)} %bitcast.105), kind=kLoop, calls=%fused_computation.4 | loop fusion | flops 8388608 | bytes 8388608 | tf_op jit(solution)/shard_map/concatenate | solution.py:195
  65.9 5.7 %copy.124 = bf16[64,2,16,1024]{3,2,1,0:T(8,128)(2,1)} copy(bf16[64,2,16,1024]{3,1,2,0:T(2,128)(2,1)} %pad_maximum_fusion) | data formatting | bytes 8388608 | tf_op jit(solution)/shard_map/concatenate | solution.py:195
  80.2 21.6 %all-to-all-done.1 = bf16[16,2,128,2,256]{4,2,3,1,0:T(8,128)(2,1)} async-done(((bf16[16,2,128,2,256]{4,2,3,1,0:T(8,128)(2,1)}), bf16[16,2,128,2,256]{4,2,3,1,0:T(8,128)(2,1)}, u32[]{:S(2)}, u32[]{:S(2)}) %all-to-all-start.1) | async-done | bytes 4194336 | tf_op jit(solution)/shard_map/all_to_all | solution.py:253
  101.8 11.4 %all-to-all-start = ((bf16[128,16,1024]{2,1,0:T(8,128)(2,1)}), bf16[128,16,1024]{2,1,0:T(8,128)(2,1)}, u32[]{:S(2)}, u32[]{:S(2)}) async-start(bf16[128,16,1024]{2,1,0:T(8,128)(2,1)} %bitcast.101), calls=%async_computation | async-start | bytes 8388608 | tf_op jit(solution)/shard_map/all_to_all | solution.py:202
  113.2 4.2 %gather_fusion.1 = bf16[16,128,2,256]{3,1,2,0:T(8,128)(2,1)} fusion(bf16[32,128,2,256]{3,1,2,0:T(8,128)(2,1)} %bitcast.13, s32[1024]{0:T(1024)S(1)} %pad_clamp_fusion.1), kind=kCustom, calls=%fused_computation.1 | custom fusion | bytes 4194368 | tf_op jit(solution)/shard_map/jit(_take)/gather | solution.py:256
  117.4 4.5 %copy.133 = bf16[16,128,2,256]{1,0,3,2:T(8,128)(2,1)} copy(bf16[16,128,2,256]{3,1,2,0:T(8,128)(2,1)} %gather_fusion.1) | data formatting | bytes 4194304 | tf_op jit(solution)/shard_map/jit(_take)/gather | solution.py:256
  121.9 4.2 %gather.28 = bf16[2048,2,2,128]{0,3,2,1:T(8,128)(2,1)} reshape(bf16[16,128,2,256]{1,0,3,2:T(8,128)(2,1)} %copy.133) | data formatting | bytes 4194304 | tf_op jit(solution)/shard_map/jit(_take)/gather | solution.py:256
  126.0 3.9 %copy.134 = bf16[2048,2,2,128]{3,0,2,1:T(8,128)(2,1)} copy(bf16[2048,2,2,128]{0,3,2,1:T(8,128)(2,1)} %gather.28) | data formatting | bytes 4194304 | tf_op jit(solution)/shard_map/jit(_take)/gather | solution.py:256
  130.0 2.8 broadcast_select_fusion
  132.7 14.5 %all-gather.3.cloned.1.call-done = bf16[2048,768]{1,0:T(8,128)(2,1)} async-done(((bf16[128,768]{1,0:T(8,128)(2,1)}), bf16[2048,768]{1,0:T(8,128)(2,1)}) %all-gather.3.cloned.1.call-update) | async-done | bytes 3145744 | tf_op jit(solution)/shard_map/all_gather | solution.py:190
  147.3 2.5 fusion.13
  155.6 9.8 %all-to-all-done = bf16[128,16,1024]{2,1,0:T(8,128)(2,1)} async-done(((bf16[128,16,1024]{2,1,0:T(8,128)(2,1)}), bf16[128,16,1024]{2,1,0:T(8,128)(2,1)}, u32[]{:S(2)}, u32[]{:S(2)}) %all-to-all-start) | async-done | bytes 4194336 | tf_op jit(solution)/shard_map/all_to_all | solution.py:202
  165.3 26.1 %shard_map.218 = f32[16,2048]{1,0:T(8,128)} custom-call(f32[128,2048]{1,0:T(8,128)} %fusion.45.x_ref), custom_call_target="tpu_custom_call" | custom-call | tf_op jit(solution)/shard_map/pallas_call | solution.py:85
  195.7 2.4 broadcast_in_dim.156
  198.1 2.6 broadcast_in_dim.157
  200.7 39.2 %shard_map.219 = bf16[128,3,2048]{2,1,0:T(4,128)(2,1)} custom-call(bf16[128,3,2048]{2,1,0:T(4,128)(2,1)} %bitcast.103), custom_call_target="tpu_custom_call" | custom-call | tf_op jit(solution)/shard_map/pallas_call | solution.py:143
  239.9 5.0 %reshape.382 = bf16[384,2048]{1,0:T(8,128)(2,1)} reshape(bf16[128,3,2048]{2,1,0:T(4,128)(2,1)} %shard_map.219) | data formatting | bytes 3145728 | tf_op jit(solution)/shard_map/reshape | solution.py:321
  244.9 4.4 %fusion = f32[384,1024]{1,0:T(8,128)S(1)} fusion(bf16[384,2048]{1,0:T(8,128)(2,1)} %reshape.382, bf16[1,2048,1024]{2,1,0:T(8,128)(2,1)} %bitcast.3), kind=kOutput, calls=%fused_computation.5 | convolution fusion | flops 1610612736 | bytes 7340032 | tf_op jit(solution)/shard_map/dot_general | solution.py:322
  251.6 5.2 %reshape.383.x_ref = bf16[128,3,2048]{2,1,0:T(4,128)(2,1)} reshape(bf16[384,2048]{1,0:T(8,128)(2,1)} %convolution_convert_fusion) | data formatting | bytes 3145728 | tf_op jit(solution)/shard_map/reshape | solution.py:327
  256.7 37.6 %shard_map.220 = bf16[128,3,2048]{2,1,0:T(4,128)(2,1)} custom-call(bf16[128,3,2048]{2,1,0:T(4,128)(2,1)} %reshape.383.x_ref), custom_call_target="tpu_custom_call" | custom-call | tf_op jit(solution)/shard_map/pallas_call | solution.py:143
  294.3 3.7 %convert_add_fusion = f32[64,1,3,2048]{3,2,0,1:T(4,128)} fusion(bf16[64,2,3,2048]{3,2,1,0:T(4,128)(2,1)} %bitcast.104), kind=kLoop, calls=%fused_computation.15 | loop fusion | flops 1179648 | bytes 3145728 | tf_op jit(solution)/shard_map/add | solution.py:331
  298.0 3.8 %add.188 = f32[192,2048]{1,0:T(8,128)} reshape(f32[64,1,3,2048]{3,2,0,1:T(4,128)} %convert_add_fusion) | data formatting | bytes 3145728 | tf_op jit(solution)/shard_map/add | solution.py:331
  301.8 2.9 gather_fusion.2
  307.1 3.8 %copy.165 = bf16[2048,768]{1,0:T(8,128)(2,1)} copy(bf16[2048,768]{1,0:T(8,128)(2,1)} %all-gather.3.cloned.1.call-done) | data formatting | bytes 6291456
  311.9 4.6 %copy.167 = bf16[1,2048,1024]{2,1,0:T(8,128)(2,1)} copy(bf16[1,2048,1024]{2,1,0:T(8,128)(2,1)} %bitcast.3) | data formatting | bytes 8388608
  (123 shorter events, 33.0 us)
Async XLA Ops:
  7.2 242.2 %copy-start = (bf16[1,512,2048]{2,1,0:T(8,128)(2,1)S(1)}, bf16[1,512,2048]{2,1,0:T(8,128)(2,1)}, u32[]{:S(2)}) copy-start(bf16[1,512,2048]{2,1,0:T(8,128)(2,1)} %param.32) | copy-start | bytes 6291460
  7.2 8.6 %copy-start.1 = (bf16[8,128,2,256]{3,2,1,0:T(2,128)(2,1)S(1)}, bf16[8,128,2,256]{3,2,1,0:T(2,128)(2,1)}, u32[]{:S(2)}) copy-start(bf16[8,128,2,256]{3,2,1,0:T(2,128)(2,1)} %param.34) | copy-start | bytes 3145732
  7.2 73.0 %all-gather.5.cloned.1.call-start = ((), (), s32[]{:S(2)}) async-start(), calls=%async_computation.3 | async-start | bytes 1114112 | tf_op jit(solution)/shard_map/all_gather | solution.py:191
  9.0 138.3 %all-gather.3.cloned.1.call-start = ((), (), s32[]{:S(2)}) async-start(), calls=%async_computation.2 | async-start | bytes 3342336 | tf_op jit(solution)/shard_map/all_gather | solution.py:190
  29.9 8.0 %copy-start.12 = (s32[32]{0:T(128)S(1)}, s32[32]{0:T(128)}, u32[]{:S(2)}) copy-start(s32[32]{0:T(128)} %param.36) | copy-start | bytes 388
  30.0 8.1 %copy-start.13 = (s32[32]{0:T(128)S(1)}, s32[32]{0:T(128)}, u32[]{:S(2)}) copy-start(s32[32]{0:T(128)} %param.35) | copy-start | bytes 388
  30.0 71.8 %all-to-all-start.1 = ((bf16[16,2,128,2,256]{4,2,3,1,0:T(8,128)(2,1)}), bf16[16,2,128,2,256]{4,2,3,1,0:T(8,128)(2,1)}, u32[]{:S(2)}, u32[]{:S(2)}) async-start(bf16[16,2,128,2,256]{4,2,3,1,0:T(8,128)(2,1)} %fusion.2), calls=%async_computation.1 | async-start | bytes 8388608 | tf_op jit(solution)/shard_map/all_to_all | solution.py:253
  65.9 5.7 %copy-start.2 = (bf16[128,2048]{1,0:T(8,128)(2,1)S(1)}, bf16[128,2048]{1,0:T(8,128)(2,1)}, u32[]{:S(2)}) copy-start(bf16[128,2048]{1,0:T(8,128)(2,1)} %param.21) | copy-start | bytes 1572868
  65.9 6.8 %copy-start.7 = (s32[16,8]{0,1:T(8,128)S(1)}, s32[16,8]{0,1:T(8,128)}, u32[]{:S(2)}) copy-start(s32[16,8]{0,1:T(8,128)} %param.39) | copy-start | bytes 1540
  101.8 63.6 %all-to-all-start = ((bf16[128,16,1024]{2,1,0:T(8,128)(2,1)}), bf16[128,16,1024]{2,1,0:T(8,128)(2,1)}, u32[]{:S(2)}, u32[]{:S(2)}) async-start(bf16[128,16,1024]{2,1,0:T(8,128)(2,1)} %bitcast.101), calls=%async_computation | async-start | bytes 8388608 | tf_op jit(solution)/shard_map/all_to_all | solution.py:202
  130.0 17.3 %copy-start.9 = (f32[2048]{0:T(1024)S(1)}, f32[2048]{0:T(1024)}, u32[]{:S(2)}) copy-start(f32[2048]{0:T(1024)} %param.22) | copy-start | bytes 24580
  132.7 18.0 %copy-start.10 = (f32[128]{0:T(128)S(1)}, f32[128]{0:T(128)}, u32[]{:S(2)}) copy-start(f32[128]{0:T(128)} %param.24) | copy-start | bytes 1540
  132.7 18.0 %copy-start.11 = (f32[128]{0:T(128)S(1)}, f32[128]{0:T(128)}, u32[]{:S(2)}) copy-start(f32[128]{0:T(128)} %param.23) | copy-start | bytes 1540
  150.7 1.6 copy-start.5
  153.0 1.2 copy-start.3
  153.7 38.9 %copy-start.6 = (bf16[2048,64]{0,1:T(8,128)(2,1)S(1)}, bf16[2048,64]{0,1:T(8,128)(2,1)}, u32[]{:S(2)}) copy-start(bf16[2048,64]{0,1:T(8,128)(2,1)} %param.33) | copy-start | bytes 786436
  153.7 38.9 %copy-start.8 = (f32[2048]{0:T(1024)S(1)}, f32[2048]{0:T(1024)}, u32[]{:S(2)}) copy-start(f32[2048]{0:T(1024)} %param.25) | copy-start | bytes 24580
  307.1 3.8 %copy-start.4 = (bf16[256,2048]{1,0:T(8,128)(2,1)S(1)}, bf16[256,2048]{1,0:T(8,128)(2,1)}, u32[]{:S(2)}) copy-start(bf16[256,2048]{1,0:T(8,128)(2,1)} %all-gather.5.cloned.1.call-done) | copy-start | bytes 3145732
Sparse Core Ops, SparseCore 0:
  10.2 69.9 all-gather.4
  82.4 64.7 all-gather.2

commit v4 on v2

--- a/solution.py
+++ b/solution.py
@@ -128,10 +128,8 @@
         ],
         axis=1,
     )
-    server_qkv, server_out = (
-        lax.all_gather(joined_local, "req", axis=0, tiled=True),
-        lax.all_gather(out_weight.astype(jnp.bfloat16), "req", axis=1, tiled=True),
-    )
+    server_qkv = lax.all_gather(joined_local, "req", axis=0, tiled=True)
+    out_block = out_weight.astype(jnp.bfloat16)
     expert_count, rows_here, hidden_units = gate_weight.shape
     half_units = hidden_units // 2
     packed = jnp.concatenate(
@@ -192,7 +190,19 @@
     outgoing_pages = jnp.where(
         send_live[:, :, None, None, None], outgoing_pages, jnp.zeros_like(outgoing_pages)
     )
-    arrived_pages = lax.all_to_all(outgoing_pages, "req", split_axis=0, concat_axis=0, tiled=True)
+    out_pair = out_block.reshape(page_shape[0], page_shape[2])
+    out_slot = jnp.stack([out_pair, jnp.zeros_like(out_pair)], axis=1)
+    outgoing_all = jnp.concatenate(
+        [outgoing_pages, jnp.broadcast_to(out_slot[None, None], (req_count, 1) + page_shape)], axis=1
+    )
+    arrived_all = lax.all_to_all(outgoing_all, "req", split_axis=0, concat_axis=0, tiled=True)
+    arrived_pages = arrived_all[:, :capacity]
+    server_out = (
+        arrived_all[:, capacity, :, 0, :]
+        .reshape((req_count,) + out_block.shape)
+        .transpose(1, 0, 2)
+        .reshape(out_block.shape[0], req_count * out_block.shape[1])
+    )
     own_owner = jnp.take(page_owner, req_index, axis=0)
     own_rank = jnp.take(page_rank, req_index, axis=0)
     context = jnp.take(

time: 307 us -> 339 us (1.10)
  local copies, waits for them, and re-layouts: 79.4 us -> 99 us
  waiting for transfers between devices: 63.5 us -> 80.4 us
  blocking collectives: 38.9 us -> 33 us
    all_to_all x1, waiting for transfers between devices: 15 us -> 46.3 us  [body(): lax.all_to_all(outgoing_all, 'req', split_axis=0, concat_axis=0, tiled=True)]
    all_gather x2 -> x1, waiting for transfers between devices: 24.1 us -> 0.02 us  [body(): server_qkv = lax.all_gather(joined_local, 'req', axis=0, tiled=True)]
    all_to_all x1, waiting for transfers between devices: 0.01 us -> 13.6 us  [body(): lax.all_to_all(packed, ('req', 'tp'), split_axis=0, concat_axis=1, tiled=...]
    gather x1 -> x2, local copies, waits for them, and re-layouts: 10 us -> 16.2 us  [body(): jnp.take(page_store, send_slot.reshape(-1), axis=0)]
    slice x0 -> x2, local copies, waits for them, and re-layouts: none -> 5.99 us  [the longest x1 4.7 us: body(): arrived_pages = arrived_all[:, :capacity]]
    all_to_all x1, blocking collectives: 38.9 us -> 33 us  [body(): lax.all_to_all(send_rows, ('req', 'tp'), split_axis=0, concat_axis=0, til...]
    all_to_all x1, waiting for transfers between devices: 24.3 us -> 20.5 us  [body(): lax.all_to_all(expert_rows, ('req', 'tp'), split_axis=0, concat_axis=0, t...]
    unnamed x35 -> x49, local copies, waits for them, and re-layouts: 11.9 us -> 11.9 us
  transfers between devices with their start and end apart: 5 -> 4, of which waited for: 3 -> 3; matrix products, arithmetic and copies ran while one was open for 30% -> 26% of each run, Pallas kernels for 0% -> 0%
where the time goes in v4:
time: 339 us; the launch traced here: 337 us
  local copies, waits for them, and re-layouts  99 us (29%)
  waiting for transfers between devices  80.4 us (24%)
  other arithmetic  46.4 us (14%)
  blocking collectives  33 us (10%)
  starting transfers between devices  25.3 us (7%)
  Pallas kernels  23.4 us (7%)
  matrix products  15.2 us (4%)
  between operations  14.6 us (4%)
    all_to_all x1, waiting for transfers between devices, body(): lax.all_to_all(outgoing_all, 'req', split_axis=0, concat_axis=0, tiled=True)  46.3 us
    all_to_all x1, blocking collectives, body(): lax.all_to_all(send_rows, ('req', 'tp'), split_axis=0, concat_axis=0, til...  33 us
    pallas_call x1, Pallas kernels, scatter_sum(): pl.pallas_call(functools.partial(scatter_sum_kernel, parts), out_shape=ja...  23.4 us
    all_to_all x1, waiting for transfers between devices, body(): lax.all_to_all(expert_rows, ('req', 'tp'), split_axis=0, concat_axis=0, t...  20.5 us
    gather x4, local copies, waits for them, and re-layouts, body(): jnp.take(arrived_pages.reshape((req_count * capacity,) + page_shape), own...  16.8 us
    gather x2, local copies, waits for them, and re-layouts, body(): jnp.take(page_store, send_slot.reshape(-1), axis=0)  16.2 us
    all_to_all x1, waiting for transfers between devices, body(): lax.all_to_all(packed, ('req', 'tp'), split_axis=0, concat_axis=1, tiled=...  13.6 us
    unnamed x49, local copies, waits for them, and re-layouts  11.9 us
  transfers between devices with their start and end apart: 4, of which 3 were waited for; matrix products, arithmetic and copies ran while one was open for 26% of the time, Pallas kernels for 0%

profile of v4, /device:TPU:1, one launch (start us, length us, event | category | flops | bytes accessed | tf_op | source)
XLA Modules:
  0.0 337.2 jit_solution(4713138440156965683)
XLA Ops:
  10.3 11.2 %gather_fusion = bf16[32,128,2,256]{3,2,1,0:T(2,128)(2,1)} fusion(bf16[8,128,2,256]{3,2,1,0:T(2,128)(2,1)} %param.34, s32[1024]{0:T(1024)S(1)} %pad_clamp_fusion.2), kind=kCustom, calls=%fused_computation | custom fusion | bytes 8388736 | tf_op jit(solution)/shard_map/jit(_take)/gather | solution.py:187
  21.6 5.0 %copy.138 = bf16[32,128,2,256]{3,1,2,0:T(8,128)(2,1)} copy(bf16[32,128,2,256]{3,2,1,0:T(2,128)(2,1)} %gather_fusion) | data formatting | bytes 8388608 | tf_op jit(solution)/shard_map/jit(_take)/gather | solution.py:187
  26.9 2.7 select_select_fusion
  29.8 3.2 pad_maximum_fusion
  33.0 8.0 %all-to-all-start = ((bf16[16,3,128,2,256]{4,2,3,1,0:T(8,128)(2,1)}), bf16[16,3,128,2,256]{4,2,3,1,0:T(8,128)(2,1)}, u32[]{:S(2)}, u32[]{:S(2)}) async-start(bf16[16,3,128,2,256]{4,2,3,1,0:T(8,128)(2,1)} %pad_maximum_fusion), calls=%async_computation | async-start | bytes 12582912 | tf_op jit(solution)/shard_map/all_to_all | solution.py:198
  42.8 3.8 %convert_element_type.114 = bf16[64,16,1024]{2,1,0:T(8,128)(2,1)} convert(f32[64,16,1024]{2,1,0:T(8,128)} %param.30) | non-fusion elementwise | flops 1048576 | bytes 6291456 | tf_op jit(solution)/shard_map/convert_element_type | solution.py:137
  46.6 4.5 %reshape.379 = bf16[64,16,2,512]{3,2,1,0:T(2,128)(2,1)} reshape(bf16[64,16,1024]{2,1,0:T(8,128)(2,1)} %convert_element_type.114) | data formatting | bytes 4194304 | tf_op jit(solution)/shard_map/reshape | solution.py:38
  51.1 3.8 %convert_element_type.115 = bf16[64,16,1024]{2,1,0:T(8,128)(2,1)} convert(f32[64,16,1024]{2,1,0:T(8,128)} %param.31) | non-fusion elementwise | flops 1048576 | bytes 6291456 | tf_op jit(solution)/shard_map/convert_element_type | solution.py:138
  55.0 4.5 %reshape.380 = bf16[64,16,2,512]{3,2,1,0:T(2,128)(2,1)} reshape(bf16[64,16,1024]{2,1,0:T(8,128)(2,1)} %convert_element_type.115) | data formatting | bytes 4194304 | tf_op jit(solution)/shard_map/reshape | solution.py:38
  59.5 10.6 %pad_maximum_fusion.1 = bf16[64,2,16,1024]{3,1,2,0:T(2,128)(2,1)} fusion(bf16[64,2,16,512]{3,1,2,0:T(2,128)(2,1)} %bitcast.114, bf16[64,2,16,512]{3,1,2,0:T(2,128)(2,1)} %bitcast.113), kind=kLoop, calls=%fused_computation.5 | loop fusion | flops 8388608 | bytes 8388608 | tf_op jit(solution)/shard_map/concatenate | solution.py:135
  70.1 5.7 %copy.140 = bf16[64,2,16,1024]{3,2,1,0:T(8,128)(2,1)} copy(bf16[64,2,16,1024]{3,1,2,0:T(2,128)(2,1)} %pad_maximum_fusion.1) | data formatting | bytes 8388608 | tf_op jit(solution)/shard_map/concatenate | solution.py:135
  85.5 46.3 %all-to-all-done = bf16[16,3,128,2,256]{4,2,3,1,0:T(8,128)(2,1)} async-done(((bf16[16,3,128,2,256]{4,2,3,1,0:T(8,128)(2,1)}), bf16[16,3,128,2,256]{4,2,3,1,0:T(8,128)(2,1)}, u32[]{:S(2)}, u32[]{:S(2)}) %all-to-all-start) | async-done | bytes 6291488 | tf_op jit(solution)/shard_map/all_to_all | solution.py:198
  131.7 10.4 %all-to-all-start.1 = ((bf16[128,16,1024]{2,1,0:T(8,128)(2,1)}), bf16[128,16,1024]{2,1,0:T(8,128)(2,1)}, u32[]{:S(2)}, u32[]{:S(2)}) async-start(bf16[128,16,1024]{2,1,0:T(8,128)(2,1)} %bitcast.107), calls=%async_computation.1 | async-start | bytes 8388608 | tf_op jit(solution)/shard_map/all_to_all | solution.py:142
  146.9 4.7 %slice.92 = bf16[16,2,128,2,256]{4,2,3,1,0:T(8,128)(2,1)} slice(bf16[16,3,128,2,256]{4,2,3,1,0:T(8,128)(2,1)} %all-to-all-done), slice={[0:16], [0:2], [0:128], [0:2], [0:256]} | slice | bytes 8388608 | tf_op jit(solution)/shard_map/slice | solution.py:199
  151.6 4.2 %gather_fusion.1 = bf16[16,128,2,256]{3,1,2,0:T(8,128)(2,1)} fusion(bf16[32,128,2,256]{3,1,2,0:T(8,128)(2,1)} %bitcast.109, s32[1024]{0:T(1024)S(1)} %pad_clamp_fusion.1), kind=kCustom, calls=%fused_computation.1 | custom fusion | bytes 4194368 | tf_op jit(solution)/shard_map/jit(_take)/gather | solution.py:208
  155.8 4.5 %copy.145 = bf16[16,128,2,256]{1,0,3,2:T(8,128)(2,1)} copy(bf16[16,128,2,256]{3,1,2,0:T(8,128)(2,1)} %gather_fusion.1) | data formatting | bytes 4194304 | tf_op jit(solution)/shard_map/jit(_take)/gather | solution.py:208
  160.2 4.2 %gather.28 = bf16[2048,2,2,128]{0,3,2,1:T(8,128)(2,1)} reshape(bf16[16,128,2,256]{1,0,3,2:T(8,128)(2,1)} %copy.145) | data formatting | bytes 4194304 | tf_op jit(solution)/shard_map/jit(_take)/gather | solution.py:208
  164.4 3.9 %copy.146 = bf16[2048,2,2,128]{3,0,2,1:T(8,128)(2,1)} copy(bf16[2048,2,2,128]{0,3,2,1:T(8,128)(2,1)} %gather.28) | data formatting | bytes 4194304 | tf_op jit(solution)/shard_map/jit(_take)/gather | solution.py:208
  179.8 13.6 %all-to-all-done.1 = bf16[128,16,1024]{2,1,0:T(8,128)(2,1)} async-done(((bf16[128,16,1024]{2,1,0:T(8,128)(2,1)}), bf16[128,16,1024]{2,1,0:T(8,128)(2,1)}, u32[]{:S(2)}, u32[]{:S(2)}) %all-to-all-start.1) | async-done | bytes 4194336 | tf_op jit(solution)/shard_map/all_to_all | solution.py:142
  193.4 23.4 %shard_map.218 = f32[16,2048]{1,0:T(8,128)} custom-call(f32[128,2048]{1,0:T(8,128)} %fusion.44.x_ref), custom_call_target="tpu_custom_call" | custom-call | tf_op jit(solution)/shard_map/pallas_call | solution.py:85
  219.3 3.3 broadcast_in_dim.163
  225.0 33.0 %all_to_all.27 = bf16[128,3,2048]{2,1,0:T(4,128)(2,1)} all-to-all(bf16[128,3,2048]{2,1,0:T(4,128)(2,1)S(1)} %bitcast.112), channel_id=1, replica_groups=mesh['req'=16,'tp'=8] {'req','tp'}, dimensions={0} | all-to-all | bytes 3145728 | tf_op jit(solution)/shard_map/all_to_all | solution.py:272
  258.0 5.0 %reshape.389 = bf16[384,2048]{1,0:T(8,128)(2,1)} reshape(bf16[128,3,2048]{2,1,0:T(4,128)(2,1)} %all_to_all.27) | data formatting | bytes 3145728 | tf_op jit(solution)/shard_map/reshape | solution.py:273
  263.0 4.4 %fusion = f32[384,1024]{1,0:T(8,128)S(1)} fusion(bf16[384,2048]{1,0:T(8,128)(2,1)} %reshape.389, bf16[1,2048,1024]{2,1,0:T(8,128)(2,1)} %bitcast.7), kind=kOutput, calls=%fused_computation.6 | convolution fusion | flops 1610612736 | bytes 7340032 | tf_op jit(solution)/shard_map/dot_general | solution.py:274
  269.6 5.2 %reshape.390 = bf16[128,3,2048]{2,1,0:T(4,128)(2,1)} reshape(bf16[384,2048]{1,0:T(8,128)(2,1)} %convolution_convert_fusion) | data formatting | bytes 3145728 | tf_op jit(solution)/shard_map/reshape | solution.py:279
  274.8 6.6 %all-to-all-start.3 = ((bf16[128,3,2048]{2,1,0:T(4,128)(2,1)}), bf16[128,3,2048]{2,1,0:T(4,128)(2,1)}, u32[]{:S(2)}, u32[]{:S(2)}) async-start(bf16[128,3,2048]{2,1,0:T(4,128)(2,1)} %reshape.390), calls=%async_computation.3 | async-start | bytes 4194304 | tf_op jit(solution)/shard_map/all_to_all | solution.py:281
  289.4 20.5 %all-to-all-done.3 = bf16[128,3,2048]{2,1,0:T(4,128)(2,1)} async-done(((bf16[128,3,2048]{2,1,0:T(4,128)(2,1)}), bf16[128,3,2048]{2,1,0:T(4,128)(2,1)}, u32[]{:S(2)}, u32[]{:S(2)}) %all-to-all-start.3) | async-done | bytes 1572896 | tf_op jit(solution)/shard_map/all_to_all | solution.py:281
  309.9 3.7 %convert_add_fusion = f32[64,1,3,2048]{3,2,0,1:T(4,128)} fusion(bf16[64,2,3,2048]{3,2,1,0:T(4,128)(2,1)} %bitcast.23), kind=kLoop, calls=%fused_computation.15 | loop fusion | flops 1179648 | bytes 3145728 | tf_op jit(solution)/shard_map/add | solution.py:283
  313.6 3.8 %add.190 = f32[192,2048]{1,0:T(8,128)} reshape(f32[64,1,3,2048]{3,2,0,1:T(4,128)} %convert_add_fusion) | data formatting | bytes 3145728 | tf_op jit(solution)/shard_map/add | solution.py:283
  317.4 3.0 gather_fusion.2
  322.0 3.8 %copy.174 = bf16[2048,768]{1,0:T(8,128)(2,1)} copy(bf16[2048,768]{1,0:T(8,128)(2,1)} %all-gather.2.cloned.1.call-done) | data formatting | bytes 6291456
  325.7 4.6 %copy.175 = bf16[1,2048,1024]{2,1,0:T(8,128)(2,1)} copy(bf16[1,2048,1024]{2,1,0:T(8,128)(2,1)} %bitcast.7) | data formatting | bytes 8388608
  (146 shorter events, 47.5 us)
Async XLA Ops:
  7.2 260.3 %copy-start = (bf16[1,512,2048]{2,1,0:T(8,128)(2,1)S(1)}, bf16[1,512,2048]{2,1,0:T(8,128)(2,1)}, u32[]{:S(2)}) copy-start(bf16[1,512,2048]{2,1,0:T(8,128)(2,1)} %param.32) | copy-start | bytes 6291460
  21.6 5.2 %copy-start.7 = (f32[256,128]{1,0:T(8,128)S(1)}, f32[256,128]{1,0:T(8,128)}, u32[]{:S(2)}) copy-start(f32[256,128]{1,0:T(8,128)} %param.29) | copy-start | bytes 393220
  33.0 8.3 %copy-start.8 = (f32[128,256]{1,0:T(8,128)S(1)}, f32[128,256]{1,0:T(8,128)}, u32[]{:S(2)}) copy-start(f32[128,256]{1,0:T(8,128)} %param.26) | copy-start | bytes 393220
  33.0 8.3 %copy-start.9 = (f32[128,256]{1,0:T(8,128)S(1)}, f32[128,256]{1,0:T(8,128)}, u32[]{:S(2)}) copy-start(f32[128,256]{1,0:T(8,128)} %param.27) | copy-start | bytes 393220
  33.0 8.3 %copy-start.10 = (f32[128,256]{1,0:T(8,128)S(1)}, f32[128,256]{1,0:T(8,128)}, u32[]{:S(2)}) copy-start(f32[128,256]{1,0:T(8,128)} %param.28) | copy-start | bytes 393220
  33.0 9.1 %copy-start.20 = (s32[32]{0:T(128)S(1)}, s32[32]{0:T(128)}, u32[]{:S(2)}) copy-start(s32[32]{0:T(128)} %param.36) | copy-start | bytes 388
  33.0 9.1 %copy-start.21 = (s32[32]{0:T(128)S(1)}, s32[32]{0:T(128)}, u32[]{:S(2)}) copy-start(s32[32]{0:T(128)} %param.35) | copy-start | bytes 388
  33.0 98.7 %all-to-all-start = ((bf16[16,3,128,2,256]{4,2,3,1,0:T(8,128)(2,1)}), bf16[16,3,128,2,256]{4,2,3,1,0:T(8,128)(2,1)}, u32[]{:S(2)}, u32[]{:S(2)}) async-start(bf16[16,3,128,2,256]{4,2,3,1,0:T(8,128)(2,1)} %pad_maximum_fusion), calls=%async_computation | async-start | bytes 12582912 | tf_op jit(solution)/shard_map/all_to_all | solution.py:198
  41.1 101.1 %all-gather.2.cloned.1.call-start = ((), (), s32[]{:S(2)}) async-start(), calls=%async_computation.4 | async-start | bytes 3342336 | tf_op jit(solution)/shard_map/all_gather | solution.py:131
  70.1 5.7 %copy-start.2 = (bf16[128,2048]{1,0:T(8,128)(2,1)S(1)}, bf16[128,2048]{1,0:T(8,128)(2,1)}, u32[]{:S(2)}) copy-start(bf16[128,2048]{1,0:T(8,128)(2,1)} %param.21) | copy-start | bytes 1572868
  70.1 6.7 %copy-start.6 = (s32[16,8]{0,1:T(8,128)S(1)}, s32[16,8]{0,1:T(8,128)}, u32[]{:S(2)}) copy-start(s32[16,8]{0,1:T(8,128)} %param.39) | copy-start | bytes 1540
  77.4 54.3 %copy-start.17 = (s32[128]{0:T(128)}, s32[128]{0:T(128)S(1)}, u32[]{:S(2)}) copy-start(s32[128]{0:T(128)S(1)} %select_reduce_fusion) | copy-start | bytes 1540
  131.7 10.5 %copy-start.13 = (f32[2048]{0:T(1024)S(1)}, f32[2048]{0:T(1024)}, u32[]{:S(2)}) copy-start(f32[2048]{0:T(1024)} %param.22) | copy-start | bytes 24580
  131.7 61.7 %all-to-all-start.1 = ((bf16[128,16,1024]{2,1,0:T(8,128)(2,1)}), bf16[128,16,1024]{2,1,0:T(8,128)(2,1)}, u32[]{:S(2)}, u32[]{:S(2)}) async-start(bf16[128,16,1024]{2,1,0:T(8,128)(2,1)} %bitcast.107), calls=%async_computation.1 | async-start | bytes 8388608 | tf_op jit(solution)/shard_map/all_to_all | solution.py:142
  144.7 0.8 copy-start.3
  173.0 3.0 copy-start.1
  176.0 0.7 copy-start.19
  177.4 0.8 copy-start.11
  178.2 39.8 %copy-start.12 = (f32[2048]{0:T(1024)S(1)}, f32[2048]{0:T(1024)}, u32[]{:S(2)}) copy-start(f32[2048]{0:T(1024)} %param.25) | copy-start | bytes 24580
  218.0 7.1 %copy-start.16 = (f32[16]{0:T(128)}, f32[16]{0:T(128)S(1)}, u32[]{:S(2)}) copy-start(f32[16]{0:T(128)S(1)} %add_rsqrt_fusion.2) | copy-start | bytes 196
  274.8 7.0 %copy-start.15 = (pred[16,8]{0,1:T(8,128)(4,1)S(1)}, pred[16,8]{0,1:T(8,128)(4,1)}, u32[]{:S(2)}) copy-start(pred[16,8]{0,1:T(8,128)(4,1)} %get-tuple-element.51) | copy-start | bytes 388
  274.8 7.6 %copy-start.18 = (s32[128]{0:T(128)S(1)}, s32[128]{0:T(128)}, u32[]{:S(2)}) copy-start(s32[128]{0:T(128)} %copy-done.17) | copy-start | bytes 1540
  274.8 35.1 %all-to-all-start.3 = ((bf16[128,3,2048]{2,1,0:T(4,128)(2,1)}), bf16[128,3,2048]{2,1,0:T(4,128)(2,1)}, u32[]{:S(2)}, u32[]{:S(2)}) async-start(bf16[128,3,2048]{2,1,0:T(4,128)(2,1)} %reshape.390), calls=%async_computation.3 | async-start | bytes 4194304 | tf_op jit(solution)/shard_map/all_to_all | solution.py:281
  283.8 1.4 copy-start.4
  286.1 1.6 copy-start.5
  317.4 3.0 copy-start.14
Sparse Core Ops, SparseCore 0:
  44.2 88.7 all-gather.1

commit v5 on v2

--- a/solution.py
+++ b/solution.py
@@ -184,13 +184,9 @@
         page_rank[:, None, :] == jnp.arange(capacity, dtype=jnp.int32)[None, :, None]
     )
     send_slot = jnp.sum(jnp.where(chosen, page_slot[:, None, :], 0), axis=2)
-    send_live = jnp.any(chosen, axis=2)
     page_shape = page_store.shape[1:]
     outgoing_pages = jnp.take(page_store, send_slot.reshape(-1), axis=0).reshape(
         (req_count, capacity) + page_shape
-    )
-    outgoing_pages = jnp.where(
-        send_live[:, :, None, None, None], outgoing_pages, jnp.zeros_like(outgoing_pages)
     )
     arrived_pages = lax.all_to_all(outgoing_pages, "req", split_axis=0, concat_axis=0, tiled=True)
     own_owner = jnp.take(page_owner, req_index, axis=0)

time: 307 us -> 305 us (level)
    select_n x1 -> x2, other arithmetic: 0.01 us -> 4.71 us  [body(): jnp.take(page_store, send_slot.reshape(-1), axis=0)]
    select_n x1 -> x0, other arithmetic: 4.14 us -> none  [body(): jnp.where(send_live[:, :, None, None, None], outgoing_pages, jnp.zeros_li...]
  transfers between devices with their start and end apart: 5 -> 5, of which waited for: 3 -> 4; matrix products, arithmetic and copies ran while one was open for 30% -> 30% of each run, Pallas kernels for 0% -> 0%
where the time goes in v5:
time: 305 us; the launch traced here: 303 us
  local copies, waits for them, and re-layouts  79.3 us (26%)
  waiting for transfers between devices  63.6 us (21%)
  other arithmetic  47 us (15%)
  blocking collectives  37.1 us (12%)
  Pallas kernels  24 us (8%)
  starting transfers between devices  22.9 us (8%)
  matrix products  14.9 us (5%)
  between operations  14.5 us (5%)
    all_to_all x1, blocking collectives, body(): lax.all_to_all(send_rows, ('req', 'tp'), split_axis=0, concat_axis=0, til...  37.1 us
    all_to_all x1, waiting for transfers between devices, body(): lax.all_to_all(expert_rows, ('req', 'tp'), split_axis=0, concat_axis=0, t...  24.3 us
    pallas_call x1, Pallas kernels, scatter_sum(): pl.pallas_call(functools.partial(scatter_sum_kernel, parts), out_shape=ja...  24 us
    all_gather x1, waiting for transfers between devices, body(): lax.all_gather(out_weight.astype(jnp.bfloat16), 'req', axis=1, tiled=True)  22.4 us
    gather x4, local copies, waits for them, and re-layouts, body(): jnp.take(arrived_pages.reshape((req_count * capacity,) + page_shape), own...  16.8 us
    all_to_all x1, waiting for transfers between devices, body(): lax.all_to_all(outgoing_pages, 'req', split_axis=0, concat_axis=0, tiled=...  16.7 us
    unnamed x35, local copies, waits for them, and re-layouts  11.9 us
    concatenate x1, other arithmetic, body(): jnp.concatenate([split_halves(gate_weight.astype(jnp.bfloat16)), split_ha...  10.6 us
  transfers between devices with their start and end apart: 5, of which 4 were waited for; matrix products, arithmetic and copies ran while one was open for 30% of the time, Pallas kernels for 0%

profile of v5, /device:TPU:1, one launch (start us, length us, event | category | flops | bytes accessed | tf_op | source)
XLA Modules:
  0.0 303.3 jit_solution(13599030905442523156)
XLA Ops:
  13.9 10.0 %gather_fusion = bf16[32,128,2,256]{3,2,1,0:T(2,128)(2,1)} fusion(bf16[8,128,2,256]{3,2,1,0:T(2,128)(2,1)S(1)} %copy-done.1, s32[1024]{0:T(1024)S(1)} %pad_clamp_fusion.2), kind=kCustom, calls=%fused_computation | custom fusion | bytes 8388736 | tf_op jit(solution)/shard_map/jit(_take)/gather | solution.py:188
  24.0 4.7 %copy_select_fusion = bf16[16,2,128,2,256]{4,2,3,1,0:T(8,128)(2,1)} fusion(bf16[16,2,128,2,256]{4,3,2,1,0:T(2,128)(2,1)} %bitcast.101, pred[16,2]{1,0:T(8,128)(4,1)S(1)} %copy.130), kind=kLoop, calls=%fused_computation.7 | loop fusion | flops 2097152 | bytes 8388640 | tf_op jit(solution)/shard_map/jit(_take)/select_n | solution.py:188
  28.7 8.1 %all-to-all-start.1 = ((bf16[16,2,128,2,256]{4,2,3,1,0:T(8,128)(2,1)}), bf16[16,2,128,2,256]{4,2,3,1,0:T(8,128)(2,1)}, u32[]{:S(2)}, u32[]{:S(2)}) async-start(bf16[16,2,128,2,256]{4,2,3,1,0:T(8,128)(2,1)} %copy_select_fusion), calls=%async_computation.1 | async-start | bytes 8388608 | tf_op jit(solution)/shard_map/all_to_all | solution.py:191
  38.2 3.9 %convert_element_type.113 = bf16[64,16,1024]{2,1,0:T(8,128)(2,1)} convert(f32[64,16,1024]{2,1,0:T(8,128)} %param.30) | non-fusion elementwise | flops 1048576 | bytes 6291456 | tf_op jit(solution)/shard_map/convert_element_type | solution.py:139
  42.1 4.5 %reshape.370 = bf16[64,16,2,512]{3,2,1,0:T(2,128)(2,1)} reshape(bf16[64,16,1024]{2,1,0:T(8,128)(2,1)} %convert_element_type.113) | data formatting | bytes 4194304 | tf_op jit(solution)/shard_map/reshape | solution.py:38
  46.6 3.9 %convert_element_type.114 = bf16[64,16,1024]{2,1,0:T(8,128)(2,1)} convert(f32[64,16,1024]{2,1,0:T(8,128)} %param.31) | non-fusion elementwise | flops 1048576 | bytes 6291456 | tf_op jit(solution)/shard_map/convert_element_type | solution.py:140
  50.5 4.5 %reshape.371 = bf16[64,16,2,512]{3,2,1,0:T(2,128)(2,1)} reshape(bf16[64,16,1024]{2,1,0:T(8,128)(2,1)} %convert_element_type.114) | data formatting | bytes 4194304 | tf_op jit(solution)/shard_map/reshape | solution.py:38
  55.0 10.6 %pad_maximum_fusion = bf16[64,2,16,1024]{3,1,2,0:T(2,128)(2,1)} fusion(bf16[64,2,16,512]{3,1,2,0:T(2,128)(2,1)} %bitcast.105, bf16[64,2,16,512]{3,1,2,0:T(2,128)(2,1)} %bitcast.104), kind=kLoop, calls=%fused_computation.4 | loop fusion | flops 8388608 | bytes 8388608 | tf_op jit(solution)/shard_map/concatenate | solution.py:137
  65.6 5.7 %copy.125 = bf16[64,2,16,1024]{3,2,1,0:T(8,128)(2,1)} copy(bf16[64,2,16,1024]{3,1,2,0:T(2,128)(2,1)} %pad_maximum_fusion) | data formatting | bytes 8388608 | tf_op jit(solution)/shard_map/concatenate | solution.py:137
  79.2 16.7 %all-to-all-done.1 = bf16[16,2,128,2,256]{4,2,3,1,0:T(8,128)(2,1)} async-done(((bf16[16,2,128,2,256]{4,2,3,1,0:T(8,128)(2,1)}), bf16[16,2,128,2,256]{4,2,3,1,0:T(8,128)(2,1)}, u32[]{:S(2)}, u32[]{:S(2)}) %all-to-all-start.1) | async-done | bytes 4194336 | tf_op jit(solution)/shard_map/all_to_all | solution.py:191
  95.9 8.2 %all-to-all-start = ((bf16[128,16,1024]{2,1,0:T(8,128)(2,1)}), bf16[128,16,1024]{2,1,0:T(8,128)(2,1)}, u32[]{:S(2)}, u32[]{:S(2)}) async-start(bf16[128,16,1024]{2,1,0:T(8,128)(2,1)} %bitcast.102), calls=%async_computation | async-start | bytes 8388608 | tf_op jit(solution)/shard_map/all_to_all | solution.py:144
  104.1 4.2 %gather_fusion.1 = bf16[16,128,2,256]{3,1,2,0:T(8,128)(2,1)} fusion(bf16[32,128,2,256]{3,1,2,0:T(8,128)(2,1)} %bitcast.13, s32[1024]{0:T(1024)S(1)} %pad_clamp_fusion.1), kind=kCustom, calls=%fused_computation.1 | custom fusion | bytes 4194368 | tf_op jit(solution)/shard_map/jit(_take)/gather | solution.py:194
  108.3 4.5 %copy.133 = bf16[16,128,2,256]{1,0,3,2:T(8,128)(2,1)} copy(bf16[16,128,2,256]{3,1,2,0:T(8,128)(2,1)} %gather_fusion.1) | data formatting | bytes 4194304 | tf_op jit(solution)/shard_map/jit(_take)/gather | solution.py:194
  112.8 4.2 %gather.28 = bf16[2048,2,2,128]{0,3,2,1:T(8,128)(2,1)} reshape(bf16[16,128,2,256]{1,0,3,2:T(8,128)(2,1)} %copy.133) | data formatting | bytes 4194304 | tf_op jit(solution)/shard_map/jit(_take)/gather | solution.py:194
  117.0 3.9 %copy.134 = bf16[2048,2,2,128]{3,0,2,1:T(8,128)(2,1)} copy(bf16[2048,2,2,128]{0,3,2,1:T(8,128)(2,1)} %gather.28) | data formatting | bytes 4194304 | tf_op jit(solution)/shard_map/jit(_take)/gather | solution.py:194
  120.9 2.8 broadcast_select_fusion
  123.7 2.5 fusion.12
  131.0 22.4 %all-gather.5.cloned.1.call-done = bf16[256,2048]{1,0:T(8,128)(2,1)} async-done(((bf16[256,128]{1,0:T(8,128)(2,1)}), bf16[256,2048]{1,0:T(8,128)(2,1)}) %all-gather.5.cloned.1.call-update) | async-done | bytes 1048592 | tf_op jit(solution)/shard_map/all_gather | solution.py:133
  153.3 2.5 fusion.43.x_ref
  156.0 24.0 %shard_map.218 = f32[16,2048]{1,0:T(8,128)} custom-call(f32[128,2048]{1,0:T(8,128)} %fusion.43.x_ref), custom_call_target="tpu_custom_call" | custom-call | tf_op jit(solution)/shard_map/pallas_call | solution.py:85
  182.4 2.4 broadcast_in_dim.142
  186.0 37.1 %all_to_all.27 = bf16[128,3,2048]{2,1,0:T(4,128)(2,1)} all-to-all(bf16[128,3,2048]{2,1,0:T(4,128)(2,1)S(1)} %bitcast.103), channel_id=1, replica_groups=mesh['req'=16,'tp'=8] {'req','tp'}, dimensions={0} | all-to-all | bytes 3145728 | tf_op jit(solution)/shard_map/all_to_all | solution.py:258
  223.1 5.0 %reshape.381 = bf16[384,2048]{1,0:T(8,128)(2,1)} reshape(bf16[128,3,2048]{2,1,0:T(4,128)(2,1)} %all_to_all.27) | data formatting | bytes 3145728 | tf_op jit(solution)/shard_map/reshape | solution.py:259
  228.2 4.4 %fusion = f32[384,1024]{1,0:T(8,128)S(1)} fusion(bf16[384,2048]{1,0:T(8,128)(2,1)} %reshape.381, bf16[1,2048,1024]{2,1,0:T(8,128)(2,1)} %bitcast.3), kind=kOutput, calls=%fused_computation.5 | convolution fusion | flops 1610612736 | bytes 7340032 | tf_op jit(solution)/shard_map/dot_general | solution.py:260
  234.8 5.2 %reshape.382 = bf16[128,3,2048]{2,1,0:T(4,128)(2,1)} reshape(bf16[384,2048]{1,0:T(8,128)(2,1)} %convolution_convert_fusion) | data formatting | bytes 3145728 | tf_op jit(solution)/shard_map/reshape | solution.py:265
  240.0 6.6 %all-to-all-start.3 = ((bf16[128,3,2048]{2,1,0:T(4,128)(2,1)}), bf16[128,3,2048]{2,1,0:T(4,128)(2,1)}, u32[]{:S(2)}, u32[]{:S(2)}) async-start(bf16[128,3,2048]{2,1,0:T(4,128)(2,1)} %reshape.382), calls=%async_computation.3 | async-start | bytes 4194304 | tf_op jit(solution)/shard_map/all_to_all | solution.py:267
  250.7 24.3 %all-to-all-done.3 = bf16[128,3,2048]{2,1,0:T(4,128)(2,1)} async-done(((bf16[128,3,2048]{2,1,0:T(4,128)(2,1)}), bf16[128,3,2048]{2,1,0:T(4,128)(2,1)}, u32[]{:S(2)}, u32[]{:S(2)}) %all-to-all-start.3) | async-done | bytes 1572896 | tf_op jit(solution)/shard_map/all_to_all | solution.py:267
  275.0 3.7 %convert_add_fusion = f32[64,1,3,2048]{3,2,0,1:T(4,128)} fusion(bf16[64,2,3,2048]{3,2,1,0:T(4,128)(2,1)} %bitcast.21), kind=kLoop, calls=%fused_computation.14 | loop fusion | flops 1179648 | bytes 3145728 | tf_op jit(solution)/shard_map/add | solution.py:269
  278.8 3.8 %add.188 = f32[192,2048]{1,0:T(8,128)} reshape(f32[64,1,3,2048]{3,2,0,1:T(4,128)} %convert_add_fusion) | data formatting | bytes 3145728 | tf_op jit(solution)/shard_map/add | solution.py:269
  282.5 2.9 gather_fusion.2
  287.0 3.8 %copy.163 = bf16[2048,768]{1,0:T(8,128)(2,1)} copy(bf16[2048,768]{1,0:T(8,128)(2,1)} %all-gather.3.cloned.1.call-done) | data formatting | bytes 6291456
  291.8 4.6 %copy.165 = bf16[1,2048,1024]{2,1,0:T(8,128)(2,1)} copy(bf16[1,2048,1024]{2,1,0:T(8,128)(2,1)} %bitcast.3) | data formatting | bytes 8388608
  (124 shorter events, 33.2 us)
Async XLA Ops:
  7.2 225.5 %copy-start = (bf16[1,512,2048]{2,1,0:T(8,128)(2,1)S(1)}, bf16[1,512,2048]{2,1,0:T(8,128)(2,1)}, u32[]{:S(2)}) copy-start(bf16[1,512,2048]{2,1,0:T(8,128)(2,1)} %param.32) | copy-start | bytes 6291460
  7.2 6.7 %copy-start.1 = (bf16[8,128,2,256]{3,2,1,0:T(2,128)(2,1)S(1)}, bf16[8,128,2,256]{3,2,1,0:T(2,128)(2,1)}, u32[]{:S(2)}) copy-start(bf16[8,128,2,256]{3,2,1,0:T(2,128)(2,1)} %param.34) | copy-start | bytes 3145732
  7.2 116.5 %all-gather.3.cloned.1.call-start = ((), (), s32[]{:S(2)}) async-start(), calls=%async_computation.4 | async-start | bytes 3342336 | tf_op jit(solution)/shard_map/all_gather | solution.py:132
  28.7 8.1 %copy-start.8 = (f32[256,128]{1,0:T(8,128)S(1)}, f32[256,128]{1,0:T(8,128)}, u32[]{:S(2)}) copy-start(f32[256,128]{1,0:T(8,128)} %param.29) | copy-start | bytes 393220
  28.7 8.8 %copy-start.13 = (s32[32]{0:T(128)S(1)}, s32[32]{0:T(128)}, u32[]{:S(2)}) copy-start(s32[32]{0:T(128)} %param.36) | copy-start | bytes 388
  28.7 8.9 %copy-start.14 = (s32[32]{0:T(128)S(1)}, s32[32]{0:T(128)}, u32[]{:S(2)}) copy-start(s32[32]{0:T(128)} %param.35) | copy-start | bytes 388
  28.7 67.2 %all-to-all-start.1 = ((bf16[16,2,128,2,256]{4,2,3,1,0:T(8,128)(2,1)}), bf16[16,2,128,2,256]{4,2,3,1,0:T(8,128)(2,1)}, u32[]{:S(2)}, u32[]{:S(2)}) async-start(bf16[16,2,128,2,256]{4,2,3,1,0:T(8,128)(2,1)} %copy_select_fusion), calls=%async_computation.1 | async-start | bytes 8388608 | tf_op jit(solution)/shard_map/all_to_all | solution.py:191
  36.8 116.6 %all-gather.5.cloned.1.call-start = ((), (), s32[]{:S(2)}) async-start(), calls=%async_computation.5 | async-start | bytes 1114112 | tf_op jit(solution)/shard_map/all_gather | solution.py:133
  65.6 5.7 %copy-start.2 = (bf16[128,2048]{1,0:T(8,128)(2,1)S(1)}, bf16[128,2048]{1,0:T(8,128)(2,1)}, u32[]{:S(2)}) copy-start(bf16[128,2048]{1,0:T(8,128)(2,1)} %param.21) | copy-start | bytes 1572868
  65.6 6.8 %copy-start.7 = (s32[16,8]{0,1:T(8,128)S(1)}, s32[16,8]{0,1:T(8,128)}, u32[]{:S(2)}) copy-start(s32[16,8]{0,1:T(8,128)} %param.39) | copy-start | bytes 1540
  95.9 60.0 %all-to-all-start = ((bf16[128,16,1024]{2,1,0:T(8,128)(2,1)}), bf16[128,16,1024]{2,1,0:T(8,128)(2,1)}, u32[]{:S(2)}, u32[]{:S(2)}) async-start(bf16[128,16,1024]{2,1,0:T(8,128)(2,1)} %bitcast.102), calls=%async_computation | async-start | bytes 8388608 | tf_op jit(solution)/shard_map/all_to_all | solution.py:144
  120.9 2.8 copy-start.10
  123.7 4.3 %copy-start.11 = (f32[128]{0:T(128)S(1)}, f32[128]{0:T(128)}, u32[]{:S(2)}) copy-start(f32[128]{0:T(128)} %param.24) | copy-start | bytes 1540
  123.7 4.3 %copy-start.12 = (f32[128]{0:T(128)S(1)}, f32[128]{0:T(128)}, u32[]{:S(2)}) copy-start(f32[128]{0:T(128)} %param.23) | copy-start | bytes 1540
  126.2 0.8 copy-start.5
  127.9 1.6 copy-start.4
  130.8 50.3 %copy-start.9 = (f32[2048]{0:T(1024)S(1)}, f32[2048]{0:T(1024)}, u32[]{:S(2)}) copy-start(f32[2048]{0:T(1024)} %param.25) | copy-start | bytes 24580
  240.0 7.1 %copy-start.6 = (bf16[2048,64]{0,1:T(8,128)(2,1)S(1)}, bf16[2048,64]{0,1:T(8,128)(2,1)}, u32[]{:S(2)}) copy-start(bf16[2048,64]{0,1:T(8,128)(2,1)} %param.33) | copy-start | bytes 786436
  240.0 35.1 %all-to-all-start.3 = ((bf16[128,3,2048]{2,1,0:T(4,128)(2,1)}), bf16[128,3,2048]{2,1,0:T(4,128)(2,1)}, u32[]{:S(2)}, u32[]{:S(2)}) async-start(bf16[128,3,2048]{2,1,0:T(4,128)(2,1)} %reshape.382), calls=%async_computation.3 | async-start | bytes 4194304 | tf_op jit(solution)/shard_map/all_to_all | solution.py:267
  287.0 3.8 %copy-start.3 = (bf16[256,2048]{1,0:T(8,128)(2,1)S(1)}, bf16[256,2048]{1,0:T(8,128)(2,1)}, u32[]{:S(2)}) copy-start(bf16[256,2048]{1,0:T(8,128)(2,1)} %all-gather.5.cloned.1.call-done) | copy-start | bytes 3145732
Sparse Core Ops, SparseCore 0:
  11.0 65.7 all-gather.2
  79.0 74.3 all-gather.4

commit v6 on v5

--- a/solution.py
+++ b/solution.py
@@ -93,6 +93,55 @@
             pltpu.SemaphoreType.DMA((parts,)),
         ],
         compiler_params=pltpu.CompilerParams(collective_id=0, has_side_effects=True),
+    )(x)
+
+
+def gather_kernel(count, x_ref, out_ref, held, send_sem, recv_sem):
+    me = lax.axis_index("req")
+    lane = lax.axis_index("tp")
+    width = x_ref.shape[1]
+    barrier = pltpu.get_barrier_semaphore()
+    for step in range(1, count):
+        peer = lax.rem(me + step, count)
+        pl.semaphore_signal(barrier, inc=1, device_id=(peer, lane), device_id_type=MESH)
+    pl.semaphore_wait(barrier, count - 1)
+
+    def transfer(peer, slot):
+        return pltpu.make_async_remote_copy(
+            src_ref=x_ref,
+            dst_ref=held.at[slot],
+            send_sem=send_sem.at[peer],
+            recv_sem=recv_sem.at[slot],
+            device_id=(peer, lane),
+            device_id_type=MESH,
+        )
+
+    for step in range(1, count):
+        peer = lax.rem(me + step, count)
+        transfer(peer, me).start()
+    held[me] = x_ref[...]
+    for step in range(1, count):
+        peer = lax.rem(me + count - step, count)
+        transfer(peer, peer).wait_recv()
+    for step in range(1, count):
+        peer = lax.rem(me + step, count)
+        transfer(peer, me).wait_send()
+    for slot in range(count):
+        out_ref[:, slot * width : (slot + 1) * width] = held[slot]
+
+
+def gather_columns(x, count):
+    return pl.pallas_call(
+        functools.partial(gather_kernel, count),
+        out_shape=jax.ShapeDtypeStruct((x.shape[0], count * x.shape[1]), x.dtype),
+        in_specs=[pl.BlockSpec(memory_space=pltpu.VMEM)],
+        out_specs=pl.BlockSpec(memory_space=pltpu.VMEM),
+        scratch_shapes=[
+            pltpu.VMEM((count,) + x.shape, x.dtype),
+            pltpu.SemaphoreType.DMA((count,)),
+            pltpu.SemaphoreType.DMA((count,)),
+        ],
+        compiler_params=pltpu.CompilerParams(collective_id=3, has_side_effects=True),
     )(x)
 
 
@@ -128,10 +177,8 @@
         ],
         axis=1,
     )
-    server_qkv, server_out = (
-        lax.all_gather(joined_local, "req", axis=0, tiled=True),
-        lax.all_gather(out_weight.astype(jnp.bfloat16), "req", axis=1, tiled=True),
-    )
+    server_qkv = lax.all_gather(joined_local, "req", axis=0, tiled=True)
+    server_out = gather_columns(out_weight.astype(jnp.bfloat16), req_count)
     expert_count, rows_here, hidden_units = gate_weight.shape
     half_units = hidden_units // 2
     packed = jnp.concatenate(
@@ -141,6 +188,7 @@
         ],
         axis=3,
     ).reshape(2 * expert_count, rows_here, hidden_units)
+    packed, server_out = lax.optimization_barrier((packed, server_out))
     server_gate_up = lax.all_to_all(packed, ("req", "tp"), split_axis=0, concat_axis=1, tiled=True)
     group_rows, model_width = tokens.shape
     tokens_f32 = tokens.astype(jnp.float32)

time: 305 us -> 327 us (1.072)
  Pallas kernels: 24 us -> 57.8 us
  waiting for transfers between devices: 63.6 us -> 46.1 us
  starting transfers between devices: 22.9 us -> 28.3 us
  blocking collectives: 37.1 us -> 33 us
  local copies, waits for them, and re-layouts: 79.3 us -> 82.6 us
    pallas_call x0 -> x1, Pallas kernels: none -> 34.4 us  [gather_columns(): pl.pallas_call(functools.partial(gather_kernel, count), out_shape=jax.Sha...]
    all_to_all x1, waiting for transfers between devices: 0.09 us -> 22.7 us  [body(): lax.all_to_all(packed, ('req', 'tp'), split_axis=0, concat_axis=1, tiled=...]
    all_gather x2 -> x1, waiting for transfers between devices: 22.4 us -> 0.01 us  [body(): server_qkv = lax.all_gather(joined_local, 'req', axis=0, tiled=True)]
    all_to_all x1, waiting for transfers between devices: 16.7 us -> 0.01 us  [body(): lax.all_to_all(outgoing_pages, 'req', split_axis=0, concat_axis=0, tiled=...]
    all_to_all x1, starting transfers between devices: 8.16 us -> 13.6 us  [body(): lax.all_to_all(packed, ('req', 'tp'), split_axis=0, concat_axis=1, tiled=...]
    all_to_all x1, blocking collectives: 37.1 us -> 33 us  [body(): lax.all_to_all(send_rows, ('req', 'tp'), split_axis=0, concat_axis=0, til...]
    unnamed x35 -> x33, local copies, waits for them, and re-layouts: 11.9 us -> 12.3 us
  transfers between devices with their start and end apart: 5 -> 4, of which waited for: 4 -> 2; matrix products, arithmetic and copies ran while one was open for 30% -> 28% of each run, Pallas kernels for 0% -> 11%
where the time goes in v6:
time: 327 us; the launch traced here: 325 us
  local copies, waits for them, and re-layouts  82.6 us (25%)
  Pallas kernels  57.8 us (18%)
  other arithmetic  48.2 us (15%)
  waiting for transfers between devices  46.1 us (14%)
  blocking collectives  33 us (10%)
  starting transfers between devices  28.3 us (9%)
  matrix products  14.7 us (4%)
  between operations  14.5 us (4%)
    pallas_call x1, Pallas kernels, gather_columns(): pl.pallas_call(functools.partial(gather_kernel, count), out_shape=jax.Sha...  34.4 us
    all_to_all x1, blocking collectives, body(): lax.all_to_all(send_rows, ('req', 'tp'), split_axis=0, concat_axis=0, til...  33 us
    pallas_call x1, Pallas kernels, scatter_sum(): pl.pallas_call(functools.partial(scatter_sum_kernel, parts), out_shape=ja...  23.4 us
    all_to_all x1, waiting for transfers between devices, body(): lax.all_to_all(expert_rows, ('req', 'tp'), split_axis=0, concat_axis=0, t...  23.4 us
    all_to_all x1, waiting for transfers between devices, body(): lax.all_to_all(packed, ('req', 'tp'), split_axis=0, concat_axis=1, tiled=...  22.7 us
    gather x4, local copies, waits for them, and re-layouts, body(): jnp.take(arrived_pages.reshape((req_count * capacity,) + page_shape), own...  16.8 us
    all_to_all x1, starting transfers between devices, body(): lax.all_to_all(packed, ('req', 'tp'), split_axis=0, concat_axis=1, tiled=...  13.6 us
    unnamed x33, local copies, waits for them, and re-layouts  12.3 us
  transfers between devices with their start and end apart: 4, of which 2 were waited for; matrix products, arithmetic and copies ran while one was open for 28% of the time, Pallas kernels for 11%

profile of v6, /device:TPU:1, one launch (start us, length us, event | category | flops | bytes accessed | tf_op | source)
XLA Modules:
  0.0 325.1 jit_solution(9502143248926262224)
XLA Ops:
  13.9 10.1 %gather_fusion = bf16[32,128,2,256]{3,2,1,0:T(2,128)(2,1)} fusion(bf16[8,128,2,256]{3,2,1,0:T(2,128)(2,1)S(1)} %copy-done.1, s32[1024]{0:T(1024)S(1)} %pad_clamp_fusion.2), kind=kCustom, calls=%fused_computation | custom fusion | bytes 8388736 | tf_op jit(solution)/shard_map/jit(_take)/gather | solution.py:236
  24.0 4.7 %copy_select_fusion = bf16[16,2,128,2,256]{4,2,3,1,0:T(8,128)(2,1)} fusion(bf16[16,2,128,2,256]{4,3,2,1,0:T(2,128)(2,1)} %bitcast.101, pred[16,2]{1,0:T(8,128)(4,1)S(1)} %copy.130), kind=kLoop, calls=%fused_computation.7 | loop fusion | flops 2097152 | bytes 8388640 | tf_op jit(solution)/shard_map/jit(_take)/select_n | solution.py:236
  28.7 8.0 %all-to-all-start.1 = ((bf16[16,2,128,2,256]{4,2,3,1,0:T(8,128)(2,1)}), bf16[16,2,128,2,256]{4,2,3,1,0:T(8,128)(2,1)}, u32[]{:S(2)}, u32[]{:S(2)}) async-start(bf16[16,2,128,2,256]{4,2,3,1,0:T(8,128)(2,1)} %copy_select_fusion), calls=%async_computation.1 | async-start | bytes 8388608 | tf_op jit(solution)/shard_map/all_to_all | solution.py:239
  37.4 3.9 %convert_element_type.112 = bf16[64,16,1024]{2,1,0:T(8,128)(2,1)} convert(f32[64,16,1024]{2,1,0:T(8,128)} %param.30) | non-fusion elementwise | flops 1048576 | bytes 6291456 | tf_op jit(solution)/shard_map/convert_element_type | solution.py:186
  41.2 4.5 %reshape.370 = bf16[64,16,2,512]{3,2,1,0:T(2,128)(2,1)} reshape(bf16[64,16,1024]{2,1,0:T(8,128)(2,1)} %convert_element_type.112) | data formatting | bytes 4194304 | tf_op jit(solution)/shard_map/reshape | solution.py:38
  45.8 3.9 %convert_element_type.113 = bf16[64,16,1024]{2,1,0:T(8,128)(2,1)} convert(f32[64,16,1024]{2,1,0:T(8,128)} %param.31) | non-fusion elementwise | flops 1048576 | bytes 6291456 | tf_op jit(solution)/shard_map/convert_element_type | solution.py:187
  49.7 4.5 %reshape.371 = bf16[64,16,2,512]{3,2,1,0:T(2,128)(2,1)} reshape(bf16[64,16,1024]{2,1,0:T(8,128)(2,1)} %convert_element_type.113) | data formatting | bytes 4194304 | tf_op jit(solution)/shard_map/reshape | solution.py:38
  54.2 10.6 %pad_maximum_fusion = bf16[64,2,16,1024]{3,1,2,0:T(2,128)(2,1)} fusion(bf16[64,2,16,512]{3,1,2,0:T(2,128)(2,1)} %bitcast.105, bf16[64,2,16,512]{3,1,2,0:T(2,128)(2,1)} %bitcast.104), kind=kLoop, calls=%fused_computation.4 | loop fusion | flops 8388608 | bytes 8388608 | tf_op jit(solution)/shard_map/concatenate | solution.py:184
  64.8 5.7 %copy.125 = bf16[64,2,16,1024]{3,2,1,0:T(8,128)(2,1)} copy(bf16[64,2,16,1024]{3,1,2,0:T(2,128)(2,1)} %pad_maximum_fusion) | data formatting | bytes 8388608 | tf_op jit(solution)/shard_map/concatenate | solution.py:184
  71.1 34.4 %shard_map.218 = bf16[256,2048]{1,0:T(8,128)(2,1)} custom-call(bf16[256,128]{1,0:T(8,128)(2,1)} %convert_element_type.114.x_ref), custom_call_target="tpu_custom_call" | custom-call | tf_op jit(solution)/shard_map/pallas_call | solution.py:134
  113.4 13.6 %all-to-all-start = ((bf16[128,16,1024]{2,1,0:T(8,128)(2,1)}), bf16[128,16,1024]{2,1,0:T(8,128)(2,1)}, u32[]{:S(2)}, u32[]{:S(2)}) async-start(bf16[128,16,1024]{2,1,0:T(8,128)(2,1)} %bitcast.102), calls=%async_computation | async-start | bytes 8388608 | tf_op jit(solution)/shard_map/all_to_all | solution.py:192
  127.1 4.2 %gather_fusion.1 = bf16[16,128,2,256]{3,1,2,0:T(8,128)(2,1)} fusion(bf16[32,128,2,256]{3,1,2,0:T(8,128)(2,1)} %bitcast.13, s32[1024]{0:T(1024)S(1)} %pad_clamp_fusion.1), kind=kCustom, calls=%fused_computation.1 | custom fusion | bytes 4194368 | tf_op jit(solution)/shard_map/jit(_take)/gather | solution.py:242
  131.3 4.5 %copy.133 = bf16[16,128,2,256]{1,0,3,2:T(8,128)(2,1)} copy(bf16[16,128,2,256]{3,1,2,0:T(8,128)(2,1)} %gather_fusion.1) | data formatting | bytes 4194304 | tf_op jit(solution)/shard_map/jit(_take)/gather | solution.py:242
  135.8 4.2 %gather.28 = bf16[2048,2,2,128]{0,3,2,1:T(8,128)(2,1)} reshape(bf16[16,128,2,256]{1,0,3,2:T(8,128)(2,1)} %copy.133) | data formatting | bytes 4194304 | tf_op jit(solution)/shard_map/jit(_take)/gather | solution.py:242
  139.9 3.9 %copy.134 = bf16[2048,2,2,128]{3,0,2,1:T(8,128)(2,1)} copy(bf16[2048,2,2,128]{0,3,2,1:T(8,128)(2,1)} %gather.28) | data formatting | bytes 4194304 | tf_op jit(solution)/shard_map/jit(_take)/gather | solution.py:242
  143.9 2.8 broadcast_select_fusion
  146.7 2.5 fusion.12
  155.7 22.7 %all-to-all-done = bf16[128,16,1024]{2,1,0:T(8,128)(2,1)} async-done(((bf16[128,16,1024]{2,1,0:T(8,128)(2,1)}), bf16[128,16,1024]{2,1,0:T(8,128)(2,1)}, u32[]{:S(2)}, u32[]{:S(2)}) %all-to-all-start) | async-done | bytes 4194336 | tf_op jit(solution)/shard_map/all_to_all | solution.py:192
  178.4 23.4 %shard_map.219 = f32[16,2048]{1,0:T(8,128)} custom-call(f32[128,2048]{1,0:T(8,128)} %fusion.43.x_ref), custom_call_target="tpu_custom_call" | custom-call | tf_op jit(solution)/shard_map/pallas_call | solution.py:85
  204.2 3.3 %broadcast_in_dim.142 = bf16[64,3,2048]{2,1,0:T(4,128)(2,1)} reshape(bf16[192,2048]{1,0:T(8,128)(2,1)} %convolution_convert_fusion.1) | data formatting | bytes 1572864 | tf_op jit(solution)/shard_map/broadcast_in_dim | solution.py:302
  207.5 2.5 broadcast_in_dim.143
  209.9 33.0 %all_to_all.27 = bf16[128,3,2048]{2,1,0:T(4,128)(2,1)} all-to-all(bf16[128,3,2048]{2,1,0:T(4,128)(2,1)S(1)} %bitcast.103), channel_id=1, replica_groups=mesh['req'=16,'tp'=8] {'req','tp'}, dimensions={0} | all-to-all | bytes 3145728 | tf_op jit(solution)/shard_map/all_to_all | solution.py:306
  242.9 5.0 %reshape.381 = bf16[384,2048]{1,0:T(8,128)(2,1)} reshape(bf16[128,3,2048]{2,1,0:T(4,128)(2,1)} %all_to_all.27) | data formatting | bytes 3145728 | tf_op jit(solution)/shard_map/reshape | solution.py:307
  247.9 4.4 %fusion = f32[384,1024]{1,0:T(8,128)S(1)} fusion(bf16[384,2048]{1,0:T(8,128)(2,1)} %reshape.381, bf16[1,2048,1024]{2,1,0:T(8,128)(2,1)} %bitcast.3), kind=kOutput, calls=%fused_computation.5 | convolution fusion | flops 1610612736 | bytes 7340032 | tf_op jit(solution)/shard_map/dot_general | solution.py:308
  254.6 5.2 %reshape.382 = bf16[128,3,2048]{2,1,0:T(4,128)(2,1)} reshape(bf16[384,2048]{1,0:T(8,128)(2,1)} %convolution_convert_fusion) | data formatting | bytes 3145728 | tf_op jit(solution)/shard_map/reshape | solution.py:313
  259.7 6.6 %all-to-all-start.3 = ((bf16[128,3,2048]{2,1,0:T(4,128)(2,1)}), bf16[128,3,2048]{2,1,0:T(4,128)(2,1)}, u32[]{:S(2)}, u32[]{:S(2)}) async-start(bf16[128,3,2048]{2,1,0:T(4,128)(2,1)} %reshape.382), calls=%async_computation.3 | async-start | bytes 4194304 | tf_op jit(solution)/shard_map/all_to_all | solution.py:315
  271.4 23.4 %all-to-all-done.3 = bf16[128,3,2048]{2,1,0:T(4,128)(2,1)} async-done(((bf16[128,3,2048]{2,1,0:T(4,128)(2,1)}), bf16[128,3,2048]{2,1,0:T(4,128)(2,1)}, u32[]{:S(2)}, u32[]{:S(2)}) %all-to-all-start.3) | async-done | bytes 1572896 | tf_op jit(solution)/shard_map/all_to_all | solution.py:315
  294.8 3.7 %convert_add_fusion = f32[64,1,3,2048]{3,2,0,1:T(4,128)} fusion(bf16[64,2,3,2048]{3,2,1,0:T(4,128)(2,1)} %bitcast.21), kind=kLoop, calls=%fused_computation.14 | loop fusion | flops 1179648 | bytes 3145728 | tf_op jit(solution)/shard_map/add | solution.py:317
  298.5 3.8 %add.188 = f32[192,2048]{1,0:T(8,128)} reshape(f32[64,1,3,2048]{3,2,0,1:T(4,128)} %convert_add_fusion) | data formatting | bytes 3145728 | tf_op jit(solution)/shard_map/add | solution.py:317
  302.3 3.8 %gather_fusion.2 = f32[128,2048]{1,0:T(8,128)} fusion(f32[192,2048]{1,0:T(8,128)} %add.188, s32[1024]{0:T(1024)S(1)} %pad_clamp_fusion), kind=kCustom, calls=%fused_computation.2 | custom fusion | bytes 2097664 | tf_op jit(solution)/shard_map/jit(_take)/gather | solution.py:320
  308.9 3.8 %copy.163 = bf16[2048,768]{1,0:T(8,128)(2,1)} copy(bf16[2048,768]{1,0:T(8,128)(2,1)} %all-gather.2.cloned.1.call-done) | data formatting | bytes 6291456
  313.6 4.6 %copy.165 = bf16[1,2048,1024]{2,1,0:T(8,128)(2,1)} copy(bf16[1,2048,1024]{2,1,0:T(8,128)(2,1)} %bitcast.3) | data formatting | bytes 8388608
  (120 shorter events, 35.7 us)
Async XLA Ops:
  7.2 245.2 %copy-start = (bf16[1,512,2048]{2,1,0:T(8,128)(2,1)S(1)}, bf16[1,512,2048]{2,1,0:T(8,128)(2,1)}, u32[]{:S(2)}) copy-start(bf16[1,512,2048]{2,1,0:T(8,128)(2,1)} %param.32) | copy-start | bytes 6291460
  7.2 6.7 %copy-start.1 = (bf16[8,128,2,256]{3,2,1,0:T(2,128)(2,1)S(1)}, bf16[8,128,2,256]{3,2,1,0:T(2,128)(2,1)}, u32[]{:S(2)}) copy-start(bf16[8,128,2,256]{3,2,1,0:T(2,128)(2,1)} %param.34) | copy-start | bytes 3145732
  7.2 139.5 %all-gather.2.cloned.1.call-start = ((), (), s32[]{:S(2)}) async-start(), calls=%async_computation.4 | async-start | bytes 3342336 | tf_op jit(solution)/shard_map/all_gather | solution.py:180
  28.7 8.0 %copy-start.12 = (s32[32]{0:T(128)S(1)}, s32[32]{0:T(128)}, u32[]{:S(2)}) copy-start(s32[32]{0:T(128)} %param.36) | copy-start | bytes 388
  28.7 8.1 %copy-start.13 = (s32[32]{0:T(128)S(1)}, s32[32]{0:T(128)}, u32[]{:S(2)}) copy-start(s32[32]{0:T(128)} %param.35) | copy-start | bytes 388
  28.7 84.7 %all-to-all-start.1 = ((bf16[16,2,128,2,256]{4,2,3,1,0:T(8,128)(2,1)}), bf16[16,2,128,2,256]{4,2,3,1,0:T(8,128)(2,1)}, u32[]{:S(2)}, u32[]{:S(2)}) async-start(bf16[16,2,128,2,256]{4,2,3,1,0:T(8,128)(2,1)} %copy_select_fusion), calls=%async_computation.1 | async-start | bytes 8388608 | tf_op jit(solution)/shard_map/all_to_all | solution.py:239
  64.7 5.7 %copy-start.7 = (f32[256,128]{1,0:T(8,128)S(1)}, f32[256,128]{1,0:T(8,128)}, u32[]{:S(2)}) copy-start(f32[256,128]{1,0:T(8,128)} %param.29) | copy-start | bytes 393220
  64.7 40.7 %copy-start.3 = (bf16[128,2048]{1,0:T(8,128)(2,1)S(1)}, bf16[128,2048]{1,0:T(8,128)(2,1)}, u32[]{:S(2)}) copy-start(bf16[128,2048]{1,0:T(8,128)(2,1)} %param.21) | copy-start | bytes 1572868
  70.4 36.1 %copy-start.6 = (s32[16,8]{0,1:T(8,128)S(1)}, s32[16,8]{0,1:T(8,128)}, u32[]{:S(2)}) copy-start(s32[16,8]{0,1:T(8,128)} %param.39) | copy-start | bytes 1540
  113.4 64.9 %all-to-all-start = ((bf16[128,16,1024]{2,1,0:T(8,128)(2,1)}), bf16[128,16,1024]{2,1,0:T(8,128)(2,1)}, u32[]{:S(2)}, u32[]{:S(2)}) async-start(bf16[128,16,1024]{2,1,0:T(8,128)(2,1)} %bitcast.102), calls=%async_computation | async-start | bytes 8388608 | tf_op jit(solution)/shard_map/all_to_all | solution.py:192
  143.9 2.8 copy-start.9
  146.6 4.3 %copy-start.10 = (f32[128]{0:T(128)S(1)}, f32[128]{0:T(128)}, u32[]{:S(2)}) copy-start(f32[128]{0:T(128)} %param.24) | copy-start | bytes 1540
  146.6 4.3 %copy-start.11 = (f32[128]{0:T(128)S(1)}, f32[128]{0:T(128)}, u32[]{:S(2)}) copy-start(f32[128]{0:T(128)} %param.23) | copy-start | bytes 1540
  149.2 0.8 copy-start.5
  150.9 1.6 copy-start.4
  153.1 1.2 copy-start.2
  153.8 49.1 %copy-start.8 = (f32[2048]{0:T(1024)S(1)}, f32[2048]{0:T(1024)}, u32[]{:S(2)}) copy-start(f32[2048]{0:T(1024)} %param.25) | copy-start | bytes 24580
  259.7 35.1 %all-to-all-start.3 = ((bf16[128,3,2048]{2,1,0:T(4,128)(2,1)}), bf16[128,3,2048]{2,1,0:T(4,128)(2,1)}, u32[]{:S(2)}, u32[]{:S(2)}) async-start(bf16[128,3,2048]{2,1,0:T(4,128)(2,1)} %reshape.382), calls=%async_computation.3 | async-start | bytes 4194304 | tf_op jit(solution)/shard_map/all_to_all | solution.py:315
Sparse Core Ops, SparseCore 0:
  11.0 65.7 all-gather.1

commit v7 on v6

--- a/solution.py
+++ b/solution.py
@@ -143,6 +143,27 @@
         ],
         compiler_params=pltpu.CompilerParams(collective_id=3, has_side_effects=True),
     )(x)
+
+
+def pack_kernel(gate_ref, up_ref, out_ref):
+    half = gate_ref.shape[2] // 2
+    for expert in range(gate_ref.shape[0]):
+        for half_id in range(2):
+            columns = slice(half_id * half, (half_id + 1) * half)
+            out_ref[2 * expert + half_id, :, :half] = gate_ref[expert, :, columns].astype(out_ref.dtype)
+            out_ref[2 * expert + half_id, :, half:] = up_ref[expert, :, columns].astype(out_ref.dtype)
+
+
+def pack_halves(gate, up, step_experts=8):
+    expert_count, rows_here, hidden_units = gate.shape
+    block = (step_experts, rows_here, hidden_units)
+    return pl.pallas_call(
+        pack_kernel,
+        out_shape=jax.ShapeDtypeStruct((2 * expert_count, rows_here, hidden_units), jnp.bfloat16),
+        grid=(expert_count // step_experts,),
+        in_specs=[pl.BlockSpec(block, lambda i: (i, 0, 0))] * 2,
+        out_specs=pl.BlockSpec((2 * step_experts, rows_here, hidden_units), lambda i: (i, 0, 0)),
+    )(gate, up)
 
 
 def body(
@@ -181,13 +202,7 @@
     server_out = gather_columns(out_weight.astype(jnp.bfloat16), req_count)
     expert_count, rows_here, hidden_units = gate_weight.shape
     half_units = hidden_units // 2
-    packed = jnp.concatenate(
-        [
-            split_halves(gate_weight.astype(jnp.bfloat16)),
-            split_halves(up_weight.astype(jnp.bfloat16)),
-        ],
-        axis=3,
-    ).reshape(2 * expert_count, rows_here, hidden_units)
+    packed = pack_halves(gate_weight, up_weight)
     packed, server_out = lax.optimization_barrier((packed, server_out))
     server_gate_up = lax.all_to_all(packed, ("req", "tp"), split_axis=0, concat_axis=1, tiled=True)
     group_rows, model_width = tokens.shape
@@ -275,7 +290,6 @@
     shard_rows = routes.shape[0]
     row_start = lane_index * shard_rows
     head_terms = jnp.dot(attended, server_out, preferred_element_type=jnp.float32)
-    server_gate_up, head_terms = lax.optimization_barrier((server_gate_up, head_terms))
     mixed_own = scatter_sum(head_terms, lax.axis_size("tp"))
     residual_own = lax.dynamic_slice_in_dim(tokens_f32, row_start, shard_rows, 0) + mixed_own
     moe_own = rms_scale(residual_own, moe_gain).astype(jnp.bfloat16)
@@ -303,6 +317,7 @@
         outgoing_rows.reshape(expert_count, 1, slot_depth, model_width),
         (expert_count, 2, slot_depth, model_width),
     ).reshape(2 * expert_count, slot_depth, model_width)
+    server_gate_up, send_rows = lax.optimization_barrier((server_gate_up, send_rows))
     arrived_rows = lax.all_to_all(send_rows, ("req", "tp"), split_axis=0, concat_axis=0, tiled=True)
     flat_rows = arrived_rows.reshape(-1, model_width)
     both = jnp.dot(flat_rows, server_gate_up[0], preferred_element_type=jnp.float32)

time: 327 us -> 325 us (level)
  Pallas kernels: 57.8 us -> 107 us
  waiting for transfers between devices: 46.1 us -> 23.4 us
  other arithmetic: 48.2 us -> 29.9 us
  local copies, waits for them, and re-layouts: 82.6 us -> 67.1 us
  blocking collectives: 33 us -> 38.6 us
    pallas_call x1, Pallas kernels: 34.4 us -> 66.6 us  [gather_columns(): pl.pallas_call(functools.partial(gather_kernel, count), out_shape=jax.Sha...]
    all_to_all x1, waiting for transfers between devices: 22.7 us -> 0.01 us  [body(): lax.all_to_all(packed, ('req', 'tp'), split_axis=0, concat_axis=1, tiled=...]
    concatenate x1 -> x0, other arithmetic: 10.6 us -> none  [body(): jnp.concatenate([split_halves(gate_weight.astype(jnp.bfloat16)), split_ha...]
    pallas_call x1, Pallas kernels: 23.4 us -> 32.7 us  [scatter_sum(): pl.pallas_call(functools.partial(scatter_sum_kernel, parts), out_shape=ja...]
    reshape x3 -> x0, local copies, waits for them, and re-layouts: 9.14 us -> none  [the longest x2 9.05 us: split_halves(): weights.reshape(expert_count, rows_here, 2, hidden_units // 2)]
    convert_element_type x2 -> x0, other arithmetic: 7.75 us -> none  [the longest x1 3.88 us: body(): up_weight.astype(jnp.bfloat16)]
    pallas_call x0 -> x1, Pallas kernels: none -> 7.58 us  [pack_halves(): pl.pallas_call(pack_kernel, out_shape=jax.ShapeDtypeStruct((2 * expert_co...]
    concatenate x1 -> x0, local copies, waits for them, and re-layouts: 5.66 us -> none  [body(): jnp.concatenate([split_halves(gate_weight.astype(jnp.bfloat16)), split_ha...]
  transfers between devices with their start and end apart: 4 -> 4, of which waited for: 2 -> 1; matrix products, arithmetic and copies ran while one was open for 28% -> 20% of each run, Pallas kernels for 11% -> 33%
where the time goes in v7:
time: 325 us; the launch traced here: 323 us
  Pallas kernels  107 us (33%)
  local copies, waits for them, and re-layouts  67.1 us (21%)
  blocking collectives  38.6 us (12%)
  other arithmetic  29.9 us (9%)
  starting transfers between devices  28.4 us (9%)
  waiting for transfers between devices  23.4 us (7%)
  matrix products  14.7 us (5%)
  between operations  14.5 us (4%)
    pallas_call x1, Pallas kernels, gather_columns(): pl.pallas_call(functools.partial(gather_kernel, count), out_shape=jax.Sha...  66.6 us
    all_to_all x1, blocking collectives, body(): lax.all_to_all(send_rows, ('req', 'tp'), split_axis=0, concat_axis=0, til...  38.6 us
    pallas_call x1, Pallas kernels, scatter_sum(): pl.pallas_call(functools.partial(scatter_sum_kernel, parts), out_shape=ja...  32.7 us
    all_to_all x1, waiting for transfers between devices, body(): lax.all_to_all(expert_rows, ('req', 'tp'), split_axis=0, concat_axis=0, t...  23.4 us
    gather x4, local copies, waits for them, and re-layouts, body(): jnp.take(arrived_pages.reshape((req_count * capacity,) + page_shape), own...  16.8 us
    all_to_all x1, starting transfers between devices, body(): lax.all_to_all(packed, ('req', 'tp'), split_axis=0, concat_axis=1, tiled=...  13.6 us
    unnamed x33, local copies, waits for them, and re-layouts  11.5 us
    gather x1, local copies, waits for them, and re-layouts, body(): jnp.take(page_store, send_slot.reshape(-1), axis=0)  10 us
  transfers between devices with their start and end apart: 4, of which 1 were waited for; matrix products, arithmetic and copies ran while one was open for 20% of the time, Pallas kernels for 33%

profile of v7, /device:TPU:1, one launch (start us, length us, event | category | flops | bytes accessed | tf_op | source)
XLA Modules:
  0.0 323.5 jit_solution(9264567406321147798)
XLA Ops:
  13.9 10.0 %gather_fusion = bf16[32,128,2,256]{3,2,1,0:T(2,128)(2,1)} fusion(bf16[8,128,2,256]{3,2,1,0:T(2,128)(2,1)S(1)} %copy-done.1, s32[1024]{0:T(1024)S(1)} %pad_clamp_fusion.2), kind=kCustom, calls=%fused_computation | custom fusion | bytes 8388736 | tf_op jit(solution)/shard_map/jit(_take)/gather | solution.py:251
  23.9 4.7 %copy_select_fusion = bf16[16,2,128,2,256]{4,2,3,1,0:T(8,128)(2,1)} fusion(bf16[16,2,128,2,256]{4,3,2,1,0:T(2,128)(2,1)} %bitcast.98, pred[16,2]{1,0:T(8,128)(4,1)S(1)} %copy.127), kind=kLoop, calls=%fused_computation.6 | loop fusion | flops 2097152 | bytes 8388640 | tf_op jit(solution)/shard_map/jit(_take)/select_n | solution.py:251
  28.7 8.1 %all-to-all-start.1 = ((bf16[16,2,128,2,256]{4,2,3,1,0:T(8,128)(2,1)}), bf16[16,2,128,2,256]{4,2,3,1,0:T(8,128)(2,1)}, u32[]{:S(2)}, u32[]{:S(2)}) async-start(bf16[16,2,128,2,256]{4,2,3,1,0:T(8,128)(2,1)} %copy_select_fusion), calls=%async_computation.1 | async-start | bytes 8388608 | tf_op jit(solution)/shard_map/all_to_all | solution.py:254
  38.9 66.6 %shard_map.219 = bf16[256,2048]{1,0:T(8,128)(2,1)} custom-call(bf16[256,128]{1,0:T(8,128)(2,1)} %convert_element_type.106.x_ref), custom_call_target="tpu_custom_call" | custom-call | tf_op jit(solution)/shard_map/pallas_call | solution.py:134
  106.7 7.6 %shard_map.218 = bf16[128,16,1024]{2,1,0:T(8,128)(2,1)} custom-call(f32[64,16,1024]{2,1,0:T(8,128)} %gate_ref.1, f32[64,16,1024]{2,1,0:T(8,128)} %up_ref.1), custom_call_target="tpu_custom_call" | custom-call | tf_op jit(solution)/shard_map/pallas_call | solution.py:160
  114.8 1.9 fusion.32
  116.8 1.9 compare_convert_fusion
  120.3 13.6 %all-to-all-start = ((bf16[128,16,1024]{2,1,0:T(8,128)(2,1)}), bf16[128,16,1024]{2,1,0:T(8,128)(2,1)}, u32[]{:S(2)}, u32[]{:S(2)}) async-start(bf16[128,16,1024]{2,1,0:T(8,128)(2,1)} %shard_map.218), calls=%async_computation | async-start | bytes 8388608 | tf_op jit(solution)/shard_map/all_to_all | solution.py:207
  133.9 4.2 %gather_fusion.1 = bf16[16,128,2,256]{3,1,2,0:T(8,128)(2,1)} fusion(bf16[32,128,2,256]{3,1,2,0:T(8,128)(2,1)} %bitcast.10, s32[1024]{0:T(1024)S(1)} %pad_clamp_fusion.1), kind=kCustom, calls=%fused_computation.1 | custom fusion | bytes 4194368 | tf_op jit(solution)/shard_map/jit(_take)/gather | solution.py:257
  138.1 4.5 %copy.130 = bf16[16,128,2,256]{1,0,3,2:T(8,128)(2,1)} copy(bf16[16,128,2,256]{3,1,2,0:T(8,128)(2,1)} %gather_fusion.1) | data formatting | bytes 4194304 | tf_op jit(solution)/shard_map/jit(_take)/gather | solution.py:257
  142.6 4.2 %gather.28 = bf16[2048,2,2,128]{0,3,2,1:T(8,128)(2,1)} reshape(bf16[16,128,2,256]{1,0,3,2:T(8,128)(2,1)} %copy.130) | data formatting | bytes 4194304 | tf_op jit(solution)/shard_map/jit(_take)/gather | solution.py:257
  146.8 4.0 %copy.131 = bf16[2048,2,2,128]{3,0,2,1:T(8,128)(2,1)} copy(bf16[2048,2,2,128]{0,3,2,1:T(8,128)(2,1)} %gather.28) | data formatting | bytes 4194304 | tf_op jit(solution)/shard_map/jit(_take)/gather | solution.py:257
  150.7 2.8 broadcast_select_fusion
  153.5 2.5 fusion.12
  160.5 1.3 fusion.43.x_ref
  161.8 32.7 %shard_map.220 = f32[16,2048]{1,0:T(8,128)} custom-call(f32[128,2048]{1,0:T(8,128)} %fusion.43.x_ref), custom_call_target="tpu_custom_call" | custom-call | tf_op jit(solution)/shard_map/pallas_call | solution.py:85
  195.6 1.3 convolution_convert_fusion.1
  196.9 3.3 %broadcast_in_dim.141 = bf16[64,3,2048]{2,1,0:T(4,128)(2,1)} reshape(bf16[192,2048]{1,0:T(8,128)(2,1)} %convolution_convert_fusion.1) | data formatting | bytes 1572864 | tf_op jit(solution)/shard_map/broadcast_in_dim | solution.py:316
  200.2 2.5 broadcast_in_dim.142
  202.7 38.6 %all_to_all.27 = bf16[128,3,2048]{2,1,0:T(4,128)(2,1)} all-to-all(bf16[128,3,2048]{2,1,0:T(4,128)(2,1)S(1)} %bitcast.99), channel_id=1, replica_groups=mesh['req'=16,'tp'=8] {'req','tp'}, dimensions={0} | all-to-all | bytes 3145728 | tf_op jit(solution)/shard_map/all_to_all | solution.py:321
  241.3 5.0 %reshape.366 = bf16[384,2048]{1,0:T(8,128)(2,1)} reshape(bf16[128,3,2048]{2,1,0:T(4,128)(2,1)} %all_to_all.27) | data formatting | bytes 3145728 | tf_op jit(solution)/shard_map/reshape | solution.py:322
  246.3 4.4 %fusion = f32[384,1024]{1,0:T(8,128)S(1)} fusion(bf16[384,2048]{1,0:T(8,128)(2,1)} %reshape.366, bf16[1,2048,1024]{2,1,0:T(8,128)(2,1)} %bitcast), kind=kOutput, calls=%fused_computation.4 | convolution fusion | flops 1610612736 | bytes 7340032 | tf_op jit(solution)/shard_map/dot_general | solution.py:323
  250.8 2.2 convolution_convert_fusion
  252.9 5.2 %reshape.367 = bf16[128,3,2048]{2,1,0:T(4,128)(2,1)} reshape(bf16[384,2048]{1,0:T(8,128)(2,1)} %convolution_convert_fusion) | data formatting | bytes 3145728 | tf_op jit(solution)/shard_map/reshape | solution.py:328
  258.1 6.6 %all-to-all-start.3 = ((bf16[128,3,2048]{2,1,0:T(4,128)(2,1)}), bf16[128,3,2048]{2,1,0:T(4,128)(2,1)}, u32[]{:S(2)}, u32[]{:S(2)}) async-start(bf16[128,3,2048]{2,1,0:T(4,128)(2,1)} %reshape.367), calls=%async_computation.3 | async-start | bytes 4194304 | tf_op jit(solution)/shard_map/all_to_all | solution.py:330
  269.8 23.4 %all-to-all-done.3 = bf16[128,3,2048]{2,1,0:T(4,128)(2,1)} async-done(((bf16[128,3,2048]{2,1,0:T(4,128)(2,1)}), bf16[128,3,2048]{2,1,0:T(4,128)(2,1)}, u32[]{:S(2)}, u32[]{:S(2)}) %all-to-all-start.3) | async-done | bytes 1572896 | tf_op jit(solution)/shard_map/all_to_all | solution.py:330
  293.2 3.7 %convert_add_fusion = f32[64,1,3,2048]{3,2,0,1:T(4,128)} fusion(bf16[64,2,3,2048]{3,2,1,0:T(4,128)(2,1)} %bitcast.18), kind=kLoop, calls=%fused_computation.13 | loop fusion | flops 1179648 | bytes 3145728 | tf_op jit(solution)/shard_map/add | solution.py:332
  296.9 3.8 %add.188 = f32[192,2048]{1,0:T(8,128)} reshape(f32[64,1,3,2048]{3,2,0,1:T(4,128)} %convert_add_fusion) | data formatting | bytes 3145728 | tf_op jit(solution)/shard_map/add | solution.py:332
  300.6 3.8 %gather_fusion.2 = f32[128,2048]{1,0:T(8,128)} fusion(f32[192,2048]{1,0:T(8,128)} %add.188, s32[1024]{0:T(1024)S(1)} %pad_clamp_fusion), kind=kCustom, calls=%fused_computation.2 | custom fusion | bytes 2097664 | tf_op jit(solution)/shard_map/jit(_take)/gather | solution.py:335
  304.4 2.2 fusion.10
  307.3 3.8 %copy.157 = bf16[2048,768]{1,0:T(8,128)(2,1)} copy(bf16[2048,768]{1,0:T(8,128)(2,1)} %all-gather.2.cloned.1.call-done) | data formatting | bytes 6291456
  312.0 4.6 %copy.159 = bf16[1,2048,1024]{2,1,0:T(8,128)(2,1)} copy(bf16[1,2048,1024]{2,1,0:T(8,128)(2,1)} %bitcast) | data formatting | bytes 8388608
  (115 shorter events, 24.0 us)
Async XLA Ops:
  7.2 243.6 %copy-start = (bf16[1,512,2048]{2,1,0:T(8,128)(2,1)S(1)}, bf16[1,512,2048]{2,1,0:T(8,128)(2,1)}, u32[]{:S(2)}) copy-start(bf16[1,512,2048]{2,1,0:T(8,128)(2,1)} %param.32) | copy-start | bytes 6291460
  7.2 6.7 %copy-start.1 = (bf16[8,128,2,256]{3,2,1,0:T(2,128)(2,1)S(1)}, bf16[8,128,2,256]{3,2,1,0:T(2,128)(2,1)}, u32[]{:S(2)}) copy-start(bf16[8,128,2,256]{3,2,1,0:T(2,128)(2,1)} %param.34) | copy-start | bytes 3145732
  7.2 146.3 %all-gather.2.cloned.1.call-start = ((), (), s32[]{:S(2)}) async-start(), calls=%async_computation.4 | async-start | bytes 3342336 | tf_op jit(solution)/shard_map/all_gather | solution.py:201
  28.6 8.1 %copy-start.12 = (s32[32]{0:T(128)S(1)}, s32[32]{0:T(128)}, u32[]{:S(2)}) copy-start(s32[32]{0:T(128)} %param.35) | copy-start | bytes 388
  28.6 8.7 %copy-start.13 = (s32[32]{0:T(128)S(1)}, s32[32]{0:T(128)}, u32[]{:S(2)}) copy-start(s32[32]{0:T(128)} %param.36) | copy-start | bytes 388
  28.6 8.8 %copy-start.6 = (s32[16,8]{0,1:T(8,128)S(1)}, s32[16,8]{0,1:T(8,128)}, u32[]{:S(2)}) copy-start(s32[16,8]{0,1:T(8,128)} %param.39) | copy-start | bytes 1540
  28.6 9.6 %copy-start.7 = (f32[256,128]{1,0:T(8,128)S(1)}, f32[256,128]{1,0:T(8,128)}, u32[]{:S(2)}) copy-start(f32[256,128]{1,0:T(8,128)} %param.29) | copy-start | bytes 393220
  28.7 76.9 %copy-start.3 = (bf16[128,2048]{1,0:T(8,128)(2,1)S(1)}, bf16[128,2048]{1,0:T(8,128)(2,1)}, u32[]{:S(2)}) copy-start(bf16[128,2048]{1,0:T(8,128)(2,1)} %param.21) | copy-start | bytes 1572868
  28.7 91.6 %all-to-all-start.1 = ((bf16[16,2,128,2,256]{4,2,3,1,0:T(8,128)(2,1)}), bf16[16,2,128,2,256]{4,2,3,1,0:T(8,128)(2,1)}, u32[]{:S(2)}, u32[]{:S(2)}) async-start(bf16[16,2,128,2,256]{4,2,3,1,0:T(8,128)(2,1)} %copy_select_fusion), calls=%async_computation.1 | async-start | bytes 8388608 | tf_op jit(solution)/shard_map/all_to_all | solution.py:254
  120.3 79.9 %all-to-all-start = ((bf16[128,16,1024]{2,1,0:T(8,128)(2,1)}), bf16[128,16,1024]{2,1,0:T(8,128)(2,1)}, u32[]{:S(2)}, u32[]{:S(2)}) async-start(bf16[128,16,1024]{2,1,0:T(8,128)(2,1)} %shard_map.218), calls=%async_computation | async-start | bytes 8388608 | tf_op jit(solution)/shard_map/all_to_all | solution.py:207
  150.7 2.8 copy-start.9
  153.5 3.5 %copy-start.10 = (f32[128]{0:T(128)S(1)}, f32[128]{0:T(128)}, u32[]{:S(2)}) copy-start(f32[128]{0:T(128)} %param.24) | copy-start | bytes 1540
  153.5 3.5 %copy-start.11 = (f32[128]{0:T(128)S(1)}, f32[128]{0:T(128)}, u32[]{:S(2)}) copy-start(f32[128]{0:T(128)} %param.23) | copy-start | bytes 1540
  156.1 1.7 copy-start.5
  157.0 1.6 copy-start.4
  159.3 1.2 copy-start.2
  159.9 35.7 %copy-start.8 = (f32[2048]{0:T(1024)S(1)}, f32[2048]{0:T(1024)}, u32[]{:S(2)}) copy-start(f32[2048]{0:T(1024)} %param.25) | copy-start | bytes 24580
  258.1 35.1 %all-to-all-start.3 = ((bf16[128,3,2048]{2,1,0:T(4,128)(2,1)}), bf16[128,3,2048]{2,1,0:T(4,128)(2,1)}, u32[]{:S(2)}, u32[]{:S(2)}) async-start(bf16[128,3,2048]{2,1,0:T(4,128)(2,1)} %reshape.367), calls=%async_computation.3 | async-start | bytes 4194304 | tf_op jit(solution)/shard_map/all_to_all | solution.py:330
Sparse Core Ops, SparseCore 0:
  11.0 65.7 all-gather.1

commit v8 on v5

--- a/solution.py
+++ b/solution.py
@@ -93,6 +93,24 @@
             pltpu.SemaphoreType.DMA((parts,)),
         ],
         compiler_params=pltpu.CompilerParams(collective_id=0, has_side_effects=True),
+    )(x)
+
+
+def copy_kernel(x_ref, o_ref):
+    o_ref[...] = x_ref[...]
+
+
+def copy_rows(x, steps):
+    rows = x.shape[0] // steps
+    block = (rows,) + x.shape[1:]
+    index = lambda i: (i,) + (0,) * (x.ndim - 1)
+    return pl.pallas_call(
+        copy_kernel,
+        out_shape=jax.ShapeDtypeStruct(x.shape, x.dtype),
+        grid=(steps,),
+        in_specs=[pl.BlockSpec(block, index)],
+        out_specs=pl.BlockSpec(block, index),
+        cost_estimate=pl.CostEstimate(flops=0, transcendentals=0, bytes_accessed=2 * x.size * x.dtype.itemsize),
     )(x)
 
 
@@ -226,6 +244,8 @@
     attended = attended.astype(jnp.bfloat16).reshape(group_rows, lane_width)
     shard_rows = routes.shape[0]
     row_start = lane_index * shard_rows
+    qkv_out = copy_rows(server_qkv, 4)
+    qkv_out, attended = lax.optimization_barrier((qkv_out, attended))
     head_terms = jnp.dot(attended, server_out, preferred_element_type=jnp.float32)
     server_gate_up, head_terms = lax.optimization_barrier((server_gate_up, head_terms))
     mixed_own = scatter_sum(head_terms, lax.axis_size("tp"))
@@ -274,7 +294,8 @@
     )
     moe_out = jnp.sum(picked_rows * entry_gates[:, :, None], axis=1)
     hidden_rows = (residual_own + moe_out).astype(jnp.bfloat16)
-    return (server_qkv, server_out, server_gate_up, hidden_rows, new_cache)
+    gate_up_out = copy_rows(server_gate_up.reshape(server_gate_up.shape[1:]), 4).reshape(server_gate_up.shape)
+    return (qkv_out, copy_rows(server_out, 1), gate_up_out, hidden_rows, new_cache)
 
 
 def solution(mesh):

time: 305 us -> 296 us (0.970)
  waiting for transfers between devices: 63.6 us -> 49 us
  Pallas kernels: 24 us -> 35.5 us
  local copies, waits for them, and re-layouts: 79.3 us -> 69.8 us
  matrix products: 14.9 us -> 18.1 us
    pallas_call x0 -> x3, Pallas kernels: none -> 11.2 us  [copy_rows(): pl.pallas_call(copy_kernel, out_shape=jax.ShapeDtypeStruct(x.shape, x.dty...]
    unnamed x35 -> x30, local copies, waits for them, and re-layouts: 11.9 us -> 2.5 us
    all_gather x1, waiting for transfers between devices: 22.4 us -> 14.9 us  [body(): lax.all_gather(out_weight.astype(jnp.bfloat16), 'req', axis=1, tiled=True)]
    all_to_all x1, waiting for transfers between devices: 24.3 us -> 17.3 us  [body(): lax.all_to_all(expert_rows, ('req', 'tp'), split_axis=0, concat_axis=0, t...]
  transfers between devices with their start and end apart: 5 -> 5, of which waited for: 4 -> 3; matrix products, arithmetic and copies ran while one was open for 30% -> 32% of each run, Pallas kernels for 0% -> 4%
where the time goes in v8:
time: 296 us; the launch traced here: 294 us
  local copies, waits for them, and re-layouts  69.8 us (24%)
  waiting for transfers between devices  49 us (17%)
  other arithmetic  47.2 us (16%)
  blocking collectives  36.8 us (12%)
  Pallas kernels  35.5 us (12%)
  starting transfers between devices  22.8 us (8%)
  matrix products  18.1 us (6%)
  between operations  14.5 us (5%)
    all_to_all x1, blocking collectives, body(): lax.all_to_all(send_rows, ('req', 'tp'), split_axis=0, concat_axis=0, til...  36.8 us
    pallas_call x1, Pallas kernels, scatter_sum(): pl.pallas_call(functools.partial(scatter_sum_kernel, parts), out_shape=ja...  24.3 us
    all_to_all x1, waiting for transfers between devices, body(): lax.all_to_all(expert_rows, ('req', 'tp'), split_axis=0, concat_axis=0, t...  17.3 us
    gather x4, local copies, waits for them, and re-layouts, body(): jnp.take(arrived_pages.reshape((req_count * capacity,) + page_shape), own...  16.8 us
    all_to_all x1, waiting for transfers between devices, body(): lax.all_to_all(outgoing_pages, 'req', split_axis=0, concat_axis=0, tiled=...  16.6 us
    all_gather x1, waiting for transfers between devices, body(): lax.all_gather(out_weight.astype(jnp.bfloat16), 'req', axis=1, tiled=True)  14.9 us
    pallas_call x3, Pallas kernels, copy_rows(): pl.pallas_call(copy_kernel, out_shape=jax.ShapeDtypeStruct(x.shape, x.dty...  11.2 us
    concatenate x1, other arithmetic, body(): jnp.concatenate([split_halves(gate_weight.astype(jnp.bfloat16)), split_ha...  10.6 us
  transfers between devices with their start and end apart: 5, of which 3 were waited for; matrix products, arithmetic and copies ran while one was open for 32% of the time, Pallas kernels for 4%

profile of v8, /device:TPU:1, one launch (start us, length us, event | category | flops | bytes accessed | tf_op | source)
XLA Modules:
  0.0 293.7 jit_solution(12909395600294539457)
XLA Ops:
  13.9 10.1 %gather_fusion = bf16[32,128,2,256]{3,2,1,0:T(2,128)(2,1)} fusion(bf16[8,128,2,256]{3,2,1,0:T(2,128)(2,1)S(1)} %copy-done.1, s32[1024]{0:T(1024)S(1)} %pad_clamp_fusion.2), kind=kCustom, calls=%fused_computation | custom fusion | bytes 8388736 | tf_op jit(solution)/shard_map/jit(_take)/gather | solution.py:206
  24.0 4.8 %copy_select_fusion = bf16[16,2,128,2,256]{4,2,3,1,0:T(8,128)(2,1)} fusion(bf16[16,2,128,2,256]{4,3,2,1,0:T(2,128)(2,1)} %bitcast.102, pred[16,2]{1,0:T(8,128)(4,1)S(1)} %copy.129), kind=kLoop, calls=%fused_computation.5 | loop fusion | flops 2097152 | bytes 8388640 | tf_op jit(solution)/shard_map/jit(_take)/select_n | solution.py:206
  28.8 8.0 %all-to-all-start = ((bf16[16,2,128,2,256]{4,2,3,1,0:T(8,128)(2,1)}), bf16[16,2,128,2,256]{4,2,3,1,0:T(8,128)(2,1)}, u32[]{:S(2)}, u32[]{:S(2)}) async-start(bf16[16,2,128,2,256]{4,2,3,1,0:T(8,128)(2,1)} %copy_select_fusion), calls=%async_computation | async-start | bytes 8388608 | tf_op jit(solution)/shard_map/all_to_all | solution.py:209
  38.2 3.9 %convert_element_type.123 = bf16[64,16,1024]{2,1,0:T(8,128)(2,1)} convert(f32[64,16,1024]{2,1,0:T(8,128)} %param.30) | non-fusion elementwise | flops 1048576 | bytes 6291456 | tf_op jit(solution)/shard_map/convert_element_type | solution.py:157
  42.1 4.5 %reshape.382 = bf16[64,16,2,512]{3,2,1,0:T(2,128)(2,1)} reshape(bf16[64,16,1024]{2,1,0:T(8,128)(2,1)} %convert_element_type.123) | data formatting | bytes 4194304 | tf_op jit(solution)/shard_map/reshape | solution.py:38
  46.6 3.9 %convert_element_type.124 = bf16[64,16,1024]{2,1,0:T(8,128)(2,1)} convert(f32[64,16,1024]{2,1,0:T(8,128)} %param.31) | non-fusion elementwise | flops 1048576 | bytes 6291456 | tf_op jit(solution)/shard_map/convert_element_type | solution.py:158
  50.5 4.5 %reshape.383 = bf16[64,16,2,512]{3,2,1,0:T(2,128)(2,1)} reshape(bf16[64,16,1024]{2,1,0:T(8,128)(2,1)} %convert_element_type.124) | data formatting | bytes 4194304 | tf_op jit(solution)/shard_map/reshape | solution.py:38
  55.0 10.6 %pad_maximum_fusion = bf16[64,2,16,1024]{3,1,2,0:T(2,128)(2,1)} fusion(bf16[64,2,16,512]{3,1,2,0:T(2,128)(2,1)} %bitcast.106, bf16[64,2,16,512]{3,1,2,0:T(2,128)(2,1)} %bitcast.105), kind=kLoop, calls=%fused_computation.4 | loop fusion | flops 8388608 | bytes 8388608 | tf_op jit(solution)/shard_map/concatenate | solution.py:155
  65.6 5.6 %copy.137 = bf16[64,2,16,1024]{3,2,1,0:T(8,128)(2,1)} copy(bf16[64,2,16,1024]{3,1,2,0:T(2,128)(2,1)} %pad_maximum_fusion) | data formatting | bytes 8388608 | tf_op jit(solution)/shard_map/concatenate | solution.py:155
  79.3 16.6 %all-to-all-done = bf16[16,2,128,2,256]{4,2,3,1,0:T(8,128)(2,1)} async-done(((bf16[16,2,128,2,256]{4,2,3,1,0:T(8,128)(2,1)}), bf16[16,2,128,2,256]{4,2,3,1,0:T(8,128)(2,1)}, u32[]{:S(2)}, u32[]{:S(2)}) %all-to-all-start) | async-done | bytes 4194336 | tf_op jit(solution)/shard_map/all_to_all | solution.py:209
  95.8 8.1 %all-to-all-start.1 = ((bf16[128,16,1024]{2,1,0:T(8,128)(2,1)}), bf16[128,16,1024]{2,1,0:T(8,128)(2,1)}, u32[]{:S(2)}, u32[]{:S(2)}) async-start(bf16[128,16,1024]{2,1,0:T(8,128)(2,1)} %bitcast.103), calls=%async_computation.1 | async-start | bytes 8388608 | tf_op jit(solution)/shard_map/all_to_all | solution.py:162
  103.9 4.2 %gather_fusion.1 = bf16[16,128,2,256]{3,1,2,0:T(8,128)(2,1)} fusion(bf16[32,128,2,256]{3,1,2,0:T(8,128)(2,1)} %bitcast.9, s32[1024]{0:T(1024)S(1)} %pad_clamp_fusion.1), kind=kCustom, calls=%fused_computation.1 | custom fusion | bytes 4194368 | tf_op jit(solution)/shard_map/jit(_take)/gather | solution.py:212
  108.1 4.5 %copy.132 = bf16[16,128,2,256]{1,0,3,2:T(8,128)(2,1)} copy(bf16[16,128,2,256]{3,1,2,0:T(8,128)(2,1)} %gather_fusion.1) | data formatting | bytes 4194304 | tf_op jit(solution)/shard_map/jit(_take)/gather | solution.py:212
  112.6 4.2 %gather.28 = bf16[2048,2,2,128]{0,3,2,1:T(8,128)(2,1)} reshape(bf16[16,128,2,256]{1,0,3,2:T(8,128)(2,1)} %copy.132) | data formatting | bytes 4194304 | tf_op jit(solution)/shard_map/jit(_take)/gather | solution.py:212
  116.8 3.9 %copy.133 = bf16[2048,2,2,128]{3,0,2,1:T(8,128)(2,1)} copy(bf16[2048,2,2,128]{0,3,2,1:T(8,128)(2,1)} %gather.28) | data formatting | bytes 4194304 | tf_op jit(solution)/shard_map/jit(_take)/gather | solution.py:212
  120.7 2.8 broadcast_select_fusion
  123.5 2.5 fusion.10
  131.3 4.2 %shard_map.218 = bf16[2048,768]{1,0:T(8,128)(2,1)} custom-call(bf16[2048,768]{1,0:T(8,128)(2,1)} %all-gather.3.cloned.1.call-done.x_ref), custom_call_target="tpu_custom_call" | custom-call | bytes 6291456 | tf_op jit(solution)/shard_map/pallas_call | solution.py:107
  135.5 2.5 fusion.6
  138.2 14.9 %all-gather.5.cloned.1.call-done.x_ref = bf16[256,2048]{1,0:T(8,128)(2,1)} async-done(((bf16[256,128]{1,0:T(8,128)(2,1)}), bf16[256,2048]{1,0:T(8,128)(2,1)}) %all-gather.5.cloned.1.call-update) | async-done | bytes 1048592 | tf_op jit(solution)/shard_map/all_gather | solution.py:151
  153.1 2.5 fusion.43.x_ref
  155.7 24.3 %shard_map.221 = f32[16,2048]{1,0:T(8,128)} custom-call(f32[128,2048]{1,0:T(8,128)} %fusion.43.x_ref), custom_call_target="tpu_custom_call" | custom-call | tf_op jit(solution)/shard_map/pallas_call | solution.py:85
  186.1 36.8 %all_to_all.27 = bf16[128,3,2048]{2,1,0:T(4,128)(2,1)} all-to-all(bf16[128,3,2048]{2,1,0:T(4,128)(2,1)S(1)} %bitcast.104), channel_id=1, replica_groups=mesh['req'=16,'tp'=8] {'req','tp'}, dimensions={0} | all-to-all | bytes 3145728 | tf_op jit(solution)/shard_map/all_to_all | solution.py:278
  222.9 5.0 %reshape.389 = bf16[384,2048]{1,0:T(8,128)(2,1)} reshape(bf16[128,3,2048]{2,1,0:T(4,128)(2,1)} %all_to_all.27) | data formatting | bytes 3145728 | tf_op jit(solution)/shard_map/reshape | solution.py:279
  228.0 4.4 %fusion.34 = f32[384,1024]{1,0:T(8,128)S(1)} fusion(bf16[384,2048]{1,0:T(8,128)(2,1)} %reshape.389, bf16[1,2048,1024]{2,1,0:T(8,128)(2,1)} %bitcast.17), kind=kOutput, calls=%fused_computation.116 | convolution fusion | flops 1610612736 | bytes 7340032 | tf_op jit(solution)/shard_map/dot_general | solution.py:280
  234.6 5.2 %reshape.390 = bf16[128,3,2048]{2,1,0:T(4,128)(2,1)} reshape(bf16[384,2048]{1,0:T(8,128)(2,1)} %convolution_convert_fusion) | data formatting | bytes 3145728 | tf_op jit(solution)/shard_map/reshape | solution.py:285
  239.8 6.6 %all-to-all-start.3 = ((bf16[128,3,2048]{2,1,0:T(4,128)(2,1)}), bf16[128,3,2048]{2,1,0:T(4,128)(2,1)}, u32[]{:S(2)}, u32[]{:S(2)}) async-start(bf16[128,3,2048]{2,1,0:T(4,128)(2,1)} %reshape.390), calls=%async_computation.3 | async-start | bytes 4194304 | tf_op jit(solution)/shard_map/all_to_all | solution.py:287
  251.0 4.7 %shard_map.220 = bf16[2048,1024]{1,0:T(8,128)(2,1)} custom-call(bf16[2048,1024]{1,0:T(8,128)(2,1)} %bitcast.18.x_ref), custom_call_target="tpu_custom_call" | custom-call | bytes 8388608 | tf_op jit(solution)/shard_map/pallas_call | solution.py:107
  257.5 17.3 %all-to-all-done.3 = bf16[128,3,2048]{2,1,0:T(4,128)(2,1)} async-done(((bf16[128,3,2048]{2,1,0:T(4,128)(2,1)}), bf16[128,3,2048]{2,1,0:T(4,128)(2,1)}, u32[]{:S(2)}, u32[]{:S(2)}) %all-to-all-start.3) | async-done | bytes 1572896 | tf_op jit(solution)/shard_map/all_to_all | solution.py:287
  274.9 3.8 %convert_add_fusion = f32[64,1,3,2048]{3,2,0,1:T(4,128)} fusion(bf16[64,2,3,2048]{3,2,1,0:T(4,128)(2,1)} %bitcast.22), kind=kLoop, calls=%fused_computation.12 | loop fusion | flops 1179648 | bytes 3145728 | tf_op jit(solution)/shard_map/add | solution.py:289
  278.6 3.8 %add.188 = f32[192,2048]{1,0:T(8,128)} reshape(f32[64,1,3,2048]{3,2,0,1:T(4,128)} %convert_add_fusion) | data formatting | bytes 3145728 | tf_op jit(solution)/shard_map/add | solution.py:289
  282.4 2.9 gather_fusion.2
  (122 shorter events, 37.6 us)
Async XLA Ops:
  7.2 225.3 %copy-start = (bf16[1,512,2048]{2,1,0:T(8,128)(2,1)S(1)}, bf16[1,512,2048]{2,1,0:T(8,128)(2,1)}, u32[]{:S(2)}) copy-start(bf16[1,512,2048]{2,1,0:T(8,128)(2,1)} %param.32) | copy-start | bytes 6291460
  7.2 6.7 %copy-start.1 = (bf16[8,128,2,256]{3,2,1,0:T(2,128)(2,1)S(1)}, bf16[8,128,2,256]{3,2,1,0:T(2,128)(2,1)}, u32[]{:S(2)}) copy-start(bf16[8,128,2,256]{3,2,1,0:T(2,128)(2,1)} %param.34) | copy-start | bytes 3145732
  7.2 116.3 %all-gather.3.cloned.1.call-start = ((), (), s32[]{:S(2)}) async-start(), calls=%async_computation.4 | async-start | bytes 3342336 | tf_op jit(solution)/shard_map/all_gather | solution.py:150
  28.8 8.1 %copy-start.7 = (f32[256,128]{1,0:T(8,128)S(1)}, f32[256,128]{1,0:T(8,128)}, u32[]{:S(2)}) copy-start(f32[256,128]{1,0:T(8,128)} %param.29) | copy-start | bytes 393220
  28.8 8.8 %copy-start.12 = (s32[32]{0:T(128)S(1)}, s32[32]{0:T(128)}, u32[]{:S(2)}) copy-start(s32[32]{0:T(128)} %param.36) | copy-start | bytes 388
  28.8 8.9 %copy-start.13 = (s32[32]{0:T(128)S(1)}, s32[32]{0:T(128)}, u32[]{:S(2)}) copy-start(s32[32]{0:T(128)} %param.35) | copy-start | bytes 388
  28.8 67.1 %all-to-all-start = ((bf16[16,2,128,2,256]{4,2,3,1,0:T(8,128)(2,1)}), bf16[16,2,128,2,256]{4,2,3,1,0:T(8,128)(2,1)}, u32[]{:S(2)}, u32[]{:S(2)}) async-start(bf16[16,2,128,2,256]{4,2,3,1,0:T(8,128)(2,1)} %copy_select_fusion), calls=%async_computation | async-start | bytes 8388608 | tf_op jit(solution)/shard_map/all_to_all | solution.py:209
  36.8 116.3 %all-gather.5.cloned.1.call-start = ((), (), s32[]{:S(2)}) async-start(), calls=%async_computation.5 | async-start | bytes 1114112 | tf_op jit(solution)/shard_map/all_gather | solution.py:151
  65.6 5.6 %copy-start.2 = (bf16[128,2048]{1,0:T(8,128)(2,1)S(1)}, bf16[128,2048]{1,0:T(8,128)(2,1)}, u32[]{:S(2)}) copy-start(bf16[128,2048]{1,0:T(8,128)(2,1)} %param.21) | copy-start | bytes 1572868
  65.6 6.8 %copy-start.6 = (s32[16,8]{0,1:T(8,128)S(1)}, s32[16,8]{0,1:T(8,128)}, u32[]{:S(2)}) copy-start(s32[16,8]{0,1:T(8,128)} %param.39) | copy-start | bytes 1540
  95.8 59.9 %all-to-all-start.1 = ((bf16[128,16,1024]{2,1,0:T(8,128)(2,1)}), bf16[128,16,1024]{2,1,0:T(8,128)(2,1)}, u32[]{:S(2)}, u32[]{:S(2)}) async-start(bf16[128,16,1024]{2,1,0:T(8,128)(2,1)} %bitcast.103), calls=%async_computation.1 | async-start | bytes 8388608 | tf_op jit(solution)/shard_map/all_to_all | solution.py:162
  120.7 2.8 copy-start.9
  123.5 4.3 %copy-start.10 = (f32[128]{0:T(128)S(1)}, f32[128]{0:T(128)}, u32[]{:S(2)}) copy-start(f32[128]{0:T(128)} %param.24) | copy-start | bytes 1540
  123.5 4.3 %copy-start.11 = (f32[128]{0:T(128)S(1)}, f32[128]{0:T(128)}, u32[]{:S(2)}) copy-start(f32[128]{0:T(128)} %param.23) | copy-start | bytes 1540
  126.1 0.8 copy-start.4
  127.7 1.6 copy-start.3
  138.0 43.1 %copy-start.8 = (f32[2048]{0:T(1024)S(1)}, f32[2048]{0:T(1024)}, u32[]{:S(2)}) copy-start(f32[2048]{0:T(1024)} %param.25) | copy-start | bytes 24580
  239.8 35.1 %all-to-all-start.3 = ((bf16[128,3,2048]{2,1,0:T(4,128)(2,1)}), bf16[128,3,2048]{2,1,0:T(4,128)(2,1)}, u32[]{:S(2)}, u32[]{:S(2)}) async-start(bf16[128,3,2048]{2,1,0:T(4,128)(2,1)} %reshape.390), calls=%async_computation.3 | async-start | bytes 4194304 | tf_op jit(solution)/shard_map/all_to_all | solution.py:287
  246.4 2.8 copy-start.5
Sparse Core Ops, SparseCore 0:
  11.0 65.8 all-gather.2
  79.0 74.0 all-gather.4

commit v9 on v8

--- a/solution.py
+++ b/solution.py
@@ -285,14 +285,24 @@
         .reshape(arrived_rows.shape)
     )
     returned = lax.all_to_all(expert_rows, ("req", "tp"), split_axis=0, concat_axis=0, tiled=True)
-    returned = returned.reshape(expert_count, 2, slot_depth, model_width)
-    joined_out = (returned[:, 0].astype(jnp.float32) + returned[:, 1].astype(jnp.float32)).reshape(
-        expert_count * slot_depth, model_width
-    )
-    picked_rows = jnp.take(joined_out, entry_slot.reshape(-1), axis=0).reshape(
-        shard_rows, top_count, model_width
-    )
-    moe_out = jnp.sum(picked_rows * entry_gates[:, :, None], axis=1)
+    slot_weights = jnp.sum(
+        jnp.where(
+            entry_slot[:, :, None] == jnp.arange(expert_count * slot_depth, dtype=jnp.int32)[None, None, :],
+            entry_gates[:, :, None],
+            jnp.float32(0.0),
+        ),
+        axis=1,
+    ).reshape(shard_rows, expert_count, 1, slot_depth)
+    slot_weights = jnp.broadcast_to(
+        slot_weights, (shard_rows, expert_count, 2, slot_depth)
+    ).reshape(shard_rows, 2 * expert_count, slot_depth)
+    moe_out = jnp.einsum(
+        "ixk,xkd->id",
+        slot_weights,
+        returned.astype(jnp.float32),
+        precision=lax.Precision.HIGHEST,
+        preferred_element_type=jnp.float32,
+    )
     hidden_rows = (residual_own + moe_out).astype(jnp.bfloat16)
     gate_up_out = copy_rows(server_gate_up.reshape(server_gate_up.shape[1:]), 4).reshape(server_gate_up.shape)
     return (qkv_out, copy_rows(server_out, 1), gate_up_out, hidden_rows, new_cache)

time: 296 us -> 288 us (0.973)
  local copies, waits for them, and re-layouts: 69.8 us -> 63 us
  other arithmetic: 47.2 us -> 42 us
  matrix products: 18.1 us -> 22.6 us
    dot_general x0 -> x1, matrix products: none -> 4.49 us  [body(): jnp.einsum('ixk,xkd->id', slot_weights, returned.astype(jnp.float32), pre...]
    add x2 -> x0, local copies, waits for them, and re-layouts: 3.83 us -> none  [the longest x1 3.76 us: body(): returned[:, 0].astype(jnp.float32) + returned[:, 1].astype(jnp.float32)]
    add x1, other arithmetic: 3.76 us -> 0.01 us  [body(): flat_routes * slot_depth + entry_rank]
  transfers between devices with their start and end apart: 5 -> 5, of which waited for: 3 -> 4; matrix products, arithmetic and copies ran while one was open for 32% -> 33% of each run, Pallas kernels for 4% -> 4%
where the time goes in v9:
time: 288 us; the launch traced here: 286 us
  local copies, waits for them, and re-layouts  63 us (22%)
  waiting for transfers between devices  49.2 us (17%)
  other arithmetic  42 us (15%)
  blocking collectives  36.9 us (13%)
  Pallas kernels  35.4 us (12%)
  starting transfers between devices  22.8 us (8%)
  matrix products  22.6 us (8%)
  between operations  14.5 us (5%)
    all_to_all x1, blocking collectives, body(): lax.all_to_all(send_rows, ('req', 'tp'), split_axis=0, concat_axis=0, til...  36.9 us
    pallas_call x1, Pallas kernels, scatter_sum(): pl.pallas_call(functools.partial(scatter_sum_kernel, parts), out_shape=ja...  24.2 us
    all_to_all x1, waiting for transfers between devices, body(): lax.all_to_all(expert_rows, ('req', 'tp'), split_axis=0, concat_axis=0, t...  17.3 us
    gather x4, local copies, waits for them, and re-layouts, body(): jnp.take(arrived_pages.reshape((req_count * capacity,) + page_shape), own...  16.8 us
    all_to_all x1, waiting for transfers between devices, body(): lax.all_to_all(outgoing_pages, 'req', split_axis=0, concat_axis=0, tiled=...  16.8 us
    all_gather x1, waiting for transfers between devices, body(): lax.all_gather(out_weight.astype(jnp.bfloat16), 'req', axis=1, tiled=True)  15 us
    pallas_call x3, Pallas kernels, copy_rows(): pl.pallas_call(copy_kernel, out_shape=jax.ShapeDtypeStruct(x.shape, x.dty...  11.2 us
    concatenate x1, other arithmetic, body(): jnp.concatenate([split_halves(gate_weight.astype(jnp.bfloat16)), split_ha...  10.6 us
  transfers between devices with their start and end apart: 5, of which 4 were waited for; matrix products, arithmetic and copies ran while one was open for 33% of the time, Pallas kernels for 4%

profile of v9, /device:TPU:1, one launch (start us, length us, event | category | flops | bytes accessed | tf_op | source)
XLA Modules:
  0.0 286.4 jit_solution(4727154952488914655)
XLA Ops:
  13.9 10.1 %gather_fusion = bf16[32,128,2,256]{3,2,1,0:T(2,128)(2,1)} fusion(bf16[8,128,2,256]{3,2,1,0:T(2,128)(2,1)S(1)} %copy-done.1, s32[1024]{0:T(1024)S(1)} %pad_clamp_fusion.1), kind=kCustom, calls=%fused_computation | custom fusion | bytes 8388736 | tf_op jit(solution)/shard_map/jit(_take)/gather | solution.py:206
  24.0 4.8 %copy_select_fusion = bf16[16,2,128,2,256]{4,2,3,1,0:T(8,128)(2,1)} fusion(bf16[16,2,128,2,256]{4,3,2,1,0:T(2,128)(2,1)} %bitcast.89, pred[16,2]{1,0:T(8,128)(4,1)S(1)} %copy.123), kind=kLoop, calls=%fused_computation.4 | loop fusion | flops 2097152 | bytes 8388640 | tf_op jit(solution)/shard_map/jit(_take)/select_n | solution.py:206
  28.8 8.0 %all-to-all-start = ((bf16[16,2,128,2,256]{4,2,3,1,0:T(8,128)(2,1)}), bf16[16,2,128,2,256]{4,2,3,1,0:T(8,128)(2,1)}, u32[]{:S(2)}, u32[]{:S(2)}) async-start(bf16[16,2,128,2,256]{4,2,3,1,0:T(8,128)(2,1)} %copy_select_fusion), calls=%async_computation | async-start | bytes 8388608 | tf_op jit(solution)/shard_map/all_to_all | solution.py:209
  38.2 3.9 %convert_element_type.114 = bf16[64,16,1024]{2,1,0:T(8,128)(2,1)} convert(f32[64,16,1024]{2,1,0:T(8,128)} %param.30) | non-fusion elementwise | flops 1048576 | bytes 6291456 | tf_op jit(solution)/shard_map/convert_element_type | solution.py:157
  42.1 4.5 %reshape.340 = bf16[64,16,2,512]{3,2,1,0:T(2,128)(2,1)} reshape(bf16[64,16,1024]{2,1,0:T(8,128)(2,1)} %convert_element_type.114) | data formatting | bytes 4194304 | tf_op jit(solution)/shard_map/reshape | solution.py:38
  46.6 3.9 %convert_element_type.115 = bf16[64,16,1024]{2,1,0:T(8,128)(2,1)} convert(f32[64,16,1024]{2,1,0:T(8,128)} %param.31) | non-fusion elementwise | flops 1048576 | bytes 6291456 | tf_op jit(solution)/shard_map/convert_element_type | solution.py:158
  50.5 4.5 %reshape.341 = bf16[64,16,2,512]{3,2,1,0:T(2,128)(2,1)} reshape(bf16[64,16,1024]{2,1,0:T(8,128)(2,1)} %convert_element_type.115) | data formatting | bytes 4194304 | tf_op jit(solution)/shard_map/reshape | solution.py:38
  55.0 10.6 %pad_maximum_fusion = bf16[64,2,16,1024]{3,1,2,0:T(2,128)(2,1)} fusion(bf16[64,2,16,512]{3,1,2,0:T(2,128)(2,1)} %bitcast.93, bf16[64,2,16,512]{3,1,2,0:T(2,128)(2,1)} %bitcast.92), kind=kLoop, calls=%fused_computation.3 | loop fusion | flops 8388608 | bytes 8388608 | tf_op jit(solution)/shard_map/concatenate | solution.py:155
  65.6 5.6 %copy.131 = bf16[64,2,16,1024]{3,2,1,0:T(8,128)(2,1)} copy(bf16[64,2,16,1024]{3,1,2,0:T(2,128)(2,1)} %pad_maximum_fusion) | data formatting | bytes 8388608 | tf_op jit(solution)/shard_map/concatenate | solution.py:155
  79.1 16.8 %all-to-all-done = bf16[16,2,128,2,256]{4,2,3,1,0:T(8,128)(2,1)} async-done(((bf16[16,2,128,2,256]{4,2,3,1,0:T(8,128)(2,1)}), bf16[16,2,128,2,256]{4,2,3,1,0:T(8,128)(2,1)}, u32[]{:S(2)}, u32[]{:S(2)}) %all-to-all-start) | async-done | bytes 4194336 | tf_op jit(solution)/shard_map/all_to_all | solution.py:209
  95.9 8.1 %all-to-all-start.1 = ((bf16[128,16,1024]{2,1,0:T(8,128)(2,1)}), bf16[128,16,1024]{2,1,0:T(8,128)(2,1)}, u32[]{:S(2)}, u32[]{:S(2)}) async-start(bf16[128,16,1024]{2,1,0:T(8,128)(2,1)} %bitcast.90), calls=%async_computation.1 | async-start | bytes 8388608 | tf_op jit(solution)/shard_map/all_to_all | solution.py:162
  104.0 4.2 %gather_fusion.1 = bf16[16,128,2,256]{3,1,2,0:T(8,128)(2,1)} fusion(bf16[32,128,2,256]{3,1,2,0:T(8,128)(2,1)} %bitcast.9, s32[1024]{0:T(1024)S(1)} %pad_clamp_fusion), kind=kCustom, calls=%fused_computation.1 | custom fusion | bytes 4194368 | tf_op jit(solution)/shard_map/jit(_take)/gather | solution.py:212
  108.2 4.5 %copy.126 = bf16[16,128,2,256]{1,0,3,2:T(8,128)(2,1)} copy(bf16[16,128,2,256]{3,1,2,0:T(8,128)(2,1)} %gather_fusion.1) | data formatting | bytes 4194304 | tf_op jit(solution)/shard_map/jit(_take)/gather | solution.py:212
  112.7 4.2 %gather.22 = bf16[2048,2,2,128]{0,3,2,1:T(8,128)(2,1)} reshape(bf16[16,128,2,256]{1,0,3,2:T(8,128)(2,1)} %copy.126) | data formatting | bytes 4194304 | tf_op jit(solution)/shard_map/jit(_take)/gather | solution.py:212
  116.8 3.9 %copy.127 = bf16[2048,2,2,128]{3,0,2,1:T(8,128)(2,1)} copy(bf16[2048,2,2,128]{0,3,2,1:T(8,128)(2,1)} %gather.22) | data formatting | bytes 4194304 | tf_op jit(solution)/shard_map/jit(_take)/gather | solution.py:212
  120.8 2.8 broadcast_select_fusion
  123.5 2.5 fusion.11
  131.4 4.2 %shard_map.218 = bf16[2048,768]{1,0:T(8,128)(2,1)} custom-call(bf16[2048,768]{1,0:T(8,128)(2,1)} %all-gather.3.cloned.1.call-done.x_ref), custom_call_target="tpu_custom_call" | custom-call | bytes 6291456 | tf_op jit(solution)/shard_map/pallas_call | solution.py:107
  135.5 2.5 fusion.9
  138.2 15.0 %all-gather.5.cloned.1.call-done.x_ref = bf16[256,2048]{1,0:T(8,128)(2,1)} async-done(((bf16[256,128]{1,0:T(8,128)(2,1)}), bf16[256,2048]{1,0:T(8,128)(2,1)}) %all-gather.5.cloned.1.call-update) | async-done | bytes 1048592 | tf_op jit(solution)/shard_map/all_gather | solution.py:151
  153.2 2.5 fusion.41.x_ref
  155.8 24.2 %shard_map.221 = f32[16,2048]{1,0:T(8,128)} custom-call(f32[128,2048]{1,0:T(8,128)} %fusion.41.x_ref), custom_call_target="tpu_custom_call" | custom-call | tf_op jit(solution)/shard_map/pallas_call | solution.py:85
  182.5 2.4 broadcast_in_dim.156
  186.2 36.9 %all_to_all.27 = bf16[128,3,2048]{2,1,0:T(4,128)(2,1)} all-to-all(bf16[128,3,2048]{2,1,0:T(4,128)(2,1)S(1)} %bitcast.91), channel_id=1, replica_groups=mesh['req'=16,'tp'=8] {'req','tp'}, dimensions={0} | all-to-all | bytes 3145728 | tf_op jit(solution)/shard_map/all_to_all | solution.py:278
  223.1 5.0 %reshape.348 = bf16[384,2048]{1,0:T(8,128)(2,1)} reshape(bf16[128,3,2048]{2,1,0:T(4,128)(2,1)} %all_to_all.27) | data formatting | bytes 3145728 | tf_op jit(solution)/shard_map/reshape | solution.py:279
  228.1 4.4 %fusion.34 = f32[384,1024]{1,0:T(8,128)S(1)} fusion(bf16[384,2048]{1,0:T(8,128)(2,1)} %reshape.348, bf16[1,2048,1024]{2,1,0:T(8,128)(2,1)} %bitcast.17), kind=kOutput, calls=%fused_computation.108 | convolution fusion | flops 1610612736 | bytes 7340032 | tf_op jit(solution)/shard_map/dot_general | solution.py:280
  234.7 5.2 %reshape.349 = bf16[128,3,2048]{2,1,0:T(4,128)(2,1)} reshape(bf16[384,2048]{1,0:T(8,128)(2,1)} %convolution_convert_fusion) | data formatting | bytes 3145728 | tf_op jit(solution)/shard_map/reshape | solution.py:285
  239.9 6.6 %all-to-all-start.3 = ((bf16[128,3,2048]{2,1,0:T(4,128)(2,1)}), bf16[128,3,2048]{2,1,0:T(4,128)(2,1)}, u32[]{:S(2)}, u32[]{:S(2)}) async-start(bf16[128,3,2048]{2,1,0:T(4,128)(2,1)} %reshape.349), calls=%async_computation.3 | async-start | bytes 4194304 | tf_op jit(solution)/shard_map/all_to_all | solution.py:287
  246.7 2.3 shard_map.219
  251.2 4.7 %shard_map.220 = bf16[2048,1024]{1,0:T(8,128)(2,1)} custom-call(bf16[2048,1024]{1,0:T(8,128)(2,1)} %bitcast.18.x_ref), custom_call_target="tpu_custom_call" | custom-call | bytes 8388608 | tf_op jit(solution)/shard_map/pallas_call | solution.py:107
  257.7 17.3 %all-to-all-done.3 = bf16[128,3,2048]{2,1,0:T(4,128)(2,1)} async-done(((bf16[128,3,2048]{2,1,0:T(4,128)(2,1)}), bf16[128,3,2048]{2,1,0:T(4,128)(2,1)}, u32[]{:S(2)}, u32[]{:S(2)}) %all-to-all-start.3) | async-done | bytes 1572896 | tf_op jit(solution)/shard_map/all_to_all | solution.py:287
  275.1 4.5 %fusion.3 = bf16[16,2048]{1,0:T(8,128)(2,1)} fusion(f32[16,2048]{1,0:T(8,128)S(1)} %get-tuple-element.56, f32[16,128,3]{0,1,2:T(8,128)S(1)} %bitcast.95, bf16[128,3,2048]{2,1,0:T(4,128)(2,1)} %all-to-all-done.3), kind=kOutput, calls=%fused_computation.12 | convolution fusion | flops 151060480 | bytes 1794048 | tf_op jit(solution)/shard_map/ixk,xkd->id/dot_general | solution.py:299
  (115 shorter events, 31.3 us)
Async XLA Ops:
  7.2 225.4 %copy-start = (bf16[1,512,2048]{2,1,0:T(8,128)(2,1)S(1)}, bf16[1,512,2048]{2,1,0:T(8,128)(2,1)}, u32[]{:S(2)}) copy-start(bf16[1,512,2048]{2,1,0:T(8,128)(2,1)} %param.32) | copy-start | bytes 6291460
  7.2 6.7 %copy-start.1 = (bf16[8,128,2,256]{3,2,1,0:T(2,128)(2,1)S(1)}, bf16[8,128,2,256]{3,2,1,0:T(2,128)(2,1)}, u32[]{:S(2)}) copy-start(bf16[8,128,2,256]{3,2,1,0:T(2,128)(2,1)} %param.34) | copy-start | bytes 3145732
  7.2 116.3 %all-gather.3.cloned.1.call-start = ((), (), s32[]{:S(2)}) async-start(), calls=%async_computation.4 | async-start | bytes 3342336 | tf_op jit(solution)/shard_map/all_gather | solution.py:150
  28.8 8.1 %copy-start.6 = (f32[256,128]{1,0:T(8,128)S(1)}, f32[256,128]{1,0:T(8,128)}, u32[]{:S(2)}) copy-start(f32[256,128]{1,0:T(8,128)} %param.29) | copy-start | bytes 393220
  28.8 8.8 %copy-start.12 = (s32[32]{0:T(128)S(1)}, s32[32]{0:T(128)}, u32[]{:S(2)}) copy-start(s32[32]{0:T(128)} %param.36) | copy-start | bytes 388
  28.8 8.9 %copy-start.13 = (s32[32]{0:T(128)S(1)}, s32[32]{0:T(128)}, u32[]{:S(2)}) copy-start(s32[32]{0:T(128)} %param.35) | copy-start | bytes 388
  28.8 67.1 %all-to-all-start = ((bf16[16,2,128,2,256]{4,2,3,1,0:T(8,128)(2,1)}), bf16[16,2,128,2,256]{4,2,3,1,0:T(8,128)(2,1)}, u32[]{:S(2)}, u32[]{:S(2)}) async-start(bf16[16,2,128,2,256]{4,2,3,1,0:T(8,128)(2,1)} %copy_select_fusion), calls=%async_computation | async-start | bytes 8388608 | tf_op jit(solution)/shard_map/all_to_all | solution.py:209
  36.8 116.4 %all-gather.5.cloned.1.call-start = ((), (), s32[]{:S(2)}) async-start(), calls=%async_computation.5 | async-start | bytes 1114112 | tf_op jit(solution)/shard_map/all_gather | solution.py:151
  65.6 5.6 %copy-start.2 = (bf16[128,2048]{1,0:T(8,128)(2,1)S(1)}, bf16[128,2048]{1,0:T(8,128)(2,1)}, u32[]{:S(2)}) copy-start(bf16[128,2048]{1,0:T(8,128)(2,1)} %param.21) | copy-start | bytes 1572868
  65.6 6.8 %copy-start.7 = (s32[16,8]{0,1:T(8,128)S(1)}, s32[16,8]{0,1:T(8,128)}, u32[]{:S(2)}) copy-start(s32[16,8]{0,1:T(8,128)} %param.39) | copy-start | bytes 1540
  95.9 60.0 %all-to-all-start.1 = ((bf16[128,16,1024]{2,1,0:T(8,128)(2,1)}), bf16[128,16,1024]{2,1,0:T(8,128)(2,1)}, u32[]{:S(2)}, u32[]{:S(2)}) async-start(bf16[128,16,1024]{2,1,0:T(8,128)(2,1)} %bitcast.90), calls=%async_computation.1 | async-start | bytes 8388608 | tf_op jit(solution)/shard_map/all_to_all | solution.py:162
  120.8 2.8 copy-start.9
  123.5 4.3 %copy-start.10 = (f32[128]{0:T(128)S(1)}, f32[128]{0:T(128)}, u32[]{:S(2)}) copy-start(f32[128]{0:T(128)} %param.24) | copy-start | bytes 1540
  123.5 4.3 %copy-start.11 = (f32[128]{0:T(128)S(1)}, f32[128]{0:T(128)}, u32[]{:S(2)}) copy-start(f32[128]{0:T(128)} %param.23) | copy-start | bytes 1540
  126.1 0.8 copy-start.4
  127.8 1.6 copy-start.3
  138.0 43.1 %copy-start.8 = (f32[2048]{0:T(1024)S(1)}, f32[2048]{0:T(1024)}, u32[]{:S(2)}) copy-start(f32[2048]{0:T(1024)} %param.25) | copy-start | bytes 24580
  239.9 35.1 %all-to-all-start.3 = ((bf16[128,3,2048]{2,1,0:T(4,128)(2,1)}), bf16[128,3,2048]{2,1,0:T(4,128)(2,1)}, u32[]{:S(2)}, u32[]{:S(2)}) async-start(bf16[128,3,2048]{2,1,0:T(4,128)(2,1)} %reshape.349), calls=%async_computation.3 | async-start | bytes 4194304 | tf_op jit(solution)/shard_map/all_to_all | solution.py:287
  246.5 2.5 copy-start.5
Sparse Core Ops, SparseCore 0:
  11.0 65.7 all-gather.2
  79.0 74.1 all-gather.4

commit v10 on v9

--- a/solution.py
+++ b/solution.py
@@ -276,14 +276,11 @@
         (expert_count, 2, slot_depth, model_width),
     ).reshape(2 * expert_count, slot_depth, model_width)
     arrived_rows = lax.all_to_all(send_rows, ("req", "tp"), split_axis=0, concat_axis=0, tiled=True)
-    flat_rows = arrived_rows.reshape(-1, model_width)
-    both = jnp.dot(flat_rows, server_gate_up[0], preferred_element_type=jnp.float32)
-    act = (jax.nn.silu(both[:, :half_units]) * both[:, half_units:]).astype(jnp.bfloat16)
-    expert_rows = (
-        jnp.dot(act, down_weight[0], preferred_element_type=jnp.float32)
-        .astype(jnp.bfloat16)
-        .reshape(arrived_rows.shape)
-    )
+    both = jnp.einsum("xkd,df->xkf", arrived_rows, server_gate_up[0], preferred_element_type=jnp.float32)
+    act = (jax.nn.silu(both[..., :half_units]) * both[..., half_units:]).astype(jnp.bfloat16)
+    expert_rows = jnp.einsum(
+        "xkf,fd->xkd", act, down_weight[0], preferred_element_type=jnp.float32
+    ).astype(jnp.bfloat16)
     returned = lax.all_to_all(expert_rows, ("req", "tp"), split_axis=0, concat_axis=0, tiled=True)
     slot_weights = jnp.sum(
         jnp.where(

time: 288 us -> 280 us (0.972)
  local copies, waits for them, and re-layouts: 63 us -> 55.5 us
    reshape x2 -> x0, local copies, waits for them, and re-layouts: 10.2 us -> none  [the longest x1 5.19 us: body(): expert_rows = jnp.dot(act, down_weight[0], preferred_element_type=jnp.flo...]
  transfers between devices with their start and end apart: 5 -> 5, of which waited for: 4 -> 4; matrix products, arithmetic and copies ran while one was open for 33% -> 34% of each run, Pallas kernels for 4% -> 4%
where the time goes in v10:
time: 280 us; the launch traced here: 278 us
  local copies, waits for them, and re-layouts  55.5 us (20%)
  waiting for transfers between devices  49.4 us (18%)
  other arithmetic  41.9 us (15%)
  blocking collectives  36.9 us (13%)
  Pallas kernels  35.1 us (13%)
  starting transfers between devices  22.8 us (8%)
  matrix products  22.1 us (8%)
  between operations  14.5 us (5%)
    all_to_all x1, blocking collectives, body(): lax.all_to_all(send_rows, ('req', 'tp'), split_axis=0, concat_axis=0, til...  36.9 us
    pallas_call x1, Pallas kernels, scatter_sum(): pl.pallas_call(functools.partial(scatter_sum_kernel, parts), out_shape=ja...  24 us
    all_to_all x1, waiting for transfers between devices, body(): lax.all_to_all(expert_rows, ('req', 'tp'), split_axis=0, concat_axis=0, t...  17.3 us
    all_to_all x1, waiting for transfers between devices, body(): lax.all_to_all(outgoing_pages, 'req', split_axis=0, concat_axis=0, tiled=...  17 us
    gather x4, local copies, waits for them, and re-layouts, body(): jnp.take(arrived_pages.reshape((req_count * capacity,) + page_shape), own...  16.8 us
    all_gather x1, waiting for transfers between devices, body(): lax.all_gather(out_weight.astype(jnp.bfloat16), 'req', axis=1, tiled=True)  15 us
    pallas_call x3, Pallas kernels, copy_rows(): pl.pallas_call(copy_kernel, out_shape=jax.ShapeDtypeStruct(x.shape, x.dty...  11.2 us
    concatenate x1, other arithmetic, body(): jnp.concatenate([split_halves(gate_weight.astype(jnp.bfloat16)), split_ha...  10.6 us
  transfers between devices with their start and end apart: 5, of which 4 were waited for; matrix products, arithmetic and copies ran while one was open for 34% of the time, Pallas kernels for 4%

profile of v10, /device:TPU:1, one launch (start us, length us, event | category | flops | bytes accessed | tf_op | source)
XLA Modules:
  0.0 278.4 jit_solution(12713649242247115218)
XLA Ops:
  13.9 10.0 %gather_fusion = bf16[32,128,2,256]{3,2,1,0:T(2,128)(2,1)} fusion(bf16[8,128,2,256]{3,2,1,0:T(2,128)(2,1)S(1)} %copy-done.1, s32[1024]{0:T(1024)S(1)} %pad_clamp_fusion.1), kind=kCustom, calls=%fused_computation | custom fusion | bytes 8388736 | tf_op jit(solution)/shard_map/jit(_take)/gather | solution.py:206
  24.0 4.7 %copy_select_fusion = bf16[16,2,128,2,256]{4,2,3,1,0:T(8,128)(2,1)} fusion(bf16[16,2,128,2,256]{4,3,2,1,0:T(2,128)(2,1)} %bitcast.90, pred[16,2]{1,0:T(8,128)(4,1)S(1)} %copy.127), kind=kLoop, calls=%fused_computation.6 | loop fusion | flops 2097152 | bytes 8388640 | tf_op jit(solution)/shard_map/jit(_take)/select_n | solution.py:206
  28.7 8.0 %all-to-all-start = ((bf16[16,2,128,2,256]{4,2,3,1,0:T(8,128)(2,1)}), bf16[16,2,128,2,256]{4,2,3,1,0:T(8,128)(2,1)}, u32[]{:S(2)}, u32[]{:S(2)}) async-start(bf16[16,2,128,2,256]{4,2,3,1,0:T(8,128)(2,1)} %copy_select_fusion), calls=%async_computation | async-start | bytes 8388608 | tf_op jit(solution)/shard_map/all_to_all | solution.py:209
  38.2 3.9 %convert_element_type.114 = bf16[64,16,1024]{2,1,0:T(8,128)(2,1)} convert(f32[64,16,1024]{2,1,0:T(8,128)} %param.30) | non-fusion elementwise | flops 1048576 | bytes 6291456 | tf_op jit(solution)/shard_map/convert_element_type | solution.py:157
  42.1 4.5 %reshape.334 = bf16[64,16,2,512]{3,2,1,0:T(2,128)(2,1)} reshape(bf16[64,16,1024]{2,1,0:T(8,128)(2,1)} %convert_element_type.114) | data formatting | bytes 4194304 | tf_op jit(solution)/shard_map/reshape | solution.py:38
  46.6 3.9 %convert_element_type.115 = bf16[64,16,1024]{2,1,0:T(8,128)(2,1)} convert(f32[64,16,1024]{2,1,0:T(8,128)} %param.31) | non-fusion elementwise | flops 1048576 | bytes 6291456 | tf_op jit(solution)/shard_map/convert_element_type | solution.py:158
  50.5 4.5 %reshape.335 = bf16[64,16,2,512]{3,2,1,0:T(2,128)(2,1)} reshape(bf16[64,16,1024]{2,1,0:T(8,128)(2,1)} %convert_element_type.115) | data formatting | bytes 4194304 | tf_op jit(solution)/shard_map/reshape | solution.py:38
  55.0 10.6 %pad_maximum_fusion = bf16[64,2,16,1024]{3,1,2,0:T(2,128)(2,1)} fusion(bf16[64,2,16,512]{3,1,2,0:T(2,128)(2,1)} %bitcast.94, bf16[64,2,16,512]{3,1,2,0:T(2,128)(2,1)} %bitcast.93), kind=kLoop, calls=%fused_computation.3 | loop fusion | flops 8388608 | bytes 8388608 | tf_op jit(solution)/shard_map/concatenate | solution.py:155
  65.5 5.6 %copy.135 = bf16[64,2,16,1024]{3,2,1,0:T(8,128)(2,1)} copy(bf16[64,2,16,1024]{3,1,2,0:T(2,128)(2,1)} %pad_maximum_fusion) | data formatting | bytes 8388608 | tf_op jit(solution)/shard_map/concatenate | solution.py:155
  79.1 17.0 %all-to-all-done = bf16[16,2,128,2,256]{4,2,3,1,0:T(8,128)(2,1)} async-done(((bf16[16,2,128,2,256]{4,2,3,1,0:T(8,128)(2,1)}), bf16[16,2,128,2,256]{4,2,3,1,0:T(8,128)(2,1)}, u32[]{:S(2)}, u32[]{:S(2)}) %all-to-all-start) | async-done | bytes 4194336 | tf_op jit(solution)/shard_map/all_to_all | solution.py:209
  96.0 8.2 %all-to-all-start.1 = ((bf16[128,16,1024]{2,1,0:T(8,128)(2,1)}), bf16[128,16,1024]{2,1,0:T(8,128)(2,1)}, u32[]{:S(2)}, u32[]{:S(2)}) async-start(bf16[128,16,1024]{2,1,0:T(8,128)(2,1)} %bitcast.91), calls=%async_computation.1 | async-start | bytes 8388608 | tf_op jit(solution)/shard_map/all_to_all | solution.py:162
  104.2 4.2 %gather_fusion.1 = bf16[16,128,2,256]{3,1,2,0:T(8,128)(2,1)} fusion(bf16[32,128,2,256]{3,1,2,0:T(8,128)(2,1)} %bitcast.9, s32[1024]{0:T(1024)S(1)} %pad_clamp_fusion), kind=kCustom, calls=%fused_computation.1 | custom fusion | bytes 4194368 | tf_op jit(solution)/shard_map/jit(_take)/gather | solution.py:212
  108.4 4.5 %copy.130 = bf16[16,128,2,256]{1,0,3,2:T(8,128)(2,1)} copy(bf16[16,128,2,256]{3,1,2,0:T(8,128)(2,1)} %gather_fusion.1) | data formatting | bytes 4194304 | tf_op jit(solution)/shard_map/jit(_take)/gather | solution.py:212
  112.9 4.2 %gather.22 = bf16[2048,2,2,128]{0,3,2,1:T(8,128)(2,1)} reshape(bf16[16,128,2,256]{1,0,3,2:T(8,128)(2,1)} %copy.130) | data formatting | bytes 4194304 | tf_op jit(solution)/shard_map/jit(_take)/gather | solution.py:212
  117.1 3.9 %copy.131 = bf16[2048,2,2,128]{3,0,2,1:T(8,128)(2,1)} copy(bf16[2048,2,2,128]{0,3,2,1:T(8,128)(2,1)} %gather.22) | data formatting | bytes 4194304 | tf_op jit(solution)/shard_map/jit(_take)/gather | solution.py:212
  121.0 2.8 broadcast_select_fusion
  123.8 2.5 fusion.14
  129.6 2.0 fusion.41
  131.6 4.2 %shard_map.218 = bf16[2048,768]{1,0:T(8,128)(2,1)} custom-call(bf16[2048,768]{1,0:T(8,128)(2,1)} %all-gather.3.cloned.1.call-done.x_ref), custom_call_target="tpu_custom_call" | custom-call | bytes 6291456 | tf_op jit(solution)/shard_map/pallas_call | solution.py:107
  135.8 2.5 fusion.12
  138.5 15.0 %all-gather.5.cloned.1.call-done.x_ref = bf16[256,2048]{1,0:T(8,128)(2,1)} async-done(((bf16[256,128]{1,0:T(8,128)(2,1)}), bf16[256,2048]{1,0:T(8,128)(2,1)}) %all-gather.5.cloned.1.call-update) | async-done | bytes 1048592 | tf_op jit(solution)/shard_map/all_gather | solution.py:151
  153.4 2.5 fusion.42.x_ref
  156.0 24.0 %shard_map.221 = f32[16,2048]{1,0:T(8,128)} custom-call(f32[128,2048]{1,0:T(8,128)} %fusion.42.x_ref), custom_call_target="tpu_custom_call" | custom-call | tf_op jit(solution)/shard_map/pallas_call | solution.py:85
  182.4 2.4 broadcast_in_dim.156
  186.1 36.9 %all_to_all.27 = bf16[128,3,2048]{2,1,0:T(4,128)(2,1)S(1)} all-to-all(bf16[128,3,2048]{2,1,0:T(4,128)(2,1)S(1)} %bitcast.92), channel_id=1, replica_groups=mesh['req'=16,'tp'=8] {'req','tp'}, dimensions={0} | all-to-all | bytes 3145728 | tf_op jit(solution)/shard_map/all_to_all | solution.py:278
  223.0 5.1 %fusion = f32[128,3,1024]{2,0,1:T(8,128)S(1)} fusion(bf16[1,2048,1024]{2,1,0:T(8,128)(2,1)} %bitcast.17, bf16[128,3,2048]{2,1,0:T(4,128)(2,1)S(1)} %all_to_all.27), kind=kOutput, calls=%fused_computation.4 | convolution fusion | flops 1610612736 | bytes 7340032 | tf_op jit(solution)/shard_map/xkd,df->xkf/dot_general | solution.py:279
  229.2 2.7 copy.144
  231.9 6.6 %all-to-all-start.3 = ((bf16[128,3,2048]{2,1,0:T(4,128)(2,1)}), bf16[128,3,2048]{2,1,0:T(4,128)(2,1)}, u32[]{:S(2)}, u32[]{:S(2)}) async-start(bf16[128,3,2048]{2,1,0:T(4,128)(2,1)} %copy.144), calls=%async_computation.3 | async-start | bytes 4194304 | tf_op jit(solution)/shard_map/all_to_all | solution.py:284
  238.7 2.3 shard_map.219
  243.1 4.7 %shard_map.220 = bf16[2048,1024]{1,0:T(8,128)(2,1)} custom-call(bf16[2048,1024]{1,0:T(8,128)(2,1)} %bitcast.18.x_ref), custom_call_target="tpu_custom_call" | custom-call | bytes 8388608 | tf_op jit(solution)/shard_map/pallas_call | solution.py:107
  249.7 17.3 %all-to-all-done.3 = bf16[128,3,2048]{2,1,0:T(4,128)(2,1)} async-done(((bf16[128,3,2048]{2,1,0:T(4,128)(2,1)}), bf16[128,3,2048]{2,1,0:T(4,128)(2,1)}, u32[]{:S(2)}, u32[]{:S(2)}) %all-to-all-start.3) | async-done | bytes 1572896 | tf_op jit(solution)/shard_map/all_to_all | solution.py:284
  267.1 4.5 %fusion.5 = bf16[16,2048]{1,0:T(8,128)(2,1)} fusion(f32[16,2048]{1,0:T(8,128)S(1)} %get-tuple-element.56, f32[16,128,3]{0,1,2:T(8,128)S(1)} %bitcast.96, bf16[128,3,2048]{2,1,0:T(4,128)(2,1)} %all-to-all-done.3), kind=kOutput, calls=%fused_computation.14 | convolution fusion | flops 151060480 | bytes 1794048 | tf_op jit(solution)/shard_map/ixk,xkd->id/dot_general | solution.py:296
  (114 shorter events, 28.1 us)
Async XLA Ops:
  7.2 221.0 %copy-start = (bf16[1,512,2048]{2,1,0:T(8,128)(2,1)S(1)}, bf16[1,512,2048]{2,1,0:T(8,128)(2,1)}, u32[]{:S(2)}) copy-start(bf16[1,512,2048]{2,1,0:T(8,128)(2,1)} %param.32) | copy-start | bytes 6291460
  7.2 6.7 %copy-start.1 = (bf16[8,128,2,256]{3,2,1,0:T(2,128)(2,1)S(1)}, bf16[8,128,2,256]{3,2,1,0:T(2,128)(2,1)}, u32[]{:S(2)}) copy-start(bf16[8,128,2,256]{3,2,1,0:T(2,128)(2,1)} %param.34) | copy-start | bytes 3145732
  7.2 116.6 %all-gather.3.cloned.1.call-start = ((), (), s32[]{:S(2)}) async-start(), calls=%async_computation.4 | async-start | bytes 3342336 | tf_op jit(solution)/shard_map/all_gather | solution.py:150
  28.7 8.1 %copy-start.6 = (f32[256,128]{1,0:T(8,128)S(1)}, f32[256,128]{1,0:T(8,128)}, u32[]{:S(2)}) copy-start(f32[256,128]{1,0:T(8,128)} %param.29) | copy-start | bytes 393220
  28.7 8.8 %copy-start.12 = (s32[32]{0:T(128)S(1)}, s32[32]{0:T(128)}, u32[]{:S(2)}) copy-start(s32[32]{0:T(128)} %param.36) | copy-start | bytes 388
  28.7 8.9 %copy-start.13 = (s32[32]{0:T(128)S(1)}, s32[32]{0:T(128)}, u32[]{:S(2)}) copy-start(s32[32]{0:T(128)} %param.35) | copy-start | bytes 388
  28.7 67.3 %all-to-all-start = ((bf16[16,2,128,2,256]{4,2,3,1,0:T(8,128)(2,1)}), bf16[16,2,128,2,256]{4,2,3,1,0:T(8,128)(2,1)}, u32[]{:S(2)}, u32[]{:S(2)}) async-start(bf16[16,2,128,2,256]{4,2,3,1,0:T(8,128)(2,1)} %copy_select_fusion), calls=%async_computation | async-start | bytes 8388608 | tf_op jit(solution)/shard_map/all_to_all | solution.py:209
  36.7 116.7 %all-gather.5.cloned.1.call-start = ((), (), s32[]{:S(2)}) async-start(), calls=%async_computation.5 | async-start | bytes 1114112 | tf_op jit(solution)/shard_map/all_gather | solution.py:151
  65.5 5.6 %copy-start.2 = (bf16[128,2048]{1,0:T(8,128)(2,1)S(1)}, bf16[128,2048]{1,0:T(8,128)(2,1)}, u32[]{:S(2)}) copy-start(bf16[128,2048]{1,0:T(8,128)(2,1)} %param.21) | copy-start | bytes 1572868
  65.5 6.8 %copy-start.7 = (s32[16,8]{0,1:T(8,128)S(1)}, s32[16,8]{0,1:T(8,128)}, u32[]{:S(2)}) copy-start(s32[16,8]{0,1:T(8,128)} %param.39) | copy-start | bytes 1540
  96.0 60.0 %all-to-all-start.1 = ((bf16[128,16,1024]{2,1,0:T(8,128)(2,1)}), bf16[128,16,1024]{2,1,0:T(8,128)(2,1)}, u32[]{:S(2)}, u32[]{:S(2)}) async-start(bf16[128,16,1024]{2,1,0:T(8,128)(2,1)} %bitcast.91), calls=%async_computation.1 | async-start | bytes 8388608 | tf_op jit(solution)/shard_map/all_to_all | solution.py:162
  121.0 2.8 copy-start.9
  123.8 4.3 %copy-start.10 = (f32[128]{0:T(128)S(1)}, f32[128]{0:T(128)}, u32[]{:S(2)}) copy-start(f32[128]{0:T(128)} %param.24) | copy-start | bytes 1540
  123.8 4.3 %copy-start.11 = (f32[128]{0:T(128)S(1)}, f32[128]{0:T(128)}, u32[]{:S(2)}) copy-start(f32[128]{0:T(128)} %param.23) | copy-start | bytes 1540
  126.3 0.8 copy-start.4
  128.0 1.6 copy-start.3
  138.3 42.8 %copy-start.8 = (f32[2048]{0:T(1024)S(1)}, f32[2048]{0:T(1024)}, u32[]{:S(2)}) copy-start(f32[2048]{0:T(1024)} %param.25) | copy-start | bytes 24580
  231.9 35.1 %all-to-all-start.3 = ((bf16[128,3,2048]{2,1,0:T(4,128)(2,1)}), bf16[128,3,2048]{2,1,0:T(4,128)(2,1)}, u32[]{:S(2)}, u32[]{:S(2)}) async-start(bf16[128,3,2048]{2,1,0:T(4,128)(2,1)} %copy.144), calls=%async_computation.3 | async-start | bytes 4194304 | tf_op jit(solution)/shard_map/all_to_all | solution.py:284
  238.5 2.5 copy-start.5
Sparse Core Ops, SparseCore 0:
  11.0 65.7 all-gather.2
  79.0 74.4 all-gather.4

commit v11 on v10

--- a/solution.py
+++ b/solution.py
@@ -111,6 +111,18 @@
         in_specs=[pl.BlockSpec(block, index)],
         out_specs=pl.BlockSpec(block, index),
         cost_estimate=pl.CostEstimate(flops=0, transcendentals=0, bytes_accessed=2 * x.size * x.dtype.itemsize),
+    )(x)
+
+
+def copy_columns(x, width, steps):
+    rows = x.shape[0] // steps
+    return pl.pallas_call(
+        copy_kernel,
+        out_shape=jax.ShapeDtypeStruct((x.shape[0], width), x.dtype),
+        grid=(steps,),
+        in_specs=[pl.BlockSpec((rows, width), lambda i: (i, 0))],
+        out_specs=pl.BlockSpec((rows, width), lambda i: (i, 0)),
+        cost_estimate=pl.CostEstimate(flops=0, transcendentals=0, bytes_accessed=2 * x.shape[0] * width * x.dtype.itemsize),
     )(x)
 
 
@@ -146,9 +158,19 @@
         ],
         axis=1,
     )
-    server_qkv, server_out = (
-        lax.all_gather(joined_local, "req", axis=0, tiled=True),
-        lax.all_gather(out_weight.astype(jnp.bfloat16), "req", axis=1, tiled=True),
+    out_block = out_weight.astype(jnp.bfloat16)
+    qkv_width = joined_local.shape[1]
+    out_rows, out_cols = out_block.shape
+    group_rows_w = joined_local.shape[0]
+    gathered = lax.all_gather(
+        jnp.concatenate([joined_local, out_block.reshape(group_rows_w, -1)], axis=1), "req", axis=0, tiled=True
+    )
+    server_qkv = gathered[:, :qkv_width]
+    server_out = (
+        gathered[:, qkv_width:]
+        .reshape(req_count, out_rows, out_cols)
+        .transpose(1, 0, 2)
+        .reshape(out_rows, req_count * out_cols)
     )
     expert_count, rows_here, hidden_units = gate_weight.shape
     half_units = hidden_units // 2
@@ -244,7 +266,7 @@
     attended = attended.astype(jnp.bfloat16).reshape(group_rows, lane_width)
     shard_rows = routes.shape[0]
     row_start = lane_index * shard_rows
-    qkv_out = copy_rows(server_qkv, 4)
+    qkv_out = copy_columns(gathered, qkv_width, 4)
     qkv_out, attended = lax.optimization_barrier((qkv_out, attended))
     head_terms = jnp.dot(attended, server_out, preferred_element_type=jnp.float32)
     server_gate_up, head_terms = lax.optimization_barrier((server_gate_up, head_terms))

time: 280 us -> 283 us (1.011)
  local copies, waits for them, and re-layouts: 55.5 us -> 62.9 us
  blocking collectives: 36.9 us -> 33 us
    all_gather x2 -> x1, waiting for transfers between devices: 15 us -> 0.01 us  [body(): lax.all_gather(jnp.concatenate([joined_local, out_block.reshape(group_row...]
    all_to_all x1, waiting for transfers between devices: 0.06 us -> 11.7 us  [body(): lax.all_to_all(packed, ('req', 'tp'), split_axis=0, concat_axis=1, tiled=...]
    all_to_all x1, waiting for transfers between devices: 17 us -> 23.4 us  [body(): lax.all_to_all(outgoing_pages, 'req', split_axis=0, concat_axis=0, tiled=...]
    pallas_call x3 -> x2, Pallas kernels: 11.2 us -> 7 us  [copy_rows(): pl.pallas_call(copy_kernel, out_shape=jax.ShapeDtypeStruct(x.shape, x.dty...]
    pallas_call x0 -> x1, Pallas kernels: none -> 4.18 us  [copy_columns(): pl.pallas_call(copy_kernel, out_shape=jax.ShapeDtypeStruct((x.shape[0], w...]
    all_to_all x1, blocking collectives: 36.9 us -> 33 us  [body(): lax.all_to_all(send_rows, ('req', 'tp'), split_axis=0, concat_axis=0, til...]
    reshape x0 -> x3, local copies, waits for them, and re-layouts: none -> 3.08 us  [the longest x2 3.05 us: body(): server_out = gathered[:, qkv_width:].reshape(req_count, out_rows, out_col...]
  transfers between devices with their start and end apart: 5 -> 4, of which waited for: 4 -> 3; matrix products, arithmetic and copies ran while one was open for 34% -> 35% of each run, Pallas kernels for 4% -> 4%
where the time goes in v11:
time: 283 us; the launch traced here: 281 us
  local copies, waits for them, and re-layouts  62.9 us (22%)
  waiting for transfers between devices  51.1 us (18%)
  other arithmetic  42.2 us (15%)
  Pallas kernels  34.4 us (12%)
  blocking collectives  33 us (12%)
  starting transfers between devices  22.4 us (8%)
  matrix products  20.9 us (7%)
  between operations  14.5 us (5%)
    all_to_all x1, blocking collectives, body(): lax.all_to_all(send_rows, ('req', 'tp'), split_axis=0, concat_axis=0, til...  33 us
    all_to_all x1, waiting for transfers between devices, body(): lax.all_to_all(outgoing_pages, 'req', split_axis=0, concat_axis=0, tiled=...  23.4 us
    pallas_call x1, Pallas kernels, scatter_sum(): pl.pallas_call(functools.partial(scatter_sum_kernel, parts), out_shape=ja...  23.2 us
    gather x4, local copies, waits for them, and re-layouts, body(): jnp.take(arrived_pages.reshape((req_count * capacity,) + page_shape), own...  16.8 us
    all_to_all x1, waiting for transfers between devices, body(): lax.all_to_all(expert_rows, ('req', 'tp'), split_axis=0, concat_axis=0, t...  16 us
    all_to_all x1, waiting for transfers between devices, body(): lax.all_to_all(packed, ('req', 'tp'), split_axis=0, concat_axis=1, tiled=...  11.7 us
    concatenate x1, other arithmetic, body(): jnp.concatenate([split_halves(gate_weight.astype(jnp.bfloat16)), split_ha...  10.6 us
    gather x1, local copies, waits for them, and re-layouts, body(): jnp.take(page_store, send_slot.reshape(-1), axis=0)  10.1 us
  transfers between devices with their start and end apart: 4, of which 3 were waited for; matrix products, arithmetic and copies ran while one was open for 35% of the time, Pallas kernels for 4%

profile of v11, /device:TPU:1, one launch (start us, length us, event | category | flops | bytes accessed | tf_op | source)
XLA Modules:
  0.0 281.4 jit_solution(16704187382398041706)
XLA Ops:
  14.9 10.1 %gather_fusion = bf16[32,128,2,256]{3,2,1,0:T(2,128)(2,1)} fusion(bf16[8,128,2,256]{3,2,1,0:T(2,128)(2,1)S(1)} %copy-done.1, s32[1024]{0:T(1024)S(1)} %pad_clamp_fusion.1), kind=kCustom, calls=%fused_computation | custom fusion | bytes 8388736 | tf_op jit(solution)/shard_map/jit(_take)/gather | solution.py:228
  25.0 4.7 %copy_select_fusion = bf16[16,2,128,2,256]{4,2,3,1,0:T(8,128)(2,1)} fusion(bf16[16,2,128,2,256]{4,3,2,1,0:T(2,128)(2,1)} %bitcast.94, pred[16,2]{1,0:T(8,128)(4,1)S(1)} %copy.132), kind=kLoop, calls=%fused_computation.6 | loop fusion | flops 2097152 | bytes 8388640 | tf_op jit(solution)/shard_map/jit(_take)/select_n | solution.py:228
  29.7 8.0 %all-to-all-start = ((bf16[16,2,128,2,256]{4,2,3,1,0:T(8,128)(2,1)}), bf16[16,2,128,2,256]{4,2,3,1,0:T(8,128)(2,1)}, u32[]{:S(2)}, u32[]{:S(2)}) async-start(bf16[16,2,128,2,256]{4,2,3,1,0:T(8,128)(2,1)} %copy_select_fusion), calls=%async_computation | async-start | bytes 8388608 | tf_op jit(solution)/shard_map/all_to_all | solution.py:231
  38.4 3.9 %convert_element_type.114 = bf16[64,16,1024]{2,1,0:T(8,128)(2,1)} convert(f32[64,16,1024]{2,1,0:T(8,128)} %param.30) | non-fusion elementwise | flops 1048576 | bytes 6291456 | tf_op jit(solution)/shard_map/convert_element_type | solution.py:179
  42.3 4.5 %reshape.346 = bf16[64,16,2,512]{3,2,1,0:T(2,128)(2,1)} reshape(bf16[64,16,1024]{2,1,0:T(8,128)(2,1)} %convert_element_type.114) | data formatting | bytes 4194304 | tf_op jit(solution)/shard_map/reshape | solution.py:38
  46.8 3.8 %convert_element_type.115 = bf16[64,16,1024]{2,1,0:T(8,128)(2,1)} convert(f32[64,16,1024]{2,1,0:T(8,128)} %param.31) | non-fusion elementwise | flops 1048576 | bytes 6291456 | tf_op jit(solution)/shard_map/convert_element_type | solution.py:180
  50.7 4.5 %reshape.347 = bf16[64,16,2,512]{3,2,1,0:T(2,128)(2,1)} reshape(bf16[64,16,1024]{2,1,0:T(8,128)(2,1)} %convert_element_type.115) | data formatting | bytes 4194304 | tf_op jit(solution)/shard_map/reshape | solution.py:38
  55.2 10.6 %pad_maximum_fusion = bf16[64,2,16,1024]{3,1,2,0:T(2,128)(2,1)} fusion(bf16[64,2,16,512]{3,1,2,0:T(2,128)(2,1)} %bitcast.100, bf16[64,2,16,512]{3,1,2,0:T(2,128)(2,1)} %bitcast.99), kind=kLoop, calls=%fused_computation.3 | loop fusion | flops 8388608 | bytes 8388608 | tf_op jit(solution)/shard_map/concatenate | solution.py:177
  65.8 5.6 %copy.141 = bf16[64,2,16,1024]{3,2,1,0:T(8,128)(2,1)} copy(bf16[64,2,16,1024]{3,1,2,0:T(2,128)(2,1)} %pad_maximum_fusion) | data formatting | bytes 8388608 | tf_op jit(solution)/shard_map/concatenate | solution.py:177
  79.3 23.4 %all-to-all-done = bf16[16,2,128,2,256]{4,2,3,1,0:T(8,128)(2,1)} async-done(((bf16[16,2,128,2,256]{4,2,3,1,0:T(8,128)(2,1)}), bf16[16,2,128,2,256]{4,2,3,1,0:T(8,128)(2,1)}, u32[]{:S(2)}, u32[]{:S(2)}) %all-to-all-start) | async-done | bytes 4194336 | tf_op jit(solution)/shard_map/all_to_all | solution.py:231
  102.6 7.8 %all-to-all-start.1 = ((bf16[128,16,1024]{2,1,0:T(8,128)(2,1)}), bf16[128,16,1024]{2,1,0:T(8,128)(2,1)}, u32[]{:S(2)}, u32[]{:S(2)}) async-start(bf16[128,16,1024]{2,1,0:T(8,128)(2,1)} %bitcast.95), calls=%async_computation.1 | async-start | bytes 8388608 | tf_op jit(solution)/shard_map/all_to_all | solution.py:184
  110.4 4.2 %gather_fusion.1 = bf16[16,128,2,256]{3,1,2,0:T(8,128)(2,1)} fusion(bf16[32,128,2,256]{3,1,2,0:T(8,128)(2,1)} %bitcast.9, s32[1024]{0:T(1024)S(1)} %pad_clamp_fusion), kind=kCustom, calls=%fused_computation.1 | custom fusion | bytes 4194368 | tf_op jit(solution)/shard_map/jit(_take)/gather | solution.py:234
  114.6 4.5 %copy.135 = bf16[16,128,2,256]{1,0,3,2:T(8,128)(2,1)} copy(bf16[16,128,2,256]{3,1,2,0:T(8,128)(2,1)} %gather_fusion.1) | data formatting | bytes 4194304 | tf_op jit(solution)/shard_map/jit(_take)/gather | solution.py:234
  119.1 4.2 %gather.22 = bf16[2048,2,2,128]{0,3,2,1:T(8,128)(2,1)} reshape(bf16[16,128,2,256]{1,0,3,2:T(8,128)(2,1)} %copy.135) | data formatting | bytes 4194304 | tf_op jit(solution)/shard_map/jit(_take)/gather | solution.py:234
  123.3 3.9 %copy.136 = bf16[2048,2,2,128]{3,0,2,1:T(8,128)(2,1)} copy(bf16[2048,2,2,128]{0,3,2,1:T(8,128)(2,1)} %gather.22) | data formatting | bytes 4194304 | tf_op jit(solution)/shard_map/jit(_take)/gather | solution.py:234
  127.2 2.8 broadcast_select_fusion
  130.0 2.5 fusion.2
  135.7 2.0 fusion.43
  137.7 4.2 %shard_map.218 = bf16[2048,768]{1,0:T(8,128)(2,1)} custom-call(bf16[2048,1024]{1,0:T(8,128)(2,1)} %all-gather.2.cloned.1.call-done.x_ref), custom_call_target="tpu_custom_call" | custom-call | bytes 6291456 | tf_op jit(solution)/shard_map/pallas_call | solution.py:119
  141.9 2.5 fusion.14
  150.0 11.7 %all-to-all-done.1 = bf16[128,16,1024]{2,1,0:T(8,128)(2,1)} async-done(((bf16[128,16,1024]{2,1,0:T(8,128)(2,1)}), bf16[128,16,1024]{2,1,0:T(8,128)(2,1)}, u32[]{:S(2)}, u32[]{:S(2)}) %all-to-all-start.1) | async-done | bytes 4194336 | tf_op jit(solution)/shard_map/all_to_all | solution.py:184
  161.7 23.2 %shard_map.221 = f32[16,2048]{1,0:T(8,128)} custom-call(f32[128,2048]{1,0:T(8,128)} %fusion.39.x_ref), custom_call_target="tpu_custom_call" | custom-call | tf_op jit(solution)/shard_map/pallas_call | solution.py:85
  187.4 3.3 %broadcast_in_dim.156 = bf16[64,3,2048]{2,1,0:T(4,128)(2,1)} reshape(bf16[192,2048]{1,0:T(8,128)(2,1)} %convolution_convert_fusion.1) | data formatting | bytes 1572864 | tf_op jit(solution)/shard_map/broadcast_in_dim | solution.py:296
  190.7 2.5 broadcast_in_dim.157
  193.1 33.0 %all_to_all.27 = bf16[128,3,2048]{2,1,0:T(4,128)(2,1)S(1)} all-to-all(bf16[128,3,2048]{2,1,0:T(4,128)(2,1)S(1)} %bitcast.98), channel_id=1, replica_groups=mesh['req'=16,'tp'=8] {'req','tp'}, dimensions={0} | all-to-all | bytes 3145728 | tf_op jit(solution)/shard_map/all_to_all | solution.py:300
  226.1 5.1 %fusion = f32[128,3,1024]{2,0,1:T(8,128)S(1)} fusion(bf16[1,2048,1024]{2,1,0:T(8,128)(2,1)} %bitcast.18, bf16[128,3,2048]{2,1,0:T(4,128)(2,1)S(1)} %all_to_all.27), kind=kOutput, calls=%fused_computation.4 | convolution fusion | flops 1610612736 | bytes 7340032 | tf_op jit(solution)/shard_map/xkd,df->xkf/dot_general | solution.py:301
  232.3 2.6 copy.150
  234.9 6.6 %all-to-all-start.3 = ((bf16[128,3,2048]{2,1,0:T(4,128)(2,1)}), bf16[128,3,2048]{2,1,0:T(4,128)(2,1)}, u32[]{:S(2)}, u32[]{:S(2)}) async-start(bf16[128,3,2048]{2,1,0:T(4,128)(2,1)} %copy.150), calls=%async_computation.3 | async-start | bytes 4194304 | tf_op jit(solution)/shard_map/all_to_all | solution.py:306
  245.2 4.7 %shard_map.220 = bf16[2048,1024]{1,0:T(8,128)(2,1)} custom-call(bf16[2048,1024]{1,0:T(8,128)(2,1)} %bitcast.19.x_ref), custom_call_target="tpu_custom_call" | custom-call | bytes 8388608 | tf_op jit(solution)/shard_map/pallas_call | solution.py:107
  251.8 2.3 shard_map.219
  254.0 16.0 %all-to-all-done.3 = bf16[128,3,2048]{2,1,0:T(4,128)(2,1)} async-done(((bf16[128,3,2048]{2,1,0:T(4,128)(2,1)}), bf16[128,3,2048]{2,1,0:T(4,128)(2,1)}, u32[]{:S(2)}, u32[]{:S(2)}) %all-to-all-start.3) | async-done | bytes 1572896 | tf_op jit(solution)/shard_map/all_to_all | solution.py:306
  270.1 4.5 %fusion.7 = bf16[16,2048]{1,0:T(8,128)(2,1)} fusion(f32[16,2048]{1,0:T(8,128)S(1)} %get-tuple-element.56, f32[16,128,3]{0,1,2:T(8,128)S(1)} %bitcast.103, bf16[128,3,2048]{2,1,0:T(4,128)(2,1)} %all-to-all-done.3), kind=kOutput, calls=%fused_computation.16 | convolution fusion | flops 151060480 | bytes 1794048 | tf_op jit(solution)/shard_map/ixk,xkd->id/dot_general | solution.py:318
  (115 shorter events, 33.7 us)
Async XLA Ops:
  7.2 224.1 %copy-start = (bf16[1,512,2048]{2,1,0:T(8,128)(2,1)S(1)}, bf16[1,512,2048]{2,1,0:T(8,128)(2,1)}, u32[]{:S(2)}) copy-start(bf16[1,512,2048]{2,1,0:T(8,128)(2,1)} %param.32) | copy-start | bytes 6291460
  7.2 7.7 %copy-start.1 = (bf16[8,128,2,256]{3,2,1,0:T(2,128)(2,1)S(1)}, bf16[8,128,2,256]{3,2,1,0:T(2,128)(2,1)}, u32[]{:S(2)}) copy-start(bf16[8,128,2,256]{3,2,1,0:T(2,128)(2,1)} %param.34) | copy-start | bytes 3145732
  7.2 122.8 %all-gather.2.cloned.1.call-start = ((), (), s32[]{:S(2)}) async-start(), calls=%async_computation.4 | async-start | bytes 4456448 | tf_op jit(solution)/shard_map/all_gather | solution.py:165
  29.7 8.0 %copy-start.11 = (s32[32]{0:T(128)S(1)}, s32[32]{0:T(128)}, u32[]{:S(2)}) copy-start(s32[32]{0:T(128)} %param.36) | copy-start | bytes 388
  29.7 8.1 %copy-start.12 = (s32[32]{0:T(128)S(1)}, s32[32]{0:T(128)}, u32[]{:S(2)}) copy-start(s32[32]{0:T(128)} %param.35) | copy-start | bytes 388
  29.7 72.9 %all-to-all-start = ((bf16[16,2,128,2,256]{4,2,3,1,0:T(8,128)(2,1)}), bf16[16,2,128,2,256]{4,2,3,1,0:T(8,128)(2,1)}, u32[]{:S(2)}, u32[]{:S(2)}) async-start(bf16[16,2,128,2,256]{4,2,3,1,0:T(8,128)(2,1)} %copy_select_fusion), calls=%async_computation | async-start | bytes 8388608 | tf_op jit(solution)/shard_map/all_to_all | solution.py:231
  65.8 5.6 %copy-start.2 = (bf16[128,2048]{1,0:T(8,128)(2,1)S(1)}, bf16[128,2048]{1,0:T(8,128)(2,1)}, u32[]{:S(2)}) copy-start(bf16[128,2048]{1,0:T(8,128)(2,1)} %param.21) | copy-start | bytes 1572868
  65.8 6.7 %copy-start.6 = (s32[16,8]{0,1:T(8,128)S(1)}, s32[16,8]{0,1:T(8,128)}, u32[]{:S(2)}) copy-start(s32[16,8]{0,1:T(8,128)} %param.39) | copy-start | bytes 1540
  102.6 59.1 %all-to-all-start.1 = ((bf16[128,16,1024]{2,1,0:T(8,128)(2,1)}), bf16[128,16,1024]{2,1,0:T(8,128)(2,1)}, u32[]{:S(2)}, u32[]{:S(2)}) async-start(bf16[128,16,1024]{2,1,0:T(8,128)(2,1)} %bitcast.95), calls=%async_computation.1 | async-start | bytes 8388608 | tf_op jit(solution)/shard_map/all_to_all | solution.py:184
  127.2 2.8 copy-start.10
  132.5 0.8 copy-start.4
  132.5 1.7 copy-start.8
  132.5 1.7 copy-start.9
  134.1 1.6 copy-start.3
  144.4 1.2 slice-start
  148.7 37.4 %copy-start.7 = (f32[2048]{0:T(1024)S(1)}, f32[2048]{0:T(1024)}, u32[]{:S(2)}) copy-start(f32[2048]{0:T(1024)} %param.25) | copy-start | bytes 24580
  234.9 35.1 %all-to-all-start.3 = ((bf16[128,3,2048]{2,1,0:T(4,128)(2,1)}), bf16[128,3,2048]{2,1,0:T(4,128)(2,1)}, u32[]{:S(2)}, u32[]{:S(2)}) async-start(bf16[128,3,2048]{2,1,0:T(4,128)(2,1)} %copy.150), calls=%async_computation.3 | async-start | bytes 4194304 | tf_op jit(solution)/shard_map/all_to_all | solution.py:306
  241.7 1.4 copy-start.5
Sparse Core Ops, SparseCore 0:
  12.0 68.3 all-gather.1

commit v12 on v11

--- a/solution.py
+++ b/solution.py
@@ -269,7 +269,6 @@
     qkv_out = copy_columns(gathered, qkv_width, 4)
     qkv_out, attended = lax.optimization_barrier((qkv_out, attended))
     head_terms = jnp.dot(attended, server_out, preferred_element_type=jnp.float32)
-    server_gate_up, head_terms = lax.optimization_barrier((server_gate_up, head_terms))
     mixed_own = scatter_sum(head_terms, lax.axis_size("tp"))
     residual_own = lax.dynamic_slice_in_dim(tokens_f32, row_start, shard_rows, 0) + mixed_own
     moe_own = rms_scale(residual_own, moe_gain).astype(jnp.bfloat16)
@@ -297,6 +296,7 @@
         outgoing_rows.reshape(expert_count, 1, slot_depth, model_width),
         (expert_count, 2, slot_depth, model_width),
     ).reshape(2 * expert_count, slot_depth, model_width)
+    server_gate_up, send_rows = lax.optimization_barrier((server_gate_up, send_rows))
     arrived_rows = lax.all_to_all(send_rows, ("req", "tp"), split_axis=0, concat_axis=0, tiled=True)
     both = jnp.einsum("xkd,df->xkf", arrived_rows, server_gate_up[0], preferred_element_type=jnp.float32)
     act = (jax.nn.silu(both[..., :half_units]) * both[..., half_units:]).astype(jnp.bfloat16)

time: 283 us -> 276 us (0.975)
  waiting for transfers between devices: 51.1 us -> 39.4 us
  blocking collectives: 33 us -> 39.3 us
    all_to_all x1, waiting for transfers between devices: 11.7 us -> 0.01 us  [body(): lax.all_to_all(packed, ('req', 'tp'), split_axis=0, concat_axis=1, tiled=...]
    all_to_all x1, blocking collectives: 33 us -> 39.3 us  [body(): lax.all_to_all(send_rows, ('req', 'tp'), split_axis=0, concat_axis=0, til...]
  transfers between devices with their start and end apart: 4 -> 4, of which waited for: 3 -> 2; matrix products, arithmetic and copies ran while one was open for 35% -> 37% of each run, Pallas kernels for 4% -> 12%
where the time goes in v12:
time: 276 us; the launch traced here: 275 us
  local copies, waits for them, and re-layouts  62.9 us (23%)
  other arithmetic  42.2 us (15%)
  waiting for transfers between devices  39.4 us (14%)
  blocking collectives  39.3 us (14%)
  Pallas kernels  32.9 us (12%)
  starting transfers between devices  22.6 us (8%)
  matrix products  20.9 us (8%)
  between operations  14.5 us (5%)
    all_to_all x1, blocking collectives, body(): lax.all_to_all(send_rows, ('req', 'tp'), split_axis=0, concat_axis=0, til...  39.3 us
    all_to_all x1, waiting for transfers between devices, body(): lax.all_to_all(outgoing_pages, 'req', split_axis=0, concat_axis=0, tiled=...  23.4 us
    pallas_call x1, Pallas kernels, scatter_sum(): pl.pallas_call(functools.partial(scatter_sum_kernel, parts), out_shape=ja...  21.7 us
    gather x4, local copies, waits for them, and re-layouts, body(): jnp.take(arrived_pages.reshape((req_count * capacity,) + page_shape), own...  16.8 us
    all_to_all x1, waiting for transfers between devices, body(): lax.all_to_all(expert_rows, ('req', 'tp'), split_axis=0, concat_axis=0, t...  16 us
    concatenate x1, other arithmetic, body(): jnp.concatenate([split_halves(gate_weight.astype(jnp.bfloat16)), split_ha...  10.6 us
    gather x1, local copies, waits for them, and re-layouts, body(): jnp.take(page_store, send_slot.reshape(-1), axis=0)  10 us
    reshape x2, local copies, waits for them, and re-layouts, split_halves(): weights.reshape(expert_count, rows_here, 2, hidden_units // 2)  9.06 us
  transfers between devices with their start and end apart: 4, of which 2 were waited for; matrix products, arithmetic and copies ran while one was open for 37% of the time, Pallas kernels for 12%

profile of v12, /device:TPU:1, one launch (start us, length us, event | category | flops | bytes accessed | tf_op | source)
XLA Modules:
  0.0 274.7 jit_solution(8709478216624776639)
XLA Ops:
  14.9 10.0 %gather_fusion = bf16[32,128,2,256]{3,2,1,0:T(2,128)(2,1)} fusion(bf16[8,128,2,256]{3,2,1,0:T(2,128)(2,1)S(1)} %copy-done.1, s32[1024]{0:T(1024)S(1)} %pad_clamp_fusion.1), kind=kCustom, calls=%fused_computation | custom fusion | bytes 8388736 | tf_op jit(solution)/shard_map/jit(_take)/gather | solution.py:228
  24.9 4.7 %copy_select_fusion = bf16[16,2,128,2,256]{4,2,3,1,0:T(8,128)(2,1)} fusion(bf16[16,2,128,2,256]{4,3,2,1,0:T(2,128)(2,1)} %bitcast.94, pred[16,2]{1,0:T(8,128)(4,1)S(1)} %copy.132), kind=kLoop, calls=%fused_computation.6 | loop fusion | flops 2097152 | bytes 8388640 | tf_op jit(solution)/shard_map/jit(_take)/select_n | solution.py:228
  29.7 8.1 %all-to-all-start = ((bf16[16,2,128,2,256]{4,2,3,1,0:T(8,128)(2,1)}), bf16[16,2,128,2,256]{4,2,3,1,0:T(8,128)(2,1)}, u32[]{:S(2)}, u32[]{:S(2)}) async-start(bf16[16,2,128,2,256]{4,2,3,1,0:T(8,128)(2,1)} %copy_select_fusion), calls=%async_computation | async-start | bytes 8388608 | tf_op jit(solution)/shard_map/all_to_all | solution.py:231
  40.2 4.0 %convert_element_type.114 = bf16[64,16,1024]{2,1,0:T(8,128)(2,1)} convert(f32[64,16,1024]{2,1,0:T(8,128)} %param.30) | non-fusion elementwise | flops 1048576 | bytes 6291456 | tf_op jit(solution)/shard_map/convert_element_type | solution.py:179
  44.2 4.5 %reshape.346 = bf16[64,16,2,512]{3,2,1,0:T(2,128)(2,1)} reshape(bf16[64,16,1024]{2,1,0:T(8,128)(2,1)} %convert_element_type.114) | data formatting | bytes 4194304 | tf_op jit(solution)/shard_map/reshape | solution.py:38
  48.7 3.9 %convert_element_type.115 = bf16[64,16,1024]{2,1,0:T(8,128)(2,1)} convert(f32[64,16,1024]{2,1,0:T(8,128)} %param.31) | non-fusion elementwise | flops 1048576 | bytes 6291456 | tf_op jit(solution)/shard_map/convert_element_type | solution.py:180
  52.6 4.5 %reshape.347 = bf16[64,16,2,512]{3,2,1,0:T(2,128)(2,1)} reshape(bf16[64,16,1024]{2,1,0:T(8,128)(2,1)} %convert_element_type.115) | data formatting | bytes 4194304 | tf_op jit(solution)/shard_map/reshape | solution.py:38
  57.1 10.6 %pad_maximum_fusion = bf16[64,2,16,1024]{3,1,2,0:T(2,128)(2,1)} fusion(bf16[64,2,16,512]{3,1,2,0:T(2,128)(2,1)} %bitcast.100, bf16[64,2,16,512]{3,1,2,0:T(2,128)(2,1)} %bitcast.99), kind=kLoop, calls=%fused_computation.3 | loop fusion | flops 8388608 | bytes 8388608 | tf_op jit(solution)/shard_map/concatenate | solution.py:177
  67.7 5.6 %copy.141 = bf16[64,2,16,1024]{3,2,1,0:T(8,128)(2,1)} copy(bf16[64,2,16,1024]{3,1,2,0:T(2,128)(2,1)} %pad_maximum_fusion) | data formatting | bytes 8388608 | tf_op jit(solution)/shard_map/concatenate | solution.py:177
  73.9 1.9 fusion.34
  75.8 2.0 compare_convert_fusion
  79.3 23.4 %all-to-all-done = bf16[16,2,128,2,256]{4,2,3,1,0:T(8,128)(2,1)} async-done(((bf16[16,2,128,2,256]{4,2,3,1,0:T(8,128)(2,1)}), bf16[16,2,128,2,256]{4,2,3,1,0:T(8,128)(2,1)}, u32[]{:S(2)}, u32[]{:S(2)}) %all-to-all-start) | async-done | bytes 4194336 | tf_op jit(solution)/shard_map/all_to_all | solution.py:231
  102.7 8.0 %all-to-all-start.1 = ((bf16[128,16,1024]{2,1,0:T(8,128)(2,1)}), bf16[128,16,1024]{2,1,0:T(8,128)(2,1)}, u32[]{:S(2)}, u32[]{:S(2)}) async-start(bf16[128,16,1024]{2,1,0:T(8,128)(2,1)} %bitcast.95), calls=%async_computation.1 | async-start | bytes 8388608 | tf_op jit(solution)/shard_map/all_to_all | solution.py:184
  110.7 4.2 %gather_fusion.1 = bf16[16,128,2,256]{3,1,2,0:T(8,128)(2,1)} fusion(bf16[32,128,2,256]{3,1,2,0:T(8,128)(2,1)} %bitcast.9, s32[1024]{0:T(1024)S(1)} %pad_clamp_fusion), kind=kCustom, calls=%fused_computation.1 | custom fusion | bytes 4194368 | tf_op jit(solution)/shard_map/jit(_take)/gather | solution.py:234
  114.9 4.5 %copy.135 = bf16[16,128,2,256]{1,0,3,2:T(8,128)(2,1)} copy(bf16[16,128,2,256]{3,1,2,0:T(8,128)(2,1)} %gather_fusion.1) | data formatting | bytes 4194304 | tf_op jit(solution)/shard_map/jit(_take)/gather | solution.py:234
  119.4 4.2 %gather.22 = bf16[2048,2,2,128]{0,3,2,1:T(8,128)(2,1)} reshape(bf16[16,128,2,256]{1,0,3,2:T(8,128)(2,1)} %copy.135) | data formatting | bytes 4194304 | tf_op jit(solution)/shard_map/jit(_take)/gather | solution.py:234
  123.5 3.9 %copy.136 = bf16[2048,2,2,128]{3,0,2,1:T(8,128)(2,1)} copy(bf16[2048,2,2,128]{0,3,2,1:T(8,128)(2,1)} %gather.22) | data formatting | bytes 4194304 | tf_op jit(solution)/shard_map/jit(_take)/gather | solution.py:234
  127.4 2.8 %broadcast_select_fusion = bf16[2048,2,2,128]{3,0,2,1:T(8,128)(2,1)} fusion(bf16[2048,2,2,128]{3,0,2,1:T(8,128)(2,1)} %copy.136, pred[2048]{0:T(1024)(128)(4,1)S(1)} %broadcast_bitcast_fusion), kind=kLoop, calls=%fused_computation.19 | loop fusion | flops 1048576 | bytes 4196352 | tf_op jit(solution)/shard_map/jit(_take)/select_n | solution.py:234
  130.2 2.5 fusion.2
  137.9 4.2 %shard_map.218 = bf16[2048,768]{1,0:T(8,128)(2,1)} custom-call(bf16[2048,1024]{1,0:T(8,128)(2,1)} %all-gather.2.cloned.1.call-done.x_ref), custom_call_target="tpu_custom_call" | custom-call | bytes 6291456 | tf_op jit(solution)/shard_map/pallas_call | solution.py:119
  142.1 2.5 fusion.14
  150.2 21.7 %shard_map.220 = f32[16,2048]{1,0:T(8,128)} custom-call(f32[128,2048]{1,0:T(8,128)} %fusion.39.x_ref), custom_call_target="tpu_custom_call" | custom-call | tf_op jit(solution)/shard_map/pallas_call | solution.py:85
  174.3 3.3 %broadcast_in_dim.151 = bf16[64,3,2048]{2,1,0:T(4,128)(2,1)} reshape(bf16[192,2048]{1,0:T(8,128)(2,1)} %convolution_convert_fusion.1) | data formatting | bytes 1572864 | tf_op jit(solution)/shard_map/broadcast_in_dim | solution.py:295
  177.6 2.5 broadcast_in_dim.152
  180.0 39.3 %all_to_all.27 = bf16[128,3,2048]{2,1,0:T(4,128)(2,1)S(1)} all-to-all(bf16[128,3,2048]{2,1,0:T(4,128)(2,1)S(1)} %bitcast.98), channel_id=1, replica_groups=mesh['req'=16,'tp'=8] {'req','tp'}, dimensions={0} | all-to-all | bytes 3145728 | tf_op jit(solution)/shard_map/all_to_all | solution.py:300
  219.4 5.1 %fusion = f32[128,3,1024]{2,0,1:T(8,128)S(1)} fusion(bf16[1,2048,1024]{2,1,0:T(8,128)(2,1)} %bitcast.18, bf16[128,3,2048]{2,1,0:T(4,128)(2,1)S(1)} %all_to_all.27), kind=kOutput, calls=%fused_computation.4 | convolution fusion | flops 1610612736 | bytes 7340032 | tf_op jit(solution)/shard_map/xkd,df->xkf/dot_general | solution.py:301
  225.6 2.6 copy.150
  228.2 6.6 %all-to-all-start.3 = ((bf16[128,3,2048]{2,1,0:T(4,128)(2,1)}), bf16[128,3,2048]{2,1,0:T(4,128)(2,1)}, u32[]{:S(2)}, u32[]{:S(2)}) async-start(bf16[128,3,2048]{2,1,0:T(4,128)(2,1)} %copy.150), calls=%async_computation.3 | async-start | bytes 4194304 | tf_op jit(solution)/shard_map/all_to_all | solution.py:306
  238.5 4.7 %shard_map.221 = bf16[2048,1024]{1,0:T(8,128)(2,1)} custom-call(bf16[2048,1024]{1,0:T(8,128)(2,1)} %bitcast.20.x_ref), custom_call_target="tpu_custom_call" | custom-call | bytes 8388608 | tf_op jit(solution)/shard_map/pallas_call | solution.py:107
  245.0 2.3 shard_map.219
  247.3 16.0 %all-to-all-done.3 = bf16[128,3,2048]{2,1,0:T(4,128)(2,1)} async-done(((bf16[128,3,2048]{2,1,0:T(4,128)(2,1)}), bf16[128,3,2048]{2,1,0:T(4,128)(2,1)}, u32[]{:S(2)}, u32[]{:S(2)}) %all-to-all-start.3) | async-done | bytes 1572896 | tf_op jit(solution)/shard_map/all_to_all | solution.py:306
  263.4 4.5 %fusion.7 = bf16[16,2048]{1,0:T(8,128)(2,1)} fusion(f32[16,2048]{1,0:T(8,128)S(1)} %get-tuple-element.56, f32[16,128,3]{0,1,2:T(8,128)S(1)} %bitcast.103, bf16[128,3,2048]{2,1,0:T(4,128)(2,1)} %all-to-all-done.3), kind=kOutput, calls=%fused_computation.16 | convolution fusion | flops 151060480 | bytes 1794048 | tf_op jit(solution)/shard_map/ixk,xkd->id/dot_general | solution.py:318
  (115 shorter events, 31.8 us)
Async XLA Ops:
  7.2 217.4 %copy-start = (bf16[1,512,2048]{2,1,0:T(8,128)(2,1)S(1)}, bf16[1,512,2048]{2,1,0:T(8,128)(2,1)}, u32[]{:S(2)}) copy-start(bf16[1,512,2048]{2,1,0:T(8,128)(2,1)} %param.32) | copy-start | bytes 6291460
  7.2 7.7 %copy-start.1 = (bf16[8,128,2,256]{3,2,1,0:T(2,128)(2,1)S(1)}, bf16[8,128,2,256]{3,2,1,0:T(2,128)(2,1)}, u32[]{:S(2)}) copy-start(bf16[8,128,2,256]{3,2,1,0:T(2,128)(2,1)} %param.34) | copy-start | bytes 3145732
  7.2 123.0 %all-gather.2.cloned.1.call-start = ((), (), s32[]{:S(2)}) async-start(), calls=%async_computation.4 | async-start | bytes 4456448 | tf_op jit(solution)/shard_map/all_gather | solution.py:165
  29.7 8.1 %copy-start.11 = (s32[32]{0:T(128)S(1)}, s32[32]{0:T(128)}, u32[]{:S(2)}) copy-start(s32[32]{0:T(128)} %param.36) | copy-start | bytes 388
  29.7 8.2 %copy-start.12 = (s32[32]{0:T(128)S(1)}, s32[32]{0:T(128)}, u32[]{:S(2)}) copy-start(s32[32]{0:T(128)} %param.35) | copy-start | bytes 388
  29.7 8.7 %copy-start.2 = (bf16[128,2048]{1,0:T(8,128)(2,1)S(1)}, bf16[128,2048]{1,0:T(8,128)(2,1)}, u32[]{:S(2)}) copy-start(bf16[128,2048]{1,0:T(8,128)(2,1)} %param.21) | copy-start | bytes 1572868
  29.7 9.8 %copy-start.6 = (s32[16,8]{0,1:T(8,128)S(1)}, s32[16,8]{0,1:T(8,128)}, u32[]{:S(2)}) copy-start(s32[16,8]{0,1:T(8,128)} %param.39) | copy-start | bytes 1540
  29.7 73.0 %all-to-all-start = ((bf16[16,2,128,2,256]{4,2,3,1,0:T(8,128)(2,1)}), bf16[16,2,128,2,256]{4,2,3,1,0:T(8,128)(2,1)}, u32[]{:S(2)}, u32[]{:S(2)}) async-start(bf16[16,2,128,2,256]{4,2,3,1,0:T(8,128)(2,1)} %copy_select_fusion), calls=%async_computation | async-start | bytes 8388608 | tf_op jit(solution)/shard_map/all_to_all | solution.py:231
  102.7 74.9 %all-to-all-start.1 = ((bf16[128,16,1024]{2,1,0:T(8,128)(2,1)}), bf16[128,16,1024]{2,1,0:T(8,128)(2,1)}, u32[]{:S(2)}, u32[]{:S(2)}) async-start(bf16[128,16,1024]{2,1,0:T(8,128)(2,1)} %bitcast.95), calls=%async_computation.1 | async-start | bytes 8388608 | tf_op jit(solution)/shard_map/all_to_all | solution.py:184
  127.4 2.8 %copy-start.10 = (f32[2048]{0:T(1024)S(1)}, f32[2048]{0:T(1024)}, u32[]{:S(2)}) copy-start(f32[2048]{0:T(1024)} %param.22) | copy-start | bytes 24580
  132.7 0.8 copy-start.4
  132.7 1.7 copy-start.8
  132.7 1.7 copy-start.9
  134.4 1.6 copy-start.3
  144.6 1.2 slice-start
  148.9 24.1 %copy-start.7 = (f32[2048]{0:T(1024)S(1)}, f32[2048]{0:T(1024)}, u32[]{:S(2)}) copy-start(f32[2048]{0:T(1024)} %param.25) | copy-start | bytes 24580
  228.2 35.1 %all-to-all-start.3 = ((bf16[128,3,2048]{2,1,0:T(4,128)(2,1)}), bf16[128,3,2048]{2,1,0:T(4,128)(2,1)}, u32[]{:S(2)}, u32[]{:S(2)}) async-start(bf16[128,3,2048]{2,1,0:T(4,128)(2,1)} %copy.150), calls=%async_computation.3 | async-start | bytes 4194304 | tf_op jit(solution)/shard_map/all_to_all | solution.py:306
  235.0 1.4 copy-start.5
Sparse Core Ops, SparseCore 0:
  12.0 68.4 all-gather.1

commit v13 on v12

--- a/solution.py
+++ b/solution.py
@@ -225,7 +225,7 @@
     )
     send_slot = jnp.sum(jnp.where(chosen, page_slot[:, None, :], 0), axis=2)
     page_shape = page_store.shape[1:]
-    outgoing_pages = jnp.take(page_store, send_slot.reshape(-1), axis=0).reshape(
+    outgoing_pages = jnp.take(page_store, send_slot.reshape(-1), axis=0, mode="clip").reshape(
         (req_count, capacity) + page_shape
     )
     arrived_pages = lax.all_to_all(outgoing_pages, "req", split_axis=0, concat_axis=0, tiled=True)
@@ -235,6 +235,7 @@
         arrived_pages.reshape((req_count * capacity,) + page_shape),
         own_owner * capacity + own_rank,
         axis=0,
+        mode="clip",
     )
     context = context.reshape(context_len, 2, lane_heads, head_dim)
     score_scale = 1.0 / math.sqrt(head_dim)

time: 276 us -> 275 us (level)
  other arithmetic: 42.2 us -> 34.7 us
  Pallas kernels: 32.9 us -> 39.2 us
    reshape x1 -> x2, local copies, waits for them, and re-layouts: 0.09 us -> 9.22 us  [the longest x1 5.02 us: body(): jnp.take(page_store, send_slot.reshape(-1), axis=0, mode='clip')]
    gather x4 -> x2, local copies, waits for them, and re-layouts: 16.8 us -> 8.68 us  [body(): jnp.take(arrived_pages.reshape((req_count * capacity,) + page_shape), own...]
    select_n x3 -> x0, other arithmetic: 7.51 us -> none  [the longest x2 4.75 us: body(): jnp.take(page_store, send_slot.reshape(-1), axis=0)]
    pallas_call x1, Pallas kernels: 21.7 us -> 28 us  [scatter_sum(): pl.pallas_call(functools.partial(scatter_sum_kernel, parts), out_shape=ja...]
  transfers between devices with their start and end apart: 4 -> 4, of which waited for: 2 -> 2; matrix products, arithmetic and copies ran while one was open for 37% -> 35% of each run, Pallas kernels for 12% -> 14%
where the time goes in v13:
time: 275 us; the launch traced here: 273 us
  local copies, waits for them, and re-layouts  63.8 us (23%)
  waiting for transfers between devices  39.5 us (14%)
  Pallas kernels  39.2 us (14%)
  blocking collectives  38.3 us (14%)
  other arithmetic  34.7 us (13%)
  starting transfers between devices  22.4 us (8%)
  matrix products  20.8 us (8%)
  between operations  14.5 us (5%)
    all_to_all x1, blocking collectives, body(): lax.all_to_all(send_rows, ('req', 'tp'), split_axis=0, concat_axis=0, til...  38.3 us
    pallas_call x1, Pallas kernels, scatter_sum(): pl.pallas_call(functools.partial(scatter_sum_kernel, parts), out_shape=ja...  28 us
    all_to_all x1, waiting for transfers between devices, body(): lax.all_to_all(outgoing_pages, 'req', split_axis=0, concat_axis=0, tiled=...  23.5 us
    all_to_all x1, waiting for transfers between devices, body(): lax.all_to_all(expert_rows, ('req', 'tp'), split_axis=0, concat_axis=0, t...  16 us
    concatenate x1, other arithmetic, body(): jnp.concatenate([split_halves(gate_weight.astype(jnp.bfloat16)), split_ha...  10.6 us
    gather x1, local copies, waits for them, and re-layouts, body(): jnp.take(page_store, send_slot.reshape(-1), axis=0, mode='clip')  10 us
    reshape x2, local copies, waits for them, and re-layouts, split_halves(): weights.reshape(expert_count, rows_here, 2, hidden_units // 2)  9.06 us
    gather x2, local copies, waits for them, and re-layouts, body(): jnp.take(arrived_pages.reshape((req_count * capacity,) + page_shape), own...  8.68 us
  transfers between devices with their start and end apart: 4, of which 2 were waited for; matrix products, arithmetic and copies ran while one was open for 35% of the time, Pallas kernels for 14%

profile of v13, /device:TPU:1, one launch (start us, length us, event | category | flops | bytes accessed | tf_op | source)
XLA Modules:
  0.0 273.1 jit_solution(7790721774445946989)
XLA Ops:
  14.8 10.0 %gather_fusion = bf16[32,128,2,256]{3,2,1,0:T(2,128)(2,1)} fusion(bf16[8,128,2,256]{3,2,1,0:T(2,128)(2,1)S(1)} %copy-done.1, s32[1024]{0:T(1024)S(1)} %pad_clamp_fusion.1), kind=kCustom, calls=%fused_computation | custom fusion | bytes 8388736 | tf_op jit(solution)/shard_map/jit(_take)/gather | solution.py:228
  24.8 5.0 %copy.128 = bf16[16,2,128,2,256]{4,2,3,1,0:T(8,128)(2,1)} copy(bf16[16,2,128,2,256]{4,3,2,1,0:T(2,128)(2,1)} %bitcast.86) | data formatting | bytes 8388608 | tf_op jit(solution)/shard_map/reshape | solution.py:228
  29.9 8.1 %all-to-all-start = ((bf16[16,2,128,2,256]{4,2,3,1,0:T(8,128)(2,1)}), bf16[16,2,128,2,256]{4,2,3,1,0:T(8,128)(2,1)}, u32[]{:S(2)}, u32[]{:S(2)}) async-start(bf16[16,2,128,2,256]{4,2,3,1,0:T(8,128)(2,1)} %copy.128), calls=%async_computation | async-start | bytes 8388608 | tf_op jit(solution)/shard_map/all_to_all | solution.py:231
  40.4 3.9 %convert_element_type.114 = bf16[64,16,1024]{2,1,0:T(8,128)(2,1)} convert(f32[64,16,1024]{2,1,0:T(8,128)} %param.30) | non-fusion elementwise | flops 1048576 | bytes 6291456 | tf_op jit(solution)/shard_map/convert_element_type | solution.py:179
  44.4 4.5 %reshape.307 = bf16[64,16,2,512]{3,2,1,0:T(2,128)(2,1)} reshape(bf16[64,16,1024]{2,1,0:T(8,128)(2,1)} %convert_element_type.114) | data formatting | bytes 4194304 | tf_op jit(solution)/shard_map/reshape | solution.py:38
  48.9 3.9 %convert_element_type.115 = bf16[64,16,1024]{2,1,0:T(8,128)(2,1)} convert(f32[64,16,1024]{2,1,0:T(8,128)} %param.31) | non-fusion elementwise | flops 1048576 | bytes 6291456 | tf_op jit(solution)/shard_map/convert_element_type | solution.py:180
  52.8 4.5 %reshape.308 = bf16[64,16,2,512]{3,2,1,0:T(2,128)(2,1)} reshape(bf16[64,16,1024]{2,1,0:T(8,128)(2,1)} %convert_element_type.115) | data formatting | bytes 4194304 | tf_op jit(solution)/shard_map/reshape | solution.py:38
  57.3 10.6 %pad_maximum_fusion = bf16[64,2,16,1024]{3,1,2,0:T(2,128)(2,1)} fusion(bf16[64,2,16,512]{3,1,2,0:T(2,128)(2,1)} %bitcast.91, bf16[64,2,16,512]{3,1,2,0:T(2,128)(2,1)} %bitcast.90), kind=kLoop, calls=%fused_computation.3 | loop fusion | flops 8388608 | bytes 8388608 | tf_op jit(solution)/shard_map/concatenate | solution.py:177
  67.9 5.6 %copy.134 = bf16[64,2,16,1024]{3,2,1,0:T(8,128)(2,1)} copy(bf16[64,2,16,1024]{3,1,2,0:T(2,128)(2,1)} %pad_maximum_fusion) | data formatting | bytes 8388608 | tf_op jit(solution)/shard_map/concatenate | solution.py:177
  74.8 1.9 fusion.33
  76.7 1.9 compare_convert_fusion
  79.5 23.5 %all-to-all-done = bf16[16,2,128,2,256]{4,2,3,1,0:T(8,128)(2,1)} async-done(((bf16[16,2,128,2,256]{4,2,3,1,0:T(8,128)(2,1)}), bf16[16,2,128,2,256]{4,2,3,1,0:T(8,128)(2,1)}, u32[]{:S(2)}, u32[]{:S(2)}) %all-to-all-start) | async-done | bytes 4194336 | tf_op jit(solution)/shard_map/all_to_all | solution.py:231
  102.9 7.6 %all-to-all-start.1 = ((bf16[128,16,1024]{2,1,0:T(8,128)(2,1)}), bf16[128,16,1024]{2,1,0:T(8,128)(2,1)}, u32[]{:S(2)}, u32[]{:S(2)}) async-start(bf16[128,16,1024]{2,1,0:T(8,128)(2,1)} %bitcast.85), calls=%async_computation.1 | async-start | bytes 8388608 | tf_op jit(solution)/shard_map/all_to_all | solution.py:184
  110.6 4.2 %gather_fusion.1 = bf16[16,128,2,256]{3,1,2,0:T(8,128)(2,1)} fusion(bf16[32,128,2,256]{3,1,2,0:T(8,128)(2,1)} %bitcast.5, s32[1024]{0:T(1024)S(1)} %pad_clamp_fusion), kind=kCustom, calls=%fused_computation.1 | custom fusion | bytes 4194368 | tf_op jit(solution)/shard_map/jit(_take)/gather | solution.py:234
  114.7 4.5 %copy.129 = bf16[16,128,2,256]{1,0,3,2:T(8,128)(2,1)} copy(bf16[16,128,2,256]{3,1,2,0:T(8,128)(2,1)} %gather_fusion.1) | data formatting | bytes 4194304 | tf_op jit(solution)/shard_map/jit(_take)/gather | solution.py:234
  119.2 4.2 %reshape.303 = bf16[2048,2,2,128]{0,3,2,1:T(8,128)(2,1)} reshape(bf16[16,128,2,256]{1,0,3,2:T(8,128)(2,1)} %copy.129) | data formatting | bytes 4194304 | tf_op jit(solution)/shard_map/reshape | solution.py:240
  123.4 2.5 fusion.2
  129.2 2.0 fusion.42
  131.1 4.2 %shard_map.218 = bf16[2048,768]{1,0:T(8,128)(2,1)} custom-call(bf16[2048,1024]{1,0:T(8,128)(2,1)} %all-gather.2.cloned.1.call-done.x_ref), custom_call_target="tpu_custom_call" | custom-call | bytes 6291456 | tf_op jit(solution)/shard_map/pallas_call | solution.py:119
  135.3 2.4 fusion.14
  140.2 1.9 copy.133
  143.4 28.0 %shard_map.220 = f32[16,2048]{1,0:T(8,128)} custom-call(f32[128,2048]{1,0:T(8,128)} %fusion.38.x_ref), custom_call_target="tpu_custom_call" | custom-call | tf_op jit(solution)/shard_map/pallas_call | solution.py:85
  173.8 3.3 %broadcast_in_dim.128 = bf16[64,3,2048]{2,1,0:T(4,128)(2,1)} reshape(bf16[192,2048]{1,0:T(8,128)(2,1)} %convolution_convert_fusion.1) | data formatting | bytes 1572864 | tf_op jit(solution)/shard_map/broadcast_in_dim | solution.py:296
  177.1 2.5 broadcast_in_dim.129
  179.5 38.3 %all_to_all.27 = bf16[128,3,2048]{2,1,0:T(4,128)(2,1)S(1)} all-to-all(bf16[128,3,2048]{2,1,0:T(4,128)(2,1)S(1)} %bitcast.89), channel_id=1, replica_groups=mesh['req'=16,'tp'=8] {'req','tp'}, dimensions={0} | all-to-all | bytes 3145728 | tf_op jit(solution)/shard_map/all_to_all | solution.py:301
  217.8 5.1 %fusion = f32[128,3,1024]{2,0,1:T(8,128)S(1)} fusion(bf16[1,2048,1024]{2,1,0:T(8,128)(2,1)} %bitcast.16, bf16[128,3,2048]{2,1,0:T(4,128)(2,1)S(1)} %all_to_all.27), kind=kOutput, calls=%fused_computation.4 | convolution fusion | flops 1610612736 | bytes 7340032 | tf_op jit(solution)/shard_map/xkd,df->xkf/dot_general | solution.py:302
  224.0 2.6 copy.143
  226.6 6.6 %all-to-all-start.3 = ((bf16[128,3,2048]{2,1,0:T(4,128)(2,1)}), bf16[128,3,2048]{2,1,0:T(4,128)(2,1)}, u32[]{:S(2)}, u32[]{:S(2)}) async-start(bf16[128,3,2048]{2,1,0:T(4,128)(2,1)} %copy.143), calls=%async_computation.3 | async-start | bytes 4194304 | tf_op jit(solution)/shard_map/all_to_all | solution.py:307
  236.9 4.7 %shard_map.221 = bf16[2048,1024]{1,0:T(8,128)(2,1)} custom-call(bf16[2048,1024]{1,0:T(8,128)(2,1)} %bitcast.18.x_ref), custom_call_target="tpu_custom_call" | custom-call | bytes 8388608 | tf_op jit(solution)/shard_map/pallas_call | solution.py:107
  243.4 2.3 shard_map.219
  245.7 16.0 %all-to-all-done.3 = bf16[128,3,2048]{2,1,0:T(4,128)(2,1)} async-done(((bf16[128,3,2048]{2,1,0:T(4,128)(2,1)}), bf16[128,3,2048]{2,1,0:T(4,128)(2,1)}, u32[]{:S(2)}, u32[]{:S(2)}) %all-to-all-start.3) | async-done | bytes 1572896 | tf_op jit(solution)/shard_map/all_to_all | solution.py:307
  261.8 4.5 %fusion.7 = bf16[16,2048]{1,0:T(8,128)(2,1)} fusion(f32[16,2048]{1,0:T(8,128)S(1)} %get-tuple-element.56, f32[16,128,3]{0,1,2:T(8,128)S(1)} %bitcast.94, bf16[128,3,2048]{2,1,0:T(4,128)(2,1)} %all-to-all-done.3), kind=kOutput, calls=%fused_computation.15 | convolution fusion | flops 151060480 | bytes 1794048 | tf_op jit(solution)/shard_map/ixk,xkd->id/dot_general | solution.py:319
  (109 shorter events, 27.7 us)
Async XLA Ops:
  7.2 215.8 %copy-start = (bf16[1,512,2048]{2,1,0:T(8,128)(2,1)S(1)}, bf16[1,512,2048]{2,1,0:T(8,128)(2,1)}, u32[]{:S(2)}) copy-start(bf16[1,512,2048]{2,1,0:T(8,128)(2,1)} %param.32) | copy-start | bytes 6291460
  7.2 7.6 %copy-start.1 = (bf16[8,128,2,256]{3,2,1,0:T(2,128)(2,1)S(1)}, bf16[8,128,2,256]{3,2,1,0:T(2,128)(2,1)}, u32[]{:S(2)}) copy-start(bf16[8,128,2,256]{3,2,1,0:T(2,128)(2,1)} %param.34) | copy-start | bytes 3145732
  7.2 116.2 %all-gather.2.cloned.1.call-start = ((), (), s32[]{:S(2)}) async-start(), calls=%async_computation.4 | async-start | bytes 4456448 | tf_op jit(solution)/shard_map/all_gather | solution.py:165
  29.8 8.1 %copy-start.11 = (s32[32]{0:T(128)S(1)}, s32[32]{0:T(128)}, u32[]{:S(2)}) copy-start(s32[32]{0:T(128)} %param.36) | copy-start | bytes 388
  29.8 8.2 %copy-start.12 = (s32[32]{0:T(128)S(1)}, s32[32]{0:T(128)}, u32[]{:S(2)}) copy-start(s32[32]{0:T(128)} %param.35) | copy-start | bytes 388
  29.8 8.8 %copy-start.2 = (bf16[128,2048]{1,0:T(8,128)(2,1)S(1)}, bf16[128,2048]{1,0:T(8,128)(2,1)}, u32[]{:S(2)}) copy-start(bf16[128,2048]{1,0:T(8,128)(2,1)} %param.21) | copy-start | bytes 1572868
  29.9 9.9 %copy-start.6 = (s32[16,8]{0,1:T(8,128)S(1)}, s32[16,8]{0,1:T(8,128)}, u32[]{:S(2)}) copy-start(s32[16,8]{0,1:T(8,128)} %param.39) | copy-start | bytes 1540
  29.9 73.1 %all-to-all-start = ((bf16[16,2,128,2,256]{4,2,3,1,0:T(8,128)(2,1)}), bf16[16,2,128,2,256]{4,2,3,1,0:T(8,128)(2,1)}, u32[]{:S(2)}, u32[]{:S(2)}) async-start(bf16[16,2,128,2,256]{4,2,3,1,0:T(8,128)(2,1)} %copy.128), calls=%async_computation | async-start | bytes 8388608 | tf_op jit(solution)/shard_map/all_to_all | solution.py:231
  102.9 74.2 %all-to-all-start.1 = ((bf16[128,16,1024]{2,1,0:T(8,128)(2,1)}), bf16[128,16,1024]{2,1,0:T(8,128)(2,1)}, u32[]{:S(2)}, u32[]{:S(2)}) async-start(bf16[128,16,1024]{2,1,0:T(8,128)(2,1)} %bitcast.85), calls=%async_computation.1 | async-start | bytes 8388608 | tf_op jit(solution)/shard_map/all_to_all | solution.py:184
  119.2 4.2 %copy-start.10 = (f32[2048]{0:T(1024)S(1)}, f32[2048]{0:T(1024)}, u32[]{:S(2)}) copy-start(f32[2048]{0:T(1024)} %param.22) | copy-start | bytes 24580
  126.0 0.8 copy-start.4
  126.0 1.7 copy-start.8
  126.0 1.7 copy-start.9
  127.6 1.6 copy-start.3
  137.8 1.2 slice-start
  142.1 30.4 %copy-start.7 = (f32[2048]{0:T(1024)S(1)}, f32[2048]{0:T(1024)}, u32[]{:S(2)}) copy-start(f32[2048]{0:T(1024)} %param.25) | copy-start | bytes 24580
  226.6 35.1 %all-to-all-start.3 = ((bf16[128,3,2048]{2,1,0:T(4,128)(2,1)}), bf16[128,3,2048]{2,1,0:T(4,128)(2,1)}, u32[]{:S(2)}, u32[]{:S(2)}) async-start(bf16[128,3,2048]{2,1,0:T(4,128)(2,1)} %copy.143), calls=%async_computation.3 | async-start | bytes 4194304 | tf_op jit(solution)/shard_map/all_to_all | solution.py:307
  233.4 1.4 copy-start.5
Sparse Core Ops, SparseCore 0:
  12.0 68.6 all-gather.1
